TPU v7x, 256 devices: a whole 4x4x8 slice. The times are simulated.
256 devices in a mesh: fsdp: 8 (over y, core), expert: 32 (over x, z).
Axes of the slice: x: 4, y: 4, z: 8, core: 2. Of those that a mesh axis runs over, the one named last changes fastest.
Arguments:
- tokens: bfloat16 [32768, 1024], P(('fsdp', 'expert')), may hold values from -6 to 6
- expert_ids: int32 [32768, 2], P(('fsdp', 'expert')), may hold values from 0 to 31, all different within a row; in each aligned block of 128 rows (0 to 127, 128 to 255, ...) at most 16 rows name the same one
- gate_weights: float32 [32768, 2], P(('fsdp', 'expert')), may hold values from 0.2 to 1
- weight_in: bfloat16 [32, 2048, 1024], P('expert', 'fsdp'), may hold values from -0.1875 to 0.1875
- weight_out: bfloat16 [32, 2048, 1024], P('expert', 'fsdp'), may hold values from -0.125 to 0.125
- cotangent: bfloat16 [32768, 1024], P(('fsdp', 'expert')), may hold values from -3 to 3
Outputs:
- layer_out: bfloat16 [32768, 1024], P(('fsdp', 'expert'))
- token_grad: bfloat16 [32768, 1024], P(('fsdp', 'expert'))
- grad_in: float32 [32, 2048, 1024], P('expert', 'fsdp')
- grad_out: float32 [32, 2048, 1024], P('expert', 'fsdp')
Inputs may be any that keep to these rules, and one draw needn't show every extreme that they name: `expert_ids`: the two experts of a token differ. Among the 128 tokens of one device no expert is chosen by more than 16 tokens, and some device has an expert chosen by exactly 16 tokens.
All inputs are finite; a program needn't handle non-finite values.
Results may differ from a plain program's by a relative error of at most 0.014.
Values may be sent and summed in bfloat16 or wider, within the bound.
No kernel may reach another device: no remote copies, remote signals or barrier semaphores. Data moves between devices by JAX's collectives and lax.ppermute only.
A program may use at most 128 MiB of HBM per device.

v0:
```python
import jax
import jax.numpy as jnp
from jax import lax
from jax.sharding import PartitionSpec as P


def in_one_piece(arrays, axis, dim, along):
    ends, at = ([], 0)
    for a in arrays[:-1]:
        at += a.shape[along]
        ends.append(at)
    both = jnp.concatenate(arrays, axis=along)
    return tuple(jnp.split(lax.all_gather(both, axis, axis=dim, tiled=True), ends, axis=along))


def gelu_back(pre_act, upstream):
    _, pullback = jax.vjp(jax.nn.gelu, pre_act)
    return pullback(upstream)[0]


def per_device(tokens, expert_ids, gate_weights, weight_in, weight_out, cotangent):
    tok_count, width = tokens.shape
    expert_count = lax.axis_size("expert")
    capacity = 4 * tok_count // expert_count
    labels = jnp.arange(expert_count, dtype=jnp.int32)
    hit_count = jnp.sum(
        (expert_ids[:, :, None] == labels).astype(jnp.int32), axis=1, dtype=jnp.int32
    )
    earlier = jnp.cumsum(hit_count, axis=0, dtype=jnp.int32) - hit_count
    slot_ids = jnp.take_along_axis(earlier, expert_ids, axis=1)
    target = expert_ids * capacity + slot_ids
    cell_ids = jnp.arange(expert_count * capacity, dtype=jnp.int32)[:, None]
    first_hit = cell_ids == target[:, 0][None, :]
    second_hit = cell_ids == target[:, 1][None, :]
    placing = (first_hit | second_hit).astype(jnp.bfloat16)
    gate_cells = jnp.sum(
        jnp.where(first_hit, gate_weights[:, 0][None, :], 0.0)
        + jnp.where(second_hit, gate_weights[:, 1][None, :], 0.0),
        axis=1,
    )
    outgoing = jnp.dot(placing, tokens, preferred_element_type=jnp.float32).astype(jnp.bfloat16)
    arrived = lax.all_to_all(
        outgoing.reshape(expert_count, capacity, width),
        "expert",
        split_axis=0,
        concat_axis=0,
        tiled=True,
    )
    expert_rows = arrived.reshape(-1, width)
    pieces = in_one_piece((weight_in, weight_out), "fsdp", 1, 0)
    full_in = None
    full_out = None
    part_in = pieces[0][0]
    part_out = pieces[1][0]
    activation = lax.dot_general(
        expert_rows, part_in, (((1,), (1,)), ((), ())), preferred_element_type=jnp.float32
    )
    hidden = jax.nn.gelu(activation).astype(jnp.bfloat16)
    summed = jnp.dot(hidden, part_out, preferred_element_type=jnp.float32)
    forward_stored = activation.astype(jnp.bfloat16)
    summed, stored, hidden_buf, full_in, full_out = (
        summed,
        forward_stored,
        hidden,
        full_in,
        full_out,
    )
    expert_out = summed.astype(jnp.bfloat16).reshape(expert_count, capacity, width)
    returned = lax.all_to_all(
        expert_out, "expert", split_axis=0, concat_axis=0, tiled=True
    ).reshape(-1, width)
    picked = returned[target].astype(jnp.float32)
    layer_out = jnp.sum(picked * gate_weights[:, :, None], axis=1).astype(jnp.bfloat16)
    grad_cells = (
        jnp.dot(placing, cotangent, preferred_element_type=jnp.float32) * gate_cells[:, None]
    )
    grad_cells = grad_cells.astype(jnp.bfloat16).reshape(expert_count, capacity, width)
    grad_rows = lax.all_to_all(
        grad_cells, "expert", split_axis=0, concat_axis=0, tiled=True
    ).reshape(-1, width)
    pieces = in_one_piece((weight_in, weight_out), "fsdp", 1, 0)
    part_in = pieces[0][0]
    part_out = pieces[1][0]
    grad_hidden = lax.dot_general(
        grad_rows, part_out, (((1,), (1,)), ((), ())), preferred_element_type=jnp.float32
    )
    pre_act = stored.astype(jnp.float32)
    grad_act = gelu_back(pre_act, grad_hidden).astype(jnp.bfloat16)
    summed_grad = jnp.dot(grad_act, part_in, preferred_element_type=jnp.float32)
    summed_grad, grad_act_buf = (summed_grad, grad_act)
    grad_back = summed_grad.astype(jnp.bfloat16).reshape(expert_count, capacity, width)
    grad_returned = lax.all_to_all(
        grad_back, "expert", split_axis=0, concat_axis=0, tiled=True
    ).reshape(-1, width)
    token_grad = jnp.sum(grad_returned[target].astype(jnp.float32), axis=1).astype(jnp.bfloat16)
    both_shards = lax.psum_scatter(
        jnp.concatenate(
            [
                lax.dot_general(
                    grad_act_buf,
                    expert_rows,
                    (((0,), (0,)), ((), ())),
                    preferred_element_type=jnp.float32,
                ),
                lax.dot_general(
                    hidden_buf,
                    grad_rows,
                    (((0,), (0,)), ((), ())),
                    preferred_element_type=jnp.float32,
                ),
            ],
            axis=1,
        ).astype(jnp.bfloat16),
        "fsdp",
        scatter_dimension=0,
        tiled=True,
    ).astype(jnp.float32)
    grad_in_shard = both_shards[:, :width]
    grad_out_shard = both_shards[:, width:]
    return (layer_out, token_grad, grad_in_shard[None], grad_out_shard[None])


def solution(mesh):
    return jax.shard_map(
        per_device,
        mesh=mesh,
        in_specs=(
            P(("fsdp", "expert"), None),
            P(("fsdp", "expert"), None),
            P(("fsdp", "expert"), None),
            P("expert", "fsdp", None),
            P("expert", "fsdp", None),
            P(("fsdp", "expert"), None),
        ),
        out_specs=(
            P(("fsdp", "expert"), None),
            P(("fsdp", "expert"), None),
            P("expert", "fsdp", None),
            P("expert", "fsdp", None),
        ),
        check_vma=False,
    )
```

profile of v0, /device:TPU:16, one launch (start us, length us, event | category | flops | bytes accessed | tf_op | source)
XLA Modules:
  0.0 204.3 jit_solution(10741326995501521809)
XLA Ops:
  7.2 2.3 %pad_maximum_fusion.1 = bf16[2,256,1024]{2,1,0:T(8,128)(2,1)} fusion(bf16[1,256,1024]{2,1,0:T(8,128)(2,1)} %param.10, bf16[1,256,1024]{2,1,0:T(8,128)(2,1)} %param.9), kind=kLoop, calls=%fused_computation.40 | loop fusion | flops 524288 | bytes 2097152 | tf_op jit(solution)/shard_map/concatenate | solution.py:12
  11.5 1.9 gather_fusion.2
  13.7 1.4 convolution_convert_fusion.2
  15.1 11.3 %all-to-all-start = ((bf16[32,16,1024]{2,1,0:T(8,128)(2,1)}), bf16[32,16,1024]{2,1,0:T(8,128)(2,1)S(1)}, u32[]{:S(2)}, u32[]{:S(2)}) async-start(bf16[32,16,1024]{2,1,0:T(8,128)(2,1)} %bitcast.3), calls=%async_computation | async-start | bytes 2097152 | tf_op jit(solution)/shard_map/all_to_all | solution.py:42
  26.6 1.5 multiply_convert_fusion
  28.1 26.9 %all-to-all-done = bf16[32,16,1024]{2,1,0:T(8,128)(2,1)S(1)} async-done(((bf16[32,16,1024]{2,1,0:T(8,128)(2,1)}), bf16[32,16,1024]{2,1,0:T(8,128)(2,1)S(1)}, u32[]{:S(2)}, u32[]{:S(2)}) %all-to-all-start) | async-done | bytes 1048608 | tf_op jit(solution)/shard_map/all_to_all | solution.py:42
  55.1 5.1 %all-to-all-start.2 = ((bf16[32,16,1024]{2,1,0:T(8,128)(2,1)}), bf16[32,16,1024]{2,1,0:T(8,128)(2,1)S(1)}, u32[]{:S(2)}, u32[]{:S(2)}) async-start(bf16[32,16,1024]{2,1,0:T(8,128)(2,1)} %bitcast.11), calls=%async_computation.2 | async-start | bytes 2097152 | tf_op jit(solution)/shard_map/all_to_all | solution.py:78
  60.2 4.1 %all-gather.2.cloned.1.call-done = bf16[2,2048,1024]{2,1,0:T(8,128)(2,1)} async-done(((bf16[2,256,1024]{2,1,0:T(8,128)(2,1)}), bf16[2,2048,1024]{2,1,0:T(8,128)(2,1)}) %all-gather.2.cloned.1.call-update) | async-done | bytes 8388624 | tf_op jit(solution)/shard_map/all_gather | solution.py:13
  64.3 6.5 %fusion.18 = f32[512,2048]{1,0:T(8,128)} fusion(bf16[512,1024]{1,0:T(8,128)(2,1)S(1)} %bitcast.48, bf16[2,2048,1024]{2,1,0:T(8,128)(2,1)} %all-gather.2.cloned.1.call-done), kind=kOutput, calls=%fused_computation.31 | convolution fusion | flops 2147483648 | bytes 9437184 | tf_op jit(solution)/shard_map/dot_general | solution.py:55
  70.8 17.6 %all-to-all-done.2 = bf16[32,16,1024]{2,1,0:T(8,128)(2,1)S(1)} async-done(((bf16[32,16,1024]{2,1,0:T(8,128)(2,1)}), bf16[32,16,1024]{2,1,0:T(8,128)(2,1)S(1)}, u32[]{:S(2)}, u32[]{:S(2)}) %all-to-all-start.2) | async-done | bytes 1048608 | tf_op jit(solution)/shard_map/all_to_all | solution.py:78
  88.4 6.8 %convolution_convert_fusion = bf16[2048,1024]{0,1:T(8,128)(2,1)} fusion(bf16[512,1024]{1,0:T(8,128)(2,1)S(1)} %bitcast.50, f32[512,2048]{1,0:T(8,128)} %fusion.18), kind=kOutput, calls=%fused_computation.28 | convolution fusion | flops 2159017984 | bytes 9437184 | tf_op jit(solution)/shard_map/dot_general | solution.py:105
  95.3 4.7 %fusion.3 = bf16[512,2048]{1,0:T(8,128)(2,1)S(1)} fusion(f32[512,2048]{1,0:T(8,128)S(1)} %copy-done.5, bf16[512,1024]{1,0:T(8,128)(2,1)S(1)} %bitcast.51, bf16[2,2048,1024]{2,1,0:T(8,128)(2,1)S(1)} %copy-done.4), kind=kOutput, calls=%fused_computation.12 | convolution fusion | flops 2170552320 | bytes 11534336 | tf_op jit(solution)/shard_map/dot_general | solution.py:84
  100.0 1.3 copy-done.6
  101.3 4.4 %convolution_convert_fusion.1 = bf16[2048,1024]{0,1:T(8,128)(2,1)} fusion(bf16[512,2048]{1,0:T(8,128)(2,1)S(1)} %fusion.3, bf16[512,1024]{1,0:T(8,128)(2,1)S(1)} %bitcast.49), kind=kOutput, calls=%fused_computation.29 | convolution fusion | flops 2149580800 | bytes 7340032 | tf_op jit(solution)/shard_map/dot_general | solution.py:99
  105.7 8.4 %pad_maximum_fusion = bf16[2048,2048]{0,1:T(8,128)(2,1)} fusion(bf16[2048,1024]{0,1:T(8,128)(2,1)} %convolution_convert_fusion, bf16[2048,1024]{0,1:T(8,128)(2,1)} %convolution_convert_fusion.1), kind=kLoop, calls=%fused_computation.3 | loop fusion | flops 16777216 | bytes 16777216 | tf_op jit(solution)/shard_map/concatenate | solution.py:97
  114.0 7.2 %fusion.21 = bf16[512,1024]{1,0:T(8,128)(2,1)} fusion(bf16[2,2048,1024]{2,1,0:T(8,128)(2,1)} %all-gather.2.cloned.1.call-done, f32[512,2048]{1,0:T(8,128)} %fusion.18), kind=kOutput, calls=%fused_computation.36 | convolution fusion | flops 2157445120 | bytes 9437184 | tf_op jit(solution)/shard_map/dot_general | solution.py:59
  121.3 4.9 %all-to-all-start.1 = ((bf16[32,16,1024]{2,1,0:T(8,128)(2,1)}), bf16[32,16,1024]{2,1,0:T(8,128)(2,1)S(1)}, u32[]{:S(2)}, u32[]{:S(2)}) async-start(bf16[32,16,1024]{2,1,0:T(8,128)(2,1)} %bitcast.7), calls=%async_computation.1 | async-start | bytes 2097152 | tf_op jit(solution)/shard_map/all_to_all | solution.py:69
  126.2 5.6 %fusion.22 = bf16[512,1024]{1,0:T(8,128)(2,1)} fusion(bf16[512,2048]{1,0:T(8,128)(2,1)S(1)} %copy-done.7, bf16[2,2048,1024]{2,1,0:T(8,128)(2,1)} %all-gather.2.cloned.1.call-done), kind=kOutput, calls=%fused_computation.37 | convolution fusion | flops 2148007936 | bytes 7340032 | tf_op jit(solution)/shard_map/dot_general | solution.py:89
  131.8 22.7 %all-to-all-done.1 = bf16[32,16,1024]{2,1,0:T(8,128)(2,1)S(1)} async-done(((bf16[32,16,1024]{2,1,0:T(8,128)(2,1)}), bf16[32,16,1024]{2,1,0:T(8,128)(2,1)S(1)}, u32[]{:S(2)}, u32[]{:S(2)}) %all-to-all-start.1) | async-done | bytes 1048608 | tf_op jit(solution)/shard_map/all_to_all | solution.py:69
  154.5 5.2 %all-to-all-start.3 = ((bf16[32,16,1024]{2,1,0:T(8,128)(2,1)}), bf16[32,16,1024]{2,1,0:T(8,128)(2,1)S(1)}, u32[]{:S(2)}, u32[]{:S(2)}) async-start(bf16[32,16,1024]{2,1,0:T(8,128)(2,1)} %bitcast.13), calls=%async_computation.3 | async-start | bytes 2097152 | tf_op jit(solution)/shard_map/all_to_all | solution.py:92
  161.9 25.8 %all-to-all-done.3 = bf16[32,16,1024]{2,1,0:T(8,128)(2,1)S(1)} async-done(((bf16[32,16,1024]{2,1,0:T(8,128)(2,1)}), bf16[32,16,1024]{2,1,0:T(8,128)(2,1)S(1)}, u32[]{:S(2)}, u32[]{:S(2)}) %all-to-all-start.3) | async-done | bytes 1048608 | tf_op jit(solution)/shard_map/all_to_all | solution.py:92
  189.1 2.1 %reduce_sum.42 = bf16[128,1024]{1,0:T(8,128)(2,1)} reduce(bf16[128,2,1024]{2,1,0:T(2,128)(2,1)S(1)} %reshape.70, bf16[]{:T(256)} %constant.40.clone.1), dimensions={1}, to_apply=%region_4.5 | reduce | flops 131072 | bytes 786434 | tf_op jit(solution)/shard_map/reduce_sum | solution.py:95
  191.2 2.1 %multiply_reduce_fusion = bf16[128,1024]{1,0:T(8,128)(2,1)} fusion(f32[128,2,1024]{2,1,0:T(2,128)S(1)} %reshape.83, f32[128,2]{1,0:T(8,128)S(1)} %copy.53), kind=kLoop, calls=%fused_computation.41 | loop fusion | flops 393216 | bytes 1311744 | tf_op jit(solution)/shard_map/reduce_sum | solution.py:73
  193.3 1.4 convert_element_type.51
  (44 shorter events, 8.8 us)
Async XLA Ops:
  7.2 6.6 %copy-start = (bf16[128,1024]{1,0:T(8,128)(2,1)S(1)}, bf16[128,1024]{1,0:T(8,128)(2,1)}, u32[]{:S(2)}) copy-start(bf16[128,1024]{1,0:T(8,128)(2,1)} %param.6) | copy-start | bytes 786436
  7.2 57.2 %all-gather.2.cloned.1.call-start = ((), (), s32[]{:S(2)}) async-start(), calls=%async_computation.5 | async-start | bytes 9437184 | tf_op jit(solution)/shard_map/all_gather | solution.py:13
  11.5 2.2 %copy-start.2 = (s32[128,2]{0,1:T(2,128)S(1)}, s32[128,2]{0,1:T(2,128)}, u32[]{:S(2)}) copy-start(s32[128,2]{0,1:T(2,128)} %param.7) | copy-start | bytes 3076
  11.5 15.0 %copy-start.3 = (f32[128,2]{0,1:T(2,128)S(1)}, f32[128,2]{0,1:T(2,128)}, u32[]{:S(2)}) copy-start(f32[128,2]{0,1:T(2,128)} %param.8) | copy-start | bytes 3076
  11.5 15.1 %copy-start.1 = (bf16[128,1024]{1,0:T(8,128)(2,1)S(1)}, bf16[128,1024]{1,0:T(8,128)(2,1)}, u32[]{:S(2)}) copy-start(bf16[128,1024]{1,0:T(8,128)(2,1)} %param.11) | copy-start | bytes 786436
  15.1 39.9 %all-to-all-start = ((bf16[32,16,1024]{2,1,0:T(8,128)(2,1)}), bf16[32,16,1024]{2,1,0:T(8,128)(2,1)S(1)}, u32[]{:S(2)}, u32[]{:S(2)}) async-start(bf16[32,16,1024]{2,1,0:T(8,128)(2,1)} %bitcast.3), calls=%async_computation | async-start | bytes 2097152 | tf_op jit(solution)/shard_map/all_to_all | solution.py:42
  55.1 33.4 %all-to-all-start.2 = ((bf16[32,16,1024]{2,1,0:T(8,128)(2,1)}), bf16[32,16,1024]{2,1,0:T(8,128)(2,1)S(1)}, u32[]{:S(2)}, u32[]{:S(2)}) async-start(bf16[32,16,1024]{2,1,0:T(8,128)(2,1)} %bitcast.11), calls=%async_computation.2 | async-start | bytes 2097152 | tf_op jit(solution)/shard_map/all_to_all | solution.py:78
  60.2 133.1 %reduce-scatter.2.cloned.1.call-start = ((), (), s32[]{:S(2)}) async-start(), calls=%async_computation.6 | async-start | bytes 9437184 | tf_op jit(solution)/shard_map/reduce_scatter | solution.py:96
  88.4 6.8 %copy-start.4 = (bf16[2,2048,1024]{2,1,0:T(8,128)(2,1)S(1)}, bf16[2,2048,1024]{2,1,0:T(8,128)(2,1)}, u32[]{:S(2)}) copy-start(bf16[2,2048,1024]{2,1,0:T(8,128)(2,1)} %all-gather.2.cloned.1.call-done) | copy-start | bytes 25165828
  88.4 6.8 %copy-start.5 = (f32[512,2048]{1,0:T(8,128)S(1)}, f32[512,2048]{1,0:T(8,128)}, u32[]{:S(2)}) copy-start(f32[512,2048]{1,0:T(8,128)} %fusion.18) | copy-start | bytes 12582916
  100.0 1.3 copy-start.6
  114.0 12.2 %copy-start.7 = (bf16[512,2048]{1,0:T(8,128)(2,1)S(1)}, bf16[512,2048]{1,0:T(8,128)(2,1)}, u32[]{:S(2)}) copy-start(bf16[512,2048]{1,0:T(8,128)(2,1)} %copy-done.6) | copy-start | bytes 6291460
  121.3 33.2 %all-to-all-start.1 = ((bf16[32,16,1024]{2,1,0:T(8,128)(2,1)}), bf16[32,16,1024]{2,1,0:T(8,128)(2,1)S(1)}, u32[]{:S(2)}, u32[]{:S(2)}) async-start(bf16[32,16,1024]{2,1,0:T(8,128)(2,1)} %bitcast.7), calls=%async_computation.1 | async-start | bytes 2097152 | tf_op jit(solution)/shard_map/all_to_all | solution.py:69
  154.5 33.2 %all-to-all-start.3 = ((bf16[32,16,1024]{2,1,0:T(8,128)(2,1)}), bf16[32,16,1024]{2,1,0:T(8,128)(2,1)S(1)}, u32[]{:S(2)}, u32[]{:S(2)}) async-start(bf16[32,16,1024]{2,1,0:T(8,128)(2,1)} %bitcast.13), calls=%async_computation.3 | async-start | bytes 2097152 | tf_op jit(solution)/shard_map/all_to_all | solution.py:92
Sparse Core Ops, SparseCore 0:
  10.4 53.8 all-gather.1
  114.2 49.2 reduce-scatter.1
where the time goes:
time: 205 us; the launch traced here: 204 us
  waiting for transfers between devices  97.2 us (47%)
  matrix products  38.1 us (19%)
  starting transfers between devices  26.6 us (13%)
  other arithmetic  18 us (9%)
  between operations  14.3 us (7%)
  local copies, waits for them, and re-layouts  10.2 us (5%)
    all_to_all x1, waiting for transfers between devices, per_device(): lax.all_to_all(outgoing.reshape(expert_count, capacity, width), 'expert',...  26.9 us
    all_to_all x1, waiting for transfers between devices, per_device(): lax.all_to_all(grad_back, 'expert', split_axis=0, concat_axis=0, tiled=True)  25.8 us
    all_to_all x1, waiting for transfers between devices, per_device(): lax.all_to_all(expert_out, 'expert', split_axis=0, concat_axis=0, tiled=T...  22.7 us
    all_to_all x1, waiting for transfers between devices, per_device(): lax.all_to_all(grad_cells, 'expert', split_axis=0, concat_axis=0, tiled=T...  17.6 us
    all_to_all x1, starting transfers between devices, per_device(): lax.all_to_all(outgoing.reshape(expert_count, capacity, width), 'expert',...  11.3 us
    concatenate x1, other arithmetic, per_device(): jnp.concatenate([lax.dot_general(grad_act_buf, expert_rows, (((0,), (0,))...  8.36 us
    dot_general x1, matrix products, per_device(): summed = jnp.dot(hidden, part_out, preferred_element_type=jnp.float32)  7.23 us
    dot_general x1, matrix products, per_device(): lax.dot_general(hidden_buf, grad_rows, (((0,), (0,)), ((), ())), preferre...  6.83 us
  transfers between devices with their start and end apart: 6, of which 5 were waited for; matrix products, arithmetic and copies ran while one was open for 17% of the time, Pallas kernels for 0%

commit v1 on v0

v1 whole, which is shorter than its diff:
```python
import functools

import jax
import jax.numpy as jnp
from jax import lax
from jax.experimental import pallas as pl
from jax.experimental.pallas import tpu as pltpu
from jax.sharding import PartitionSpec as P


PAIR_A = [(2 * y + c, 2 * (y ^ 1) + c) for y in range(4) for c in range(2)]
PAIR_B = [(2 * y + c, 2 * (3 - y) + c) for y in range(4) for c in range(2)]
PAIR_C = [(f, f ^ 1) for f in range(8)]
F32 = jnp.float32
BF16 = jnp.bfloat16


def place_kernel(
    experts, ids_hbm, gate_hbm, tok_hbm, cells_ref, place_ref, hi_ref, lo_ref, ids_ref, gate_ref, tok_ref, sems
):
    copies = [
        pltpu.make_async_copy(a, b, sems.at[i])
        for i, (a, b) in enumerate([(ids_hbm, ids_ref), (gate_hbm, gate_ref), (tok_hbm, tok_ref)])
    ]
    for copy in copies:
        copy.start()
    copies[0].wait()
    cells, n = place_ref.shape
    capacity = cells // experts
    ids0, ids1 = ids_ref[0:1, :], ids_ref[1:2, :]
    label = lax.broadcasted_iota(jnp.int32, (experts, n), 0)
    oh0, oh1 = ids0 == label, ids1 == label
    hit = jnp.where(oh0 | oh1, 1.0, 0.0).astype(BF16)
    before = lax.broadcasted_iota(jnp.int32, (n, n), 0) < lax.broadcasted_iota(jnp.int32, (n, n), 1)
    earlier = jnp.dot(hit, jnp.where(before, 1.0, 0.0).astype(BF16), preferred_element_type=F32)
    slot0 = jnp.sum(jnp.where(oh0, earlier, 0.0), axis=0, keepdims=True).astype(jnp.int32)
    slot1 = jnp.sum(jnp.where(oh1, earlier, 0.0), axis=0, keepdims=True).astype(jnp.int32)
    cell = lax.broadcasted_iota(jnp.int32, (cells, n), 0)
    at0 = cell == ids0 * capacity + slot0
    at1 = cell == ids1 * capacity + slot1
    place = jnp.where(at0 | at1, 1.0, 0.0).astype(BF16)
    place_ref[...] = place
    copies[1].wait()
    gate = jnp.where(at0, gate_ref[0:1, :], 0.0) + jnp.where(at1, gate_ref[1:2, :], 0.0)
    hi = gate.astype(BF16)
    hi_ref[...] = hi
    lo_ref[...] = (gate - hi.astype(F32)).astype(BF16)
    copies[2].wait()
    cells_ref[...] = jnp.dot(place, tok_ref[...], preferred_element_type=F32).astype(BF16)


def scatter_kernel(hi_ref, lo_ref, cot_ref, cells_ref):
    cot = cot_ref[...]
    cells_ref[...] = (
        jnp.dot(hi_ref[...], cot, preferred_element_type=F32)
        + jnp.dot(lo_ref[...], cot, preferred_element_type=F32)
    ).astype(BF16)


def gated_kernel(hi_ref, lo_ref, rows_ref, out_ref):
    rows = rows_ref[...]
    out_ref[...] = (dot_0(hi_ref[...], rows) + dot_0(lo_ref[...], rows)).astype(BF16)


def plain_kernel(place_ref, rows_ref, out_ref):
    out_ref[...] = dot_0(place_ref[...], rows_ref[...]).astype(BF16)


def call(kernel, outs, *args, flops=3e8):
    shapes = [jax.ShapeDtypeStruct(s, d) for s, d in outs]
    return pl.pallas_call(
        kernel,
        out_shape=shapes if len(shapes) > 1 else shapes[0],
        in_specs=[pl.BlockSpec(memory_space=pltpu.VMEM)] * len(args),
        out_specs=[pl.BlockSpec(memory_space=pltpu.VMEM)] * len(shapes)
        if len(shapes) > 1
        else pl.BlockSpec(memory_space=pltpu.VMEM),
        cost_estimate=pl.CostEstimate(flops=int(flops), bytes_accessed=3 << 20, transcendentals=0),
        compiler_params=pltpu.CompilerParams(vmem_limit_bytes=16 << 20),
    )(*args)


def gelu_back(pre_act, upstream):
    _, pullback = jax.vjp(jax.nn.gelu, pre_act)
    return pullback(upstream)[0]


def dot_t(a, b):
    return lax.dot_general(a, b, (((1,), (1,)), ((), ())), preferred_element_type=F32)


def dot_0(a, b):
    return lax.dot_general(a, b, (((0,), (0,)), ((), ())), preferred_element_type=F32)


def exchange(rows, experts):
    count, width = rows.shape
    return lax.all_to_all(
        rows.reshape(experts, count // experts, width),
        "expert",
        split_axis=0,
        concat_axis=0,
        tiled=True,
    ).reshape(count, width)


def permute(x, pairs):
    return lax.ppermute(x, "fsdp", pairs)


def gather(shard, first, second):
    got = permute(shard, first)
    two = jnp.concatenate([shard, got], axis=0)
    other = permute(two, second)
    core_two = permute(two, PAIR_C)
    core_other = permute(other, PAIR_C)
    return two, other, core_two, core_other


def layer(tokens, expert_ids, gate_weights, weight_in, weight_out, cotangent):
    n, width = tokens.shape
    experts = lax.axis_size("expert")
    cells = 4 * n
    unit = weight_in.shape[1]
    in_a, in_b, in_ca, in_cb = gather(weight_in[0], PAIR_A, PAIR_B)
    out_a, out_b, out_ca, out_cb = gather(weight_out[0], PAIR_B, PAIR_A)

    tok_cells, place, hi, lo = pl.pallas_call(
        functools.partial(place_kernel, experts),
        out_shape=[jax.ShapeDtypeStruct((cells, width), BF16)] + [jax.ShapeDtypeStruct((cells, n), BF16)] * 3,
        in_specs=[pl.BlockSpec(memory_space=pl.ANY)] * 3,
        out_specs=[pl.BlockSpec(memory_space=pltpu.VMEM)] * 4,
        scratch_shapes=[
            pltpu.VMEM((2, n), jnp.int32),
            pltpu.VMEM((2, n), F32),
            pltpu.VMEM(tokens.shape, BF16),
            pltpu.SemaphoreType.DMA((3,)),
        ],
        cost_estimate=pl.CostEstimate(flops=1 << 28, bytes_accessed=3 << 20, transcendentals=0),
        compiler_params=pltpu.CompilerParams(vmem_limit_bytes=16 << 20),
    )(expert_ids.T, gate_weights.T, tokens)
    rows = exchange(tok_cells, experts)
    cot_cells = call(scatter_kernel, [((cells, width), BF16)], hi, lo, cotangent)
    grad_rows = exchange(cot_cells, experts)

    full_in = jnp.concatenate([in_a, in_b, in_ca, in_cb], axis=0)
    full_out = jnp.concatenate(
        [
            out_a[:unit],
            out_b[:unit],
            out_a[unit:],
            out_b[unit:],
            out_ca[:unit],
            out_cb[:unit],
            out_ca[unit:],
            out_cb[unit:],
        ],
        axis=0,
    )
    activation = dot_t(rows, full_in)
    hidden = jax.nn.gelu(activation).astype(BF16)
    stored = activation.astype(BF16)
    expert_out = jnp.dot(hidden, full_out, preferred_element_type=F32).astype(BF16)
    returned = exchange(expert_out, experts)

    half = 4 * unit
    part_out = dot_0(hidden, grad_rows)
    got = permute(part_out[half:].astype(BF16), PAIR_C)
    sum_out = part_out[:half] + got.astype(F32)
    grad_hidden = dot_t(grad_rows, full_out)
    grad_act = gelu_back(stored.astype(F32), grad_hidden).astype(BF16)
    part_in = dot_0(grad_act, rows)
    got = permute(part_in[half:].astype(BF16), PAIR_C)
    sum_in = part_in[:half] + got.astype(F32)
    grad_back = jnp.dot(grad_act, full_in, preferred_element_type=F32).astype(BF16)
    grad_returned = exchange(grad_back, experts)

    sum_in, sum_out = sum_in.astype(BF16), sum_out.astype(BF16)
    got = permute(jnp.concatenate([sum_out[unit : 2 * unit], sum_out[3 * unit :]], axis=0), PAIR_A)
    two_out = (
        jnp.concatenate([sum_out[:unit], sum_out[2 * unit : 3 * unit]], axis=0).astype(F32)
        + got.astype(F32)
    )
    got = permute(two_out[unit:].astype(BF16), PAIR_B)
    grad_out = two_out[:unit] + got.astype(F32)
    got = permute(sum_in[2 * unit :], PAIR_B)
    two_in = sum_in[: 2 * unit].astype(F32) + got.astype(F32)
    got = permute(two_in[unit:].astype(BF16), PAIR_A)
    grad_in = two_in[:unit] + got.astype(F32)

    layer_out = call(gated_kernel, [((n, width), BF16)], hi, lo, returned)
    token_grad = call(plain_kernel, [((n, width), BF16)], place, grad_returned)
    return (layer_out, token_grad, grad_in[None], grad_out[None])


def solution(mesh):
    rows = P(("fsdp", "expert"), None)
    weights = P("expert", "fsdp", None)
    return jax.shard_map(
        layer,
        mesh=mesh,
        in_specs=(rows, rows, rows, weights, weights, rows),
        out_specs=(rows, rows, weights, weights),
        check_vma=False,
    )
```

time: 205 us -> 191 us (0.932); the launches traced: 204 us -> 188 us
  waiting for transfers between devices: 97.2 us -> 74.8 us
  between operations: 14.3 us -> 0.98 us
  local copies, waits for them, and re-layouts: 10.2 us -> 22 us
  starting transfers between devices: 26.6 us -> 37.6 us
  matrix products: 38.1 us -> 32.3 us
  Pallas kernels: 0 us -> 5.63 us
  other arithmetic: 18 us -> 14.8 us
    all_to_all x4, waiting for transfers between devices: 93 us -> 27.1 us  [exchange(): lax.all_to_all(rows.reshape(experts, count // experts, width), 'expert',...]
    ppermute x0 -> x14, waiting for transfers between devices: none -> 47.7 us  [permute(): return lax.ppermute(x, 'fsdp', pairs)]
    unnamed x19 -> x47, local copies, waits for them, and re-layouts: 4.08 us -> 17.3 us
    ppermute x0 -> x14, starting transfers between devices: none -> 8.33 us  [permute(): return lax.ppermute(x, 'fsdp', pairs)]
    concatenate x2 -> x3, other arithmetic: 10.7 us -> 3.18 us  [the longest x2 3.11 us: gather(): two = jnp.concatenate([shard, got], axis=0)]
    dot_general x8 -> x6, matrix products: 38.1 us -> 32.3 us  [the longest x2 12.4 us: dot_t(): lax.dot_general(a, b, (((1,), (1,)), ((), ())), preferred_element_type=F32)]
    pallas_call x0 -> x4, Pallas kernels: none -> 5.63 us  [the longest x3 3.89 us: call(): pl.pallas_call(kernel, out_shape=shapes if len(shapes) > 1 else shapes[0]...]
    reduce_sum x4 -> x0, other arithmetic: 5.01 us -> none  [the longest x1 2.09 us: per_device(): jnp.sum(grad_returned[target].astype(jnp.float32), axis=1)]
  transfers between devices with their start and end apart: 6 -> 18, of which waited for: 5 -> 9; matrix products, arithmetic and copies ran while one was open for 17% -> 26% of each run, Pallas kernels for 0% -> 2%
where the time goes in v1:
time: 191 us; the launch traced here: 188 us
  waiting for transfers between devices  74.8 us (39%)
  starting transfers between devices  37.6 us (20%)
  matrix products  32.3 us (17%)
  local copies, waits for them, and re-layouts  22 us (12%)
  other arithmetic  14.8 us (8%)
  Pallas kernels  5.63 us (3%)
    ppermute x14, waiting for transfers between devices, permute(): return lax.ppermute(x, 'fsdp', pairs)  47.7 us
    all_to_all x4, starting transfers between devices, exchange(): lax.all_to_all(rows.reshape(experts, count // experts, width), 'expert',...  29.2 us
    all_to_all x4, waiting for transfers between devices, exchange(): lax.all_to_all(rows.reshape(experts, count // experts, width), 'expert',...  27.1 us
    unnamed x47, local copies, waits for them, and re-layouts  17.3 us
    dot_general x2, matrix products, dot_t(): lax.dot_general(a, b, (((1,), (1,)), ((), ())), preferred_element_type=F32)  12.4 us
    dot_general x2, matrix products, dot_0(): lax.dot_general(a, b, (((0,), (0,)), ((), ())), preferred_element_type=F32)  9.96 us
    ppermute x14, starting transfers between devices, permute(): return lax.ppermute(x, 'fsdp', pairs)  8.33 us
    dot_general x1, matrix products, layer(): jnp.dot(grad_act, full_in, preferred_element_type=F32).astype(BF16)  6.27 us
  transfers between devices with their start and end apart: 18, of which 9 were waited for; matrix products, arithmetic and copies ran while one was open for 26% of the time, Pallas kernels for 2%

profile of v1, /device:TPU:16, one launch (start us, length us, event | category | flops | bytes accessed | tf_op | source)
XLA Modules:
  0.0 188.1 jit_solution(16772491689675521719)
XLA Ops:
  4.8 11.5 %all-to-all-start = ((bf16[32,16,1024]{2,1,0:T(8,128)(2,1)}), bf16[32,16,1024]{2,1,0:T(8,128)(2,1)}, u32[]{:S(2)}, u32[]{:S(2)}) async-start(bf16[32,16,1024]{2,1,0:T(8,128)(2,1)} %bitcast.2), calls=%async_computation | async-start | bytes 2097152 | tf_op jit(solution)/shard_map/all_to_all | solution.py:98
  17.8 12.1 %collective-permute-done.4 = bf16[256,1024]{1,0:T(8,128)(2,1)S(1)} collective-permute-done((bf16[256,1024]{1,0:T(8,128)(2,1)}, bf16[256,1024]{1,0:T(8,128)(2,1)S(1)}, u32[]{:S(2)}, u32[]{:S(2)}) %collective-permute-start.4) | collective-permute-done | bytes 524320 | tf_op jit(solution)/shard_map/ppermute | solution.py:108
  29.9 2.1 %pad_maximum_fusion.1 = bf16[512,1024]{1,0:T(8,128)(2,1)} fusion(bf16[256,1024]{1,0:T(8,128)(2,1)S(1)} %collective-permute-done.4, bf16[256,1024]{1,0:T(8,128)(2,1)} %bitcast.33), kind=kLoop, calls=%fused_computation.39 | loop fusion | flops 2097152 | bytes 2097152 | tf_op jit(solution)/shard_map/concatenate | solution.py:113
  32.0 2.5 %collective-permute-start.5 = (bf16[512,1024]{1,0:T(8,128)(2,1)}, bf16[512,1024]{1,0:T(8,128)(2,1)}, u32[]{:S(2)}, u32[]{:S(2)}) collective-permute-start(bf16[512,1024]{1,0:T(8,128)(2,1)} %pad_maximum_fusion.1), channel_id=1, source_target_pairs={{0,64},{32,96},{64,0},{96,32},{128,192},{160,224},{192,128},{224,1... | collective-permute-start | bytes 3145736 | tf_op jit(solution)/shard_map/ppermute | solution.py:108
  38.6 6.3 %all-to-all-done = bf16[32,16,1024]{2,1,0:T(8,128)(2,1)} async-done(((bf16[32,16,1024]{2,1,0:T(8,128)(2,1)}), bf16[32,16,1024]{2,1,0:T(8,128)(2,1)}, u32[]{:S(2)}, u32[]{:S(2)}) %all-to-all-start) | async-done | bytes 1048608 | tf_op jit(solution)/shard_map/all_to_all | solution.py:98
  44.8 5.2 %all-to-all-start.2 = ((bf16[32,16,1024]{2,1,0:T(8,128)(2,1)}), bf16[32,16,1024]{2,1,0:T(8,128)(2,1)}, u32[]{:S(2)}, u32[]{:S(2)}) async-start(bf16[32,16,1024]{2,1,0:T(8,128)(2,1)} %bitcast.8), calls=%async_computation.2 | async-start | bytes 2097152 | tf_op jit(solution)/shard_map/all_to_all | solution.py:98
  50.1 6.8 %collective-permute-done.5 = bf16[512,1024]{1,0:T(8,128)(2,1)} collective-permute-done((bf16[512,1024]{1,0:T(8,128)(2,1)}, bf16[512,1024]{1,0:T(8,128)(2,1)}, u32[]{:S(2)}, u32[]{:S(2)}) %collective-permute-start.5) | collective-permute-done | bytes 1048608 | tf_op jit(solution)/shard_map/ppermute | solution.py:108
  56.9 2.5 %collective-permute-done.1 = bf16[512,1024]{1,0:T(8,128)(2,1)} collective-permute-done((bf16[512,1024]{1,0:T(8,128)(2,1)}, bf16[512,1024]{1,0:T(8,128)(2,1)}, u32[]{:S(2)}, u32[]{:S(2)}) %collective-permute-start.1) | collective-permute-done | bytes 1048608 | tf_op jit(solution)/shard_map/ppermute | solution.py:108
  70.5 5.6 %fusion.25 = f32[512,2048]{1,0:T(8,128)} fusion(bf16[512,1024]{1,0:T(8,128)(2,1)} %bitcast.3, bf16[2048,1024]{1,0:T(8,128)(2,1)S(1)} %constant_dynamic-update-slice_fusion), kind=kOutput, calls=%fused_computation.56 | convolution fusion | flops 2147483648 | bytes 9437184 | tf_op jit(solution)/shard_map/dot_general | solution.py:89
  76.1 2.2 %all-to-all-done.2 = bf16[32,16,1024]{2,1,0:T(8,128)(2,1)} async-done(((bf16[32,16,1024]{2,1,0:T(8,128)(2,1)}), bf16[32,16,1024]{2,1,0:T(8,128)(2,1)}, u32[]{:S(2)}, u32[]{:S(2)}) %all-to-all-start.2) | async-done | bytes 1048608 | tf_op jit(solution)/shard_map/all_to_all | solution.py:98
  78.3 5.6 %fusion.21 = f32[2048,1024]{1,0:T(8,128)S(1)} fusion(bf16[512,1024]{1,0:T(8,128)(2,1)} %bitcast.9, f32[512,2048]{1,0:T(8,128)} %fusion.25), kind=kOutput, calls=%fused_computation.54 | convolution fusion | flops 2156920832 | bytes 13631488 | tf_op jit(solution)/shard_map/dot_general | solution.py:93
  85.5 6.8 %fusion.3 = bf16[512,2048]{1,0:T(8,128)(2,1)S(1)} fusion(f32[512,2048]{1,0:T(8,128)S(1)} %copy-done.17, bf16[512,1024]{1,0:T(8,128)(2,1)} %bitcast.9, bf16[2048,1024]{1,0:T(8,128)(2,1)S(1)} %slice_dynamic-update-slice_fusion), kind=kOutput, calls=%fused_computation.8 | convolution fusion | flops 2170552320 | bytes 11534336 | tf_op jit(solution)/shard_map/dot_general | solution.py:89
  92.3 4.4 %fusion.26 = f32[2048,1024]{1,0:T(8,128)S(1)} fusion(bf16[512,2048]{1,0:T(8,128)(2,1)S(1)} %fusion.3, bf16[512,1024]{1,0:T(8,128)(2,1)} %bitcast.3), kind=kOutput, calls=%fused_computation.57 | convolution fusion | flops 2147483648 | bytes 11534336 | tf_op jit(solution)/shard_map/dot_general | solution.py:93
  97.1 2.1 %slice.127 = bf16[1024,1024]{1,0:T(8,128)(2,1)} slice(f32[2048,1024]{1,0:T(8,128)S(1)} %fusion.21), slice={[1024:2048], [0:1024]} | slice | bytes 4194304 | tf_op jit(solution)/shard_map/slice | solution.py:168
  99.4 3.6 %convolution_convert_fusion.1 = bf16[512,1024]{1,0:T(8,128)(2,1)} fusion(bf16[2048,1024]{1,0:T(8,128)(2,1)S(1)} %slice_dynamic-update-slice_fusion, f32[512,2048]{1,0:T(8,128)S(1)} %copy-done.17), kind=kOutput, calls=%fused_computation.31 | convolution fusion | flops 2157445120 | bytes 9437184 | tf_op jit(solution)/shard_map/dot_general | solution.py:163
  103.0 7.4 %all-to-all-start.1 = ((bf16[32,16,1024]{2,1,0:T(8,128)(2,1)}), bf16[32,16,1024]{2,1,0:T(8,128)(2,1)S(1)}, u32[]{:S(2)}, u32[]{:S(2)}) async-start(bf16[32,16,1024]{2,1,0:T(8,128)(2,1)} %bitcast.36), calls=%async_computation.1 | async-start | bytes 2097152 | tf_op jit(solution)/shard_map/all_to_all | solution.py:98
  110.4 6.3 %convolution_convert_fusion = bf16[512,1024]{1,0:T(8,128)(2,1)} fusion(bf16[512,2048]{1,0:T(8,128)(2,1)} %copy-done.16, bf16[2048,1024]{1,0:T(8,128)(2,1)} %copy-done.15), kind=kOutput, calls=%fused_computation.30 | convolution fusion | flops 2148007936 | bytes 7340032 | tf_op jit(solution)/shard_map/dot_general | solution.py:175
  116.7 2.5 %fusion.18 = bf16[1024,1024]{1,0:T(8,128)(2,1)S(1)} fusion(f32[2048,1024]{1,0:T(8,128)S(1)} %copy-done.11, bf16[1024,1024]{1,0:T(8,128)(2,1)} %collective-permute-done.8), kind=kLoop, calls=%fused_computation.27 | loop fusion | flops 3145728 | bytes 8388608 | tf_op jit(solution)/shard_map/convert_element_type | solution.py:178
  120.8 18.7 %all-to-all-done.1 = bf16[32,16,1024]{2,1,0:T(8,128)(2,1)S(1)} async-done(((bf16[32,16,1024]{2,1,0:T(8,128)(2,1)}), bf16[32,16,1024]{2,1,0:T(8,128)(2,1)S(1)}, u32[]{:S(2)}, u32[]{:S(2)}) %all-to-all-start.1) | async-done | bytes 1048608 | tf_op jit(solution)/shard_map/all_to_all | solution.py:98
  139.6 5.2 %all-to-all-start.3 = ((bf16[32,16,1024]{2,1,0:T(8,128)(2,1)}), bf16[32,16,1024]{2,1,0:T(8,128)(2,1)S(1)}, u32[]{:S(2)}, u32[]{:S(2)}) async-start(bf16[32,16,1024]{2,1,0:T(8,128)(2,1)} %bitcast.10), calls=%async_computation.3 | async-start | bytes 2097152 | tf_op jit(solution)/shard_map/all_to_all | solution.py:98
  144.8 3.6 %fusion.17 = bf16[1024,1024]{1,0:T(8,128)(2,1)S(1)} fusion(f32[2048,1024]{1,0:T(8,128)} %copy-done.9, bf16[1024,1024]{1,0:T(8,128)(2,1)} %collective-permute-done.11), kind=kLoop, calls=%fused_computation.24 | loop fusion | flops 3145728 | bytes 8388608 | tf_op jit(solution)/shard_map/convert_element_type | solution.py:178
  154.1 20.7 %collective-permute-done.12 = bf16[512,1024]{1,0:T(8,128)(2,1)S(1)} collective-permute-done((bf16[512,1024]{1,0:T(8,128)(2,1)S(1)}, bf16[512,1024]{1,0:T(8,128)(2,1)S(1)}, u32[]{:S(2)}, u32[]{:S(2)}) %collective-permute-start.12) | collective-permute-done | bytes 1048608 | tf_op jit(solution)/shard_map/ppermute | solution.py:108
  178.9 5.4 %collective-permute-done.10 = bf16[256,1024]{1,0:T(8,128)(2,1)S(1)} collective-permute-done((bf16[256,1024]{1,0:T(8,128)(2,1)}, bf16[256,1024]{1,0:T(8,128)(2,1)S(1)}, u32[]{:S(2)}, u32[]{:S(2)}) %collective-permute-start.10) | collective-permute-done | bytes 524320 | tf_op jit(solution)/shard_map/ppermute | solution.py:108
  184.3 2.4 %fusion.20 = f32[1,256,1024]{2,1,0:T(8,128)} fusion(f32[512,1024]{1,0:T(8,128)} %copy-done.6, bf16[256,1024]{1,0:T(8,128)(2,1)S(1)} %collective-permute-done.10), kind=kLoop, calls=%fused_computation.37 | loop fusion | flops 524288 | bytes 2621440 | tf_op jit(solution)/shard_map/broadcast_in_dim | solution.py:193
  (86 shorter events, 35.8 us)
Async XLA Ops:
  0.6 34.9 %copy-start = (bf16[128,1024]{1,0:T(8,128)(2,1)S(1)}, bf16[128,1024]{1,0:T(8,128)(2,1)}, u32[]{:S(2)}) copy-start(bf16[128,1024]{1,0:T(8,128)(2,1)} %cot_ref.1) | copy-start | bytes 786436
  3.0 31.5 %copy-start.13 = (bf16[1,256,1024]{2,1,0:T(8,128)(2,1)S(1)}, bf16[1,256,1024]{2,1,0:T(8,128)(2,1)}, u32[]{:S(2)}) copy-start(bf16[1,256,1024]{2,1,0:T(8,128)(2,1)} %param.9) | copy-start | bytes 1572868
  3.0 34.2 %copy-start.12 = (bf16[1,256,1024]{2,1,0:T(8,128)(2,1)S(1)}, bf16[1,256,1024]{2,1,0:T(8,128)(2,1)}, u32[]{:S(2)}) copy-start(bf16[1,256,1024]{2,1,0:T(8,128)(2,1)} %param.10) | copy-start | bytes 1572868
  4.8 40.1 %all-to-all-start = ((bf16[32,16,1024]{2,1,0:T(8,128)(2,1)}), bf16[32,16,1024]{2,1,0:T(8,128)(2,1)}, u32[]{:S(2)}, u32[]{:S(2)}) async-start(bf16[32,16,1024]{2,1,0:T(8,128)(2,1)} %bitcast.2), calls=%async_computation | async-start | bytes 2097152 | tf_op jit(solution)/shard_map/all_to_all | solution.py:98
  16.2 13.7 %collective-permute-start.4 = (bf16[256,1024]{1,0:T(8,128)(2,1)}, bf16[256,1024]{1,0:T(8,128)(2,1)S(1)}, u32[]{:S(2)}, u32[]{:S(2)}) collective-permute-start(bf16[256,1024]{1,0:T(8,128)(2,1)} %bitcast.32), channel_id=1, source_target_pairs={{0,192},{32,224},{64,128},{96,160},{128,64},{160,96},{192,0},{224,... | collective-permute-start | bytes 1572872 | tf_op jit(solution)/shard_map/ppermute | solution.py:108
  16.8 17.7 %collective-permute-start = (bf16[256,1024]{1,0:T(8,128)(2,1)}, bf16[256,1024]{1,0:T(8,128)(2,1)S(1)}, u32[]{:S(2)}, u32[]{:S(2)}) collective-permute-start(bf16[256,1024]{1,0:T(8,128)(2,1)} %bitcast.34), channel_id=1, source_target_pairs={{0,64},{32,96},{64,0},{96,32},{128,192},{160,224},{192,128},{224,1... | collective-permute-start | bytes 1572872 | tf_op jit(solution)/shard_map/ppermute | solution.py:108
  32.0 24.9 %collective-permute-start.5 = (bf16[512,1024]{1,0:T(8,128)(2,1)}, bf16[512,1024]{1,0:T(8,128)(2,1)}, u32[]{:S(2)}, u32[]{:S(2)}) collective-permute-start(bf16[512,1024]{1,0:T(8,128)(2,1)} %pad_maximum_fusion.1), channel_id=1, source_target_pairs={{0,64},{32,96},{64,0},{96,32},{128,192},{160,224},{192,128},{224,1... | collective-permute-start | bytes 3145736 | tf_op jit(solution)/shard_map/ppermute | solution.py:108
  35.5 23.9 %collective-permute-start.1 = (bf16[512,1024]{1,0:T(8,128)(2,1)}, bf16[512,1024]{1,0:T(8,128)(2,1)}, u32[]{:S(2)}, u32[]{:S(2)}) collective-permute-start(bf16[512,1024]{1,0:T(8,128)(2,1)} %pad_maximum_fusion), channel_id=1, source_target_pairs={{0,192},{32,224},{64,128},{96,160},{128,64},{160,96},{192,0},{224,... | collective-permute-start | bytes 3145736 | tf_op jit(solution)/shard_map/ppermute | solution.py:108
  37.2 26.2 %collective-permute-start.2 = (bf16[512,1024]{1,0:T(8,128)(2,1)}, bf16[512,1024]{1,0:T(8,128)(2,1)}, u32[]{:S(2)}, u32[]{:S(2)}) collective-permute-start(bf16[512,1024]{1,0:T(8,128)(2,1)} %pad_maximum_fusion), channel_id=1, source_target_pairs={{0,32},{32,0},{64,96},{96,64},{128,160},{160,128},{192,224},{224,1... | collective-permute-start | bytes 3145736 | tf_op jit(solution)/shard_map/ppermute | solution.py:108
  38.0 28.6 %collective-permute-start.6 = (bf16[512,1024]{1,0:T(8,128)(2,1)}, bf16[512,1024]{1,0:T(8,128)(2,1)}, u32[]{:S(2)}, u32[]{:S(2)}) collective-permute-start(bf16[512,1024]{1,0:T(8,128)(2,1)} %pad_maximum_fusion.1), channel_id=1, source_target_pairs={{0,32},{32,0},{64,96},{96,64},{128,160},{160,128},{192,224},{224,1... | collective-permute-start | bytes 3145736 | tf_op jit(solution)/shard_map/ppermute | solution.py:108
  44.8 33.5 %all-to-all-start.2 = ((bf16[32,16,1024]{2,1,0:T(8,128)(2,1)}), bf16[32,16,1024]{2,1,0:T(8,128)(2,1)}, u32[]{:S(2)}, u32[]{:S(2)}) async-start(bf16[32,16,1024]{2,1,0:T(8,128)(2,1)} %bitcast.8), calls=%async_computation.2 | async-start | bytes 2097152 | tf_op jit(solution)/shard_map/all_to_all | solution.py:98
  56.9 27.0 %collective-permute-start.7 = (bf16[512,1024]{1,0:T(8,128)(2,1)}, bf16[512,1024]{1,0:T(8,128)(2,1)S(1)}, u32[]{:S(2)}, u32[]{:S(2)}) collective-permute-start(bf16[512,1024]{1,0:T(8,128)(2,1)} %collective-permute-done.5), channel_id=1, source_target_pairs={{0,32},{32,0},{64,96},{96,64},{128,160},{160,128},{192,224},{224,1... | collective-permute-start | bytes 3145736 | tf_op jit(solution)/shard_map/ppermute | solution.py:108
  59.4 9.1 %collective-permute-start.3 = (bf16[512,1024]{1,0:T(8,128)(2,1)}, bf16[512,1024]{1,0:T(8,128)(2,1)S(1)}, u32[]{:S(2)}, u32[]{:S(2)}) collective-permute-start(bf16[512,1024]{1,0:T(8,128)(2,1)} %collective-permute-done.1), channel_id=1, source_target_pairs={{0,32},{32,0},{64,96},{96,64},{128,160},{160,128},{192,224},{224,1... | collective-permute-start | bytes 3145736 | tf_op jit(solution)/shard_map/ppermute | solution.py:108
  83.9 13.2 %copy-start.9 = (f32[2048,1024]{1,0:T(8,128)}, f32[2048,1024]{1,0:T(8,128)S(1)}, u32[]{:S(2)}) copy-start(f32[2048,1024]{1,0:T(8,128)S(1)} %fusion.21) | copy-start | bytes 25165828
  97.0 19.6 %collective-permute-start.8 = (bf16[1024,1024]{1,0:T(8,128)(2,1)S(1)}, bf16[1024,1024]{1,0:T(8,128)(2,1)}, u32[]{:S(2)}, u32[]{:S(2)}) collective-permute-start(bf16[1024,1024]{1,0:T(8,128)(2,1)S(1)} %slice.128), channel_id=1, source_target_pairs={{0,32},{32,0},{64,96},{96,64},{128,160},{160,128},{192,224},{224,1... | collective-permute-start | bytes 6291464 | tf_op jit(solution)/shard_map/ppermute | solution.py:108
  99.3 45.5 %collective-permute-start.11 = (bf16[1024,1024]{1,0:T(8,128)(2,1)}, bf16[1024,1024]{1,0:T(8,128)(2,1)}, u32[]{:S(2)}, u32[]{:S(2)}) collective-permute-start(bf16[1024,1024]{1,0:T(8,128)(2,1)} %slice.127), channel_id=1, source_target_pairs={{0,32},{32,0},{64,96},{96,64},{128,160},{160,128},{192,224},{224,1... | collective-permute-start | bytes 6291464 | tf_op jit(solution)/shard_map/ppermute | solution.py:108
  103.0 36.6 %all-to-all-start.1 = ((bf16[32,16,1024]{2,1,0:T(8,128)(2,1)}), bf16[32,16,1024]{2,1,0:T(8,128)(2,1)S(1)}, u32[]{:S(2)}, u32[]{:S(2)}) async-start(bf16[32,16,1024]{2,1,0:T(8,128)(2,1)} %bitcast.36), calls=%async_computation.1 | async-start | bytes 2097152 | tf_op jit(solution)/shard_map/all_to_all | solution.py:98
  120.5 29.8 %collective-permute-start.9 = (bf16[512,1024]{1,0:T(8,128)(2,1)S(1)}, bf16[512,1024]{1,0:T(8,128)(2,1)}, u32[]{:S(2)}, u32[]{:S(2)}) collective-permute-start(bf16[512,1024]{1,0:T(8,128)(2,1)S(1)} %slice.93), channel_id=1, source_target_pairs={{0,192},{32,224},{64,128},{96,160},{128,64},{160,96},{192,0},{224,... | collective-permute-start | bytes 3145736 | tf_op jit(solution)/shard_map/ppermute | solution.py:108
  139.6 38.3 %all-to-all-start.3 = ((bf16[32,16,1024]{2,1,0:T(8,128)(2,1)}), bf16[32,16,1024]{2,1,0:T(8,128)(2,1)S(1)}, u32[]{:S(2)}, u32[]{:S(2)}) async-start(bf16[32,16,1024]{2,1,0:T(8,128)(2,1)} %bitcast.10), calls=%async_computation.3 | async-start | bytes 2097152 | tf_op jit(solution)/shard_map/all_to_all | solution.py:98
  148.7 26.1 %collective-permute-start.12 = (bf16[512,1024]{1,0:T(8,128)(2,1)S(1)}, bf16[512,1024]{1,0:T(8,128)(2,1)S(1)}, u32[]{:S(2)}, u32[]{:S(2)}) collective-permute-start(bf16[512,1024]{1,0:T(8,128)(2,1)S(1)} %pad_maximum_fusion.2), channel_id=1, source_target_pairs={{0,64},{32,96},{64,0},{96,32},{128,192},{160,224},{192,128},{224,1... | collective-permute-start | bytes 3145736 | tf_op jit(solution)/shard_map/ppermute | solution.py:108
  151.9 24.6 %copy-start.6 = (f32[512,1024]{1,0:T(8,128)}, f32[512,1024]{1,0:T(8,128)S(1)}, u32[]{:S(2)}) copy-start(f32[512,1024]{1,0:T(8,128)S(1)} %convert_add_fusion.2) | copy-start | bytes 6291460
  152.9 31.4 %collective-permute-start.10 = (bf16[256,1024]{1,0:T(8,128)(2,1)}, bf16[256,1024]{1,0:T(8,128)(2,1)S(1)}, u32[]{:S(2)}, u32[]{:S(2)}) collective-permute-start(bf16[256,1024]{1,0:T(8,128)(2,1)} %slice.130), channel_id=1, source_target_pairs={{0,64},{32,96},{64,0},{96,32},{128,192},{160,224},{192,128},{224,1... | collective-permute-start | bytes 1572872 | tf_op jit(solution)/shard_map/ppermute | solution.py:108
  176.2 10.8 %collective-permute-start.13 = (bf16[256,1024]{1,0:T(8,128)(2,1)}, bf16[256,1024]{1,0:T(8,128)(2,1)S(1)}, u32[]{:S(2)}, u32[]{:S(2)}) collective-permute-start(bf16[256,1024]{1,0:T(8,128)(2,1)} %slice.129), channel_id=1, source_target_pairs={{0,192},{32,224},{64,128},{96,160},{128,64},{160,96},{192,0},{224,... | collective-permute-start | bytes 1572872 | tf_op jit(solution)/shard_map/ppermute | solution.py:108
  177.9 9.1 %copy-start.8 = (f32[512,1024]{1,0:T(8,128)S(1)}, f32[512,1024]{1,0:T(8,128)}, u32[]{:S(2)}) copy-start(f32[512,1024]{1,0:T(8,128)} %copy-done.7) | copy-start | bytes 6291460
  (12 other events, 38.9 us)

commit v2 on v1

--- a/solution.py
+++ b/solution.py
@@ -66,6 +66,33 @@
     out_ref[...] = dot_0(place_ref[...], rows_ref[...]).astype(BF16)
 
 
+def pack_kernel(unit, *refs):
+    in_a, in_b, in_ca, in_cb, out_a, out_b, out_ca, out_cb, full_in, full_out, sems = refs
+    pieces = []
+    for at, (first, second) in enumerate([(in_a, in_b), (in_ca, in_cb)]):
+        for place, (ref, row) in enumerate([(first, 0), (first, 1), (second, 1), (second, 0)]):
+            pieces.append((ref, row, full_in, 4 * at + place))
+    for at, (first, second) in enumerate([(out_a, out_b), (out_ca, out_cb)]):
+        for place, (ref, row) in enumerate([(first, 0), (second, 0), (second, 1), (first, 1)]):
+            pieces.append((ref, row, full_out, 4 * at + place))
+    copies = [
+        pltpu.make_async_copy(
+            ref.at[pl.ds(row * unit, unit)], full.at[pl.ds(to * unit, unit)], sems.at[i]
+        )
+        for i, (ref, row, full, to) in enumerate(pieces)
+    ]
+    for copy in copies:
+        copy.start()
+    for copy in copies:
+        copy.wait()
+
+
+def finish_kernel(own_l_ref, got_l_ref, own_r_ref, got_r_ref, out_ref):
+    half = own_l_ref.shape[1]
+    out_ref[:, :half] = own_l_ref[...] + got_l_ref[...].astype(F32)
+    out_ref[:, half:] = own_r_ref[...] + got_r_ref[...].astype(F32)
+
+
 def call(kernel, outs, *args, flops=3e8):
     shapes = [jax.ShapeDtypeStruct(s, d) for s, d in outs]
     return pl.pallas_call(
@@ -117,6 +144,20 @@
     return two, other, core_two, core_other
 
 
+def scatter(total, unit):
+    half = total.shape[1] // 2
+    left, right = total[:, :half], total[:, half:]
+    got_l = permute(left[unit : 3 * unit], PAIR_A)
+    got_r = permute(right[2 * unit :], PAIR_B)
+    own_l = left[:unit].astype(F32) + got_l[:unit].astype(F32)
+    next_l = left[3 * unit :].astype(F32) + got_l[unit:].astype(F32)
+    own_r = right[:unit].astype(F32) + got_r[unit:].astype(F32)
+    next_r = right[unit : 2 * unit].astype(F32) + got_r[:unit].astype(F32)
+    got_l = permute(next_l.astype(BF16), PAIR_B)
+    got_r = permute(next_r.astype(BF16), PAIR_A)
+    return call(finish_kernel, [((unit, 2 * half), F32)], own_l, got_l, own_r, got_r)
+
+
 def layer(tokens, expert_ids, gate_weights, weight_in, weight_out, cotangent):
     n, width = tokens.shape
     experts = lax.axis_size("expert")
@@ -128,7 +169,7 @@
     tok_cells, place, hi, lo = pl.pallas_call(
         functools.partial(place_kernel, experts),
         out_shape=[jax.ShapeDtypeStruct((cells, width), BF16)] + [jax.ShapeDtypeStruct((cells, n), BF16)] * 3,
-        in_specs=[pl.BlockSpec(memory_space=pl.ANY)] * 3,
+        in_specs=[pl.BlockSpec(memory_space=pltpu.HBM)] * 3,
         out_specs=[pl.BlockSpec(memory_space=pltpu.VMEM)] * 4,
         scratch_shapes=[
             pltpu.VMEM((2, n), jnp.int32),
@@ -143,20 +184,15 @@
     cot_cells = call(scatter_kernel, [((cells, width), BF16)], hi, lo, cotangent)
     grad_rows = exchange(cot_cells, experts)
 
-    full_in = jnp.concatenate([in_a, in_b, in_ca, in_cb], axis=0)
-    full_out = jnp.concatenate(
-        [
-            out_a[:unit],
-            out_b[:unit],
-            out_a[unit:],
-            out_b[unit:],
-            out_ca[:unit],
-            out_cb[:unit],
-            out_ca[unit:],
-            out_cb[unit:],
-        ],
-        axis=0,
-    )
+    full_in, full_out = pl.pallas_call(
+        functools.partial(pack_kernel, unit),
+        out_shape=[jax.ShapeDtypeStruct((8 * unit, width), BF16)] * 2,
+        in_specs=[pl.BlockSpec(memory_space=pl.ANY)] * 8,
+        out_specs=[pl.BlockSpec(memory_space=pltpu.VMEM)] * 2,
+        scratch_shapes=[pltpu.SemaphoreType.DMA((16,))],
+        cost_estimate=pl.CostEstimate(flops=0, bytes_accessed=16 << 20, transcendentals=0),
+        compiler_params=pltpu.CompilerParams(vmem_limit_bytes=16 << 20),
+    )(in_a, in_b, in_ca, in_cb, out_a, out_b, out_ca, out_cb)
     activation = dot_t(rows, full_in)
     hidden = jax.nn.gelu(activation).astype(BF16)
     stored = activation.astype(BF16)
@@ -175,18 +211,8 @@
     grad_back = jnp.dot(grad_act, full_in, preferred_element_type=F32).astype(BF16)
     grad_returned = exchange(grad_back, experts)
 
-    sum_in, sum_out = sum_in.astype(BF16), sum_out.astype(BF16)
-    got = permute(jnp.concatenate([sum_out[unit : 2 * unit], sum_out[3 * unit :]], axis=0), PAIR_A)
-    two_out = (
-        jnp.concatenate([sum_out[:unit], sum_out[2 * unit : 3 * unit]], axis=0).astype(F32)
-        + got.astype(F32)
-    )
-    got = permute(two_out[unit:].astype(BF16), PAIR_B)
-    grad_out = two_out[:unit] + got.astype(F32)
-    got = permute(sum_in[2 * unit :], PAIR_B)
-    two_in = sum_in[: 2 * unit].astype(F32) + got.astype(F32)
-    got = permute(two_in[unit:].astype(BF16), PAIR_A)
-    grad_in = two_in[:unit] + got.astype(F32)
+    grad_out = scatter(sum_out.astype(BF16), unit)
+    grad_in = scatter(sum_in.astype(BF16), unit)
 
     layer_out = call(gated_kernel, [((n, width), BF16)], hi, lo, returned)
     token_grad = call(plain_kernel, [((n, width), BF16)], place, grad_returned)

time: 191 us -> 177 us (0.927)
  waiting for transfers between devices: 74.8 us -> 56.6 us
  starting transfers between devices: 37.6 us -> 52.8 us
  local copies, waits for them, and re-layouts: 22 us -> 14.9 us
  Pallas kernels: 5.63 us -> 12.5 us
  matrix products: 32.3 us -> 26.5 us
  other arithmetic: 14.8 us -> 11.1 us
    all_to_all x4, waiting for transfers between devices: 27.1 us -> 16.4 us  [exchange(): lax.all_to_all(rows.reshape(experts, count // experts, width), 'expert',...]
    ppermute x14 -> x18, starting transfers between devices: 8.33 us -> 18.3 us  [permute(): return lax.ppermute(x, 'fsdp', pairs)]
    ppermute x14 -> x18, waiting for transfers between devices: 47.7 us -> 40.2 us  [permute(): return lax.ppermute(x, 'fsdp', pairs)]
    unnamed x47 -> x30, local copies, waits for them, and re-layouts: 17.3 us -> 11.3 us
    all_to_all x4, starting transfers between devices: 29.2 us -> 34.5 us  [exchange(): lax.all_to_all(rows.reshape(experts, count // experts, width), 'expert',...]
    pallas_call x3 -> x5, Pallas kernels: 3.89 us -> 8.04 us  [call(): pl.pallas_call(kernel, out_shape=shapes if len(shapes) > 1 else shapes[0]...]
    broadcast_in_dim x2 -> x0, other arithmetic: 3.54 us -> none  [layer(): return (layer_out, token_grad, grad_in[None], grad_out[None])]
    dot_general x1, matrix products: 6.27 us -> 3.32 us  [layer(): jnp.dot(grad_act, full_in, preferred_element_type=F32).astype(BF16)]
  transfers between devices with their start and end apart: 18 -> 22, of which waited for: 9 -> 9; matrix products, arithmetic and copies ran while one was open for 26% -> 23% of each run, Pallas kernels for 2% -> 6%
where the time goes in v2:
time: 177 us; the launch traced here: 175 us
  waiting for transfers between devices  56.6 us (32%)
  starting transfers between devices  52.8 us (30%)
  matrix products  26.5 us (15%)
  local copies, waits for them, and re-layouts  14.9 us (8%)
  Pallas kernels  12.5 us (7%)
  other arithmetic  11.1 us (6%)
    ppermute x18, waiting for transfers between devices, permute(): return lax.ppermute(x, 'fsdp', pairs)  40.2 us
    all_to_all x4, starting transfers between devices, exchange(): lax.all_to_all(rows.reshape(experts, count // experts, width), 'expert',...  34.5 us
    ppermute x18, starting transfers between devices, permute(): return lax.ppermute(x, 'fsdp', pairs)  18.3 us
    all_to_all x4, waiting for transfers between devices, exchange(): lax.all_to_all(rows.reshape(experts, count // experts, width), 'expert',...  16.4 us
    unnamed x30, local copies, waits for them, and re-layouts  11.3 us
    dot_general x2, matrix products, dot_t(): lax.dot_general(a, b, (((1,), (1,)), ((), ())), preferred_element_type=F32)  10.3 us
    dot_general x2, matrix products, dot_0(): lax.dot_general(a, b, (((0,), (0,)), ((), ())), preferred_element_type=F32)  9.21 us
    pallas_call x5, Pallas kernels, call(): pl.pallas_call(kernel, out_shape=shapes if len(shapes) > 1 else shapes[0]...  8.04 us
  transfers between devices with their start and end apart: 22, of which 9 were waited for; matrix products, arithmetic and copies ran while one was open for 23% of the time, Pallas kernels for 6%

profile of v2, /device:TPU:16, one launch (start us, length us, event | category | flops | bytes accessed | tf_op | source)
XLA Modules:
  0.0 175.3 jit_solution(14979375676510839134)
XLA Ops:
  1.2 2.8 %collective-permute-start = (bf16[256,1024]{1,0:T(8,128)(2,1)}, bf16[256,1024]{1,0:T(8,128)(2,1)}, u32[]{:S(2)}, u32[]{:S(2)}) collective-permute-start(bf16[256,1024]{1,0:T(8,128)(2,1)} %bitcast.32), channel_id=1, source_target_pairs={{0,64},{32,96},{64,0},{96,32},{128,192},{160,224},{192,128},{224,1... | collective-permute-start | bytes 1572872 | tf_op jit(solution)/shard_map/ppermute | solution.py:135
  8.0 9.7 %all-to-all-start = ((bf16[32,16,1024]{2,1,0:T(8,128)(2,1)}), bf16[32,16,1024]{2,1,0:T(8,128)(2,1)}, u32[]{:S(2)}, u32[]{:S(2)}) async-start(bf16[32,16,1024]{2,1,0:T(8,128)(2,1)} %bitcast.2), calls=%async_computation | async-start | bytes 2097152 | tf_op jit(solution)/shard_map/all_to_all | solution.py:125
  23.4 19.8 %collective-permute-done.5.refs_5_ = bf16[512,1024]{1,0:T(8,128)(2,1)S(1)} collective-permute-done((bf16[512,1024]{1,0:T(8,128)(2,1)S(1)}, bf16[512,1024]{1,0:T(8,128)(2,1)S(1)}, u32[]{:S(2)}, u32[]{:S(2)}) %collective-permute-start.5) | collective-permute-done | bytes 1048608 | tf_op jit(solution)/shard_map/ppermute | solution.py:135
  46.9 9.7 %all-to-all-start.2 = ((bf16[32,16,1024]{2,1,0:T(8,128)(2,1)}), bf16[32,16,1024]{2,1,0:T(8,128)(2,1)}, u32[]{:S(2)}, u32[]{:S(2)}) async-start(bf16[32,16,1024]{2,1,0:T(8,128)(2,1)} %bitcast.8), calls=%async_computation.2 | async-start | bytes 2097152 | tf_op jit(solution)/shard_map/all_to_all | solution.py:125
  56.7 2.7 %shard_map.94 = (bf16[2048,1024]{1,0:T(8,128)(2,1)S(1)}, bf16[2048,1024]{1,0:T(8,128)(2,1)S(1)}) custom-call(bf16[512,1024]{1,0:T(8,128)(2,1)S(1)} %pad_maximum_fusion.refs_0_, bf16[512,1024]{1,0:T(8,128)(2,1)} %collective-permute-done.1.refs_1_, bf16[512,1024]{1,0:T(8,128)(2,1)} %collective-permute-done.2.refs_2_, ...), custom_call_target="tpu_custom_call" | custom-call | bytes 16777216 | tf_op jit(solution)/shard_map/pallas_call | solution.py:187
  59.4 4.4 %fusion.24 = f32[512,2048]{1,0:T(8,128)S(1)} fusion(bf16[512,1024]{1,0:T(8,128)(2,1)} %bitcast.3, bf16[2048,1024]{1,0:T(8,128)(2,1)S(1)} %get-tuple-element.13), kind=kOutput, calls=%fused_computation.43 | convolution fusion | flops 2147483648 | bytes 9437184 | tf_op jit(solution)/shard_map/dot_general | solution.py:116
  65.8 3.6 %convolution_convert_fusion.1 = bf16[512,1024]{1,0:T(8,128)(2,1)} fusion(bf16[2048,1024]{1,0:T(8,128)(2,1)S(1)} %get-tuple-element.14, f32[512,2048]{1,0:T(8,128)S(1)} %fusion.24), kind=kOutput, calls=%fused_computation.29 | convolution fusion | flops 2157445120 | bytes 9437184 | tf_op jit(solution)/shard_map/dot_general | solution.py:199
  69.4 16.4 %all-to-all-done.2 = bf16[32,16,1024]{2,1,0:T(8,128)(2,1)} async-done(((bf16[32,16,1024]{2,1,0:T(8,128)(2,1)}), bf16[32,16,1024]{2,1,0:T(8,128)(2,1)}, u32[]{:S(2)}, u32[]{:S(2)}) %all-to-all-start.2) | async-done | bytes 1048608 | tf_op jit(solution)/shard_map/all_to_all | solution.py:125
  85.8 5.4 %all-to-all-start.1 = ((bf16[32,16,1024]{2,1,0:T(8,128)(2,1)}), bf16[32,16,1024]{2,1,0:T(8,128)(2,1)S(1)}, u32[]{:S(2)}, u32[]{:S(2)}) async-start(bf16[32,16,1024]{2,1,0:T(8,128)(2,1)} %bitcast.6), calls=%async_computation.1 | async-start | bytes 2097152 | tf_op jit(solution)/shard_map/all_to_all | solution.py:125
  91.2 5.6 %fusion.19 = f32[2048,1024]{1,0:T(8,128)S(1)} fusion(bf16[512,1024]{1,0:T(8,128)(2,1)} %bitcast.9, f32[512,2048]{1,0:T(8,128)} %copy-done.13), kind=kOutput, calls=%fused_computation.40 | convolution fusion | flops 2156920832 | bytes 13631488 | tf_op jit(solution)/shard_map/dot_general | solution.py:120
  98.5 3.5 %copy-done.6 = bf16[2048,1024]{1,0:T(8,128)(2,1)S(1)} copy-done((bf16[2048,1024]{1,0:T(8,128)(2,1)S(1)}, bf16[2048,1024]{1,0:T(8,128)(2,1)}, u32[]{:S(2)}) %copy-start.6) | copy-done | bytes 4194328
  102.1 6.0 %fusion.3 = bf16[512,2048]{1,0:T(8,128)(2,1)S(1)} fusion(f32[512,2048]{1,0:T(8,128)S(1)} %copy-done.14, bf16[512,1024]{1,0:T(8,128)(2,1)} %bitcast.9, bf16[2048,1024]{1,0:T(8,128)(2,1)S(1)} %copy-done.6), kind=kOutput, calls=%fused_computation.8 | convolution fusion | flops 2170552320 | bytes 11534336 | tf_op jit(solution)/shard_map/dot_general | solution.py:116
  108.0 3.6 %fusion.25 = f32[2048,1024]{1,0:T(8,128)S(1)} fusion(bf16[512,2048]{1,0:T(8,128)(2,1)S(1)} %fusion.3, bf16[512,1024]{1,0:T(8,128)(2,1)} %bitcast.3), kind=kOutput, calls=%fused_computation.44 | convolution fusion | flops 2147483648 | bytes 11534336 | tf_op jit(solution)/shard_map/dot_general | solution.py:120
  113.4 3.2 %copy-done.10 = f32[2048,1024]{1,0:T(8,128)} copy-done((f32[2048,1024]{1,0:T(8,128)}, f32[2048,1024]{1,0:T(8,128)S(1)}, u32[]{:S(2)}) %copy-start.10) | copy-done | bytes 8388632
  116.9 3.3 %convolution_convert_fusion = bf16[512,1024]{1,0:T(8,128)(2,1)} fusion(bf16[512,2048]{1,0:T(8,128)(2,1)S(1)} %fusion.3, bf16[2048,1024]{1,0:T(8,128)(2,1)S(1)} %copy-done.4), kind=kOutput, calls=%fused_computation.28 | convolution fusion | flops 2148007936 | bytes 7340032 | tf_op jit(solution)/shard_map/dot_general | solution.py:211
  120.3 9.6 %all-to-all-start.3 = ((bf16[32,16,1024]{2,1,0:T(8,128)(2,1)}), bf16[32,16,1024]{2,1,0:T(8,128)(2,1)S(1)}, u32[]{:S(2)}, u32[]{:S(2)}) async-start(bf16[32,16,1024]{2,1,0:T(8,128)(2,1)} %bitcast.10), calls=%async_computation.3 | async-start | bytes 2097152 | tf_op jit(solution)/shard_map/all_to_all | solution.py:125
  129.9 3.8 %fusion.17 = bf16[1024,1024]{1,0:T(8,128)(2,1)S(1)} fusion(f32[2048,1024]{1,0:T(8,128)} %copy-done.12, bf16[1024,1024]{1,0:T(8,128)(2,1)} %collective-permute-done.13), kind=kLoop, calls=%fused_computation.24 | loop fusion | flops 3145728 | bytes 8388608 | tf_op jit(solution)/shard_map/convert_element_type | solution.py:214
  135.7 3.5 %collective-permute-start.14 = (bf16[512,512]{1,0:T(8,128)(2,1)S(1)}, bf16[512,512]{1,0:T(8,128)(2,1)S(1)}, u32[]{:S(2)}, u32[]{:S(2)}) collective-permute-start(bf16[512,512]{1,0:T(8,128)(2,1)S(1)} %get-tuple-element.27), channel_id=1, source_target_pairs={{0,64},{32,96},{64,0},{96,32},{128,192},{160,224},{192,128},{224,1... | collective-permute-start | bytes 1572872 | tf_op jit(solution)/shard_map/ppermute | solution.py:135
  139.2 2.5 %fusion.18 = bf16[1024,1024]{1,0:T(8,128)(2,1)S(1)} fusion(f32[2048,1024]{1,0:T(8,128)S(1)} %copy-done.11, bf16[1024,1024]{1,0:T(8,128)(2,1)} %collective-permute-done.8), kind=kLoop, calls=%fused_computation.27 | loop fusion | flops 3145728 | bytes 8388608 | tf_op jit(solution)/shard_map/convert_element_type | solution.py:215
  142.8 6.0 %collective-permute-done.16 = bf16[512,512]{1,0:T(8,128)(2,1)S(1)} collective-permute-done((bf16[512,512]{1,0:T(8,128)(2,1)S(1)}, bf16[512,512]{1,0:T(8,128)(2,1)S(1)}, u32[]{:S(2)}, u32[]{:S(2)}) %collective-permute-start.16) | collective-permute-done | bytes 524320 | tf_op jit(solution)/shard_map/ppermute | solution.py:135
  148.9 3.1 %collective-permute-done.14 = bf16[512,512]{1,0:T(8,128)(2,1)S(1)} collective-permute-done((bf16[512,512]{1,0:T(8,128)(2,1)S(1)}, bf16[512,512]{1,0:T(8,128)(2,1)S(1)}, u32[]{:S(2)}, u32[]{:S(2)}) %collective-permute-start.14) | collective-permute-done | bytes 524320 | tf_op jit(solution)/shard_map/ppermute | solution.py:135
  155.6 4.5 %collective-permute-done.11 = bf16[512,512]{1,0:T(8,128)(2,1)S(1)} collective-permute-done((bf16[512,512]{1,0:T(8,128)(2,1)S(1)}, bf16[512,512]{1,0:T(8,128)(2,1)S(1)}, u32[]{:S(2)}, u32[]{:S(2)}) %collective-permute-start.11) | collective-permute-done | bytes 524320 | tf_op jit(solution)/shard_map/ppermute | solution.py:135
  160.1 3.1 %collective-permute-done.9 = bf16[512,512]{1,0:T(8,128)(2,1)S(1)} collective-permute-done((bf16[512,512]{1,0:T(8,128)(2,1)S(1)}, bf16[512,512]{1,0:T(8,128)(2,1)S(1)}, u32[]{:S(2)}, u32[]{:S(2)}) %collective-permute-start.9) | collective-permute-done | bytes 524320 | tf_op jit(solution)/shard_map/ppermute | solution.py:135
  169.3 2.1 %shard_map.99 = f32[256,1024]{1,0:T(8,128)} custom-call(f32[256,512]{1,0:T(8,128)S(1)} %get-tuple-element.24.own_l_ref, bf16[256,512]{1,0:T(8,128)(2,1)} %collective-permute-done.15.got_l_ref, f32[256,512]{1,0:T(8,128)S(1)} %get-tuple-element.17.own_r_ref, bf16[256,512]{1,0:T(8,128)(2,1)} %collective-permute-done.17.got_r_ref), custom_call_target="tpu_custom_call" | custom-call | flops 300000000 | bytes 3145728 | tf_op jit(solution)/shard_map/pallas_call | solution.py:98
  (73 shorter events, 36.5 us)
Async XLA Ops:
  0.6 17.1 %collective-permute-start.4 = (bf16[256,1024]{1,0:T(8,128)(2,1)}, bf16[256,1024]{1,0:T(8,128)(2,1)S(1)}, u32[]{:S(2)}, u32[]{:S(2)}) collective-permute-start(bf16[256,1024]{1,0:T(8,128)(2,1)} %bitcast.30), channel_id=1, source_target_pairs={{0,192},{32,224},{64,128},{96,160},{128,64},{160,96},{192,0},{224,... | collective-permute-start | bytes 1572872 | tf_op jit(solution)/shard_map/ppermute | solution.py:135
  1.2 18.8 %collective-permute-start = (bf16[256,1024]{1,0:T(8,128)(2,1)}, bf16[256,1024]{1,0:T(8,128)(2,1)}, u32[]{:S(2)}, u32[]{:S(2)}) collective-permute-start(bf16[256,1024]{1,0:T(8,128)(2,1)} %bitcast.32), channel_id=1, source_target_pairs={{0,64},{32,96},{64,0},{96,32},{128,192},{160,224},{192,128},{224,1... | collective-permute-start | bytes 1572872 | tf_op jit(solution)/shard_map/ppermute | solution.py:135
  8.0 38.9 %all-to-all-start = ((bf16[32,16,1024]{2,1,0:T(8,128)(2,1)}), bf16[32,16,1024]{2,1,0:T(8,128)(2,1)}, u32[]{:S(2)}, u32[]{:S(2)}) async-start(bf16[32,16,1024]{2,1,0:T(8,128)(2,1)} %bitcast.2), calls=%async_computation | async-start | bytes 2097152 | tf_op jit(solution)/shard_map/all_to_all | solution.py:125
  17.8 27.5 %copy-start.2 = (bf16[128,1024]{1,0:T(8,128)(2,1)S(1)}, bf16[128,1024]{1,0:T(8,128)(2,1)}, u32[]{:S(2)}) copy-start(bf16[128,1024]{1,0:T(8,128)(2,1)} %cot_ref.1) | copy-start | bytes 786436
  18.9 24.3 %collective-permute-start.5 = (bf16[512,1024]{1,0:T(8,128)(2,1)S(1)}, bf16[512,1024]{1,0:T(8,128)(2,1)S(1)}, u32[]{:S(2)}, u32[]{:S(2)}) collective-permute-start(bf16[512,1024]{1,0:T(8,128)(2,1)S(1)} %pad_maximum_fusion.1.refs_4_), channel_id=1, source_target_pairs={{0,64},{32,96},{64,0},{96,32},{128,192},{160,224},{192,128},{224,1... | collective-permute-start | bytes 3145736 | tf_op jit(solution)/shard_map/ppermute | solution.py:135
  21.3 24.0 %collective-permute-start.1 = (bf16[512,1024]{1,0:T(8,128)(2,1)S(1)}, bf16[512,1024]{1,0:T(8,128)(2,1)}, u32[]{:S(2)}, u32[]{:S(2)}) collective-permute-start(bf16[512,1024]{1,0:T(8,128)(2,1)S(1)} %pad_maximum_fusion.refs_0_), channel_id=1, source_target_pairs={{0,192},{32,224},{64,128},{96,160},{128,64},{160,96},{192,0},{224,... | collective-permute-start | bytes 3145736 | tf_op jit(solution)/shard_map/ppermute | solution.py:135
  22.9 33.7 %collective-permute-start.6 = (bf16[512,1024]{1,0:T(8,128)(2,1)S(1)}, bf16[512,1024]{1,0:T(8,128)(2,1)}, u32[]{:S(2)}, u32[]{:S(2)}) collective-permute-start(bf16[512,1024]{1,0:T(8,128)(2,1)S(1)} %pad_maximum_fusion.1.refs_4_), channel_id=1, source_target_pairs={{0,32},{32,0},{64,96},{96,64},{128,160},{160,128},{192,224},{224,1... | collective-permute-start | bytes 3145736 | tf_op jit(solution)/shard_map/ppermute | solution.py:135
  22.9 33.7 %collective-permute-start.2 = (bf16[512,1024]{1,0:T(8,128)(2,1)S(1)}, bf16[512,1024]{1,0:T(8,128)(2,1)}, u32[]{:S(2)}, u32[]{:S(2)}) collective-permute-start(bf16[512,1024]{1,0:T(8,128)(2,1)S(1)} %pad_maximum_fusion.refs_0_), channel_id=1, source_target_pairs={{0,32},{32,0},{64,96},{96,64},{128,160},{160,128},{192,224},{224,1... | collective-permute-start | bytes 3145736 | tf_op jit(solution)/shard_map/ppermute | solution.py:135
  43.2 13.4 %collective-permute-start.7 = (bf16[512,1024]{1,0:T(8,128)(2,1)S(1)}, bf16[512,1024]{1,0:T(8,128)(2,1)}, u32[]{:S(2)}, u32[]{:S(2)}) collective-permute-start(bf16[512,1024]{1,0:T(8,128)(2,1)S(1)} %collective-permute-done.5.refs_5_), channel_id=1, source_target_pairs={{0,32},{32,0},{64,96},{96,64},{128,160},{160,128},{192,224},{224,1... | collective-permute-start | bytes 3145736 | tf_op jit(solution)/shard_map/ppermute | solution.py:135
  45.2 11.4 %collective-permute-start.3 = (bf16[512,1024]{1,0:T(8,128)(2,1)}, bf16[512,1024]{1,0:T(8,128)(2,1)}, u32[]{:S(2)}, u32[]{:S(2)}) collective-permute-start(bf16[512,1024]{1,0:T(8,128)(2,1)} %collective-permute-done.1.refs_1_), channel_id=1, source_target_pairs={{0,32},{32,0},{64,96},{96,64},{128,160},{160,128},{192,224},{224,1... | collective-permute-start | bytes 3145736 | tf_op jit(solution)/shard_map/ppermute | solution.py:135
  46.9 38.9 %all-to-all-start.2 = ((bf16[32,16,1024]{2,1,0:T(8,128)(2,1)}), bf16[32,16,1024]{2,1,0:T(8,128)(2,1)}, u32[]{:S(2)}, u32[]{:S(2)}) async-start(bf16[32,16,1024]{2,1,0:T(8,128)(2,1)} %bitcast.8), calls=%async_computation.2 | async-start | bytes 2097152 | tf_op jit(solution)/shard_map/all_to_all | solution.py:125
  85.8 34.4 %all-to-all-start.1 = ((bf16[32,16,1024]{2,1,0:T(8,128)(2,1)}), bf16[32,16,1024]{2,1,0:T(8,128)(2,1)S(1)}, u32[]{:S(2)}, u32[]{:S(2)}) async-start(bf16[32,16,1024]{2,1,0:T(8,128)(2,1)} %bitcast.6), calls=%async_computation.1 | async-start | bytes 2097152 | tf_op jit(solution)/shard_map/all_to_all | solution.py:125
  96.8 11.2 %copy-start.12 = (f32[2048,1024]{1,0:T(8,128)}, f32[2048,1024]{1,0:T(8,128)S(1)}, u32[]{:S(2)}) copy-start(f32[2048,1024]{1,0:T(8,128)S(1)} %fusion.19) | copy-start | bytes 25165828
  98.5 31.4 %collective-permute-start.13 = (bf16[1024,1024]{1,0:T(8,128)(2,1)}, bf16[1024,1024]{1,0:T(8,128)(2,1)}, u32[]{:S(2)}, u32[]{:S(2)}) collective-permute-start(bf16[1024,1024]{1,0:T(8,128)(2,1)} %slice.162), channel_id=1, source_target_pairs={{0,32},{32,0},{64,96},{96,64},{128,160},{160,128},{192,224},{224,1... | collective-permute-start | bytes 6291464 | tf_op jit(solution)/shard_map/ppermute | solution.py:135
  113.4 25.8 %collective-permute-start.8 = (bf16[1024,1024]{1,0:T(8,128)(2,1)}, bf16[1024,1024]{1,0:T(8,128)(2,1)}, u32[]{:S(2)}, u32[]{:S(2)}) collective-permute-start(bf16[1024,1024]{1,0:T(8,128)(2,1)} %slice.163), channel_id=1, source_target_pairs={{0,32},{32,0},{64,96},{96,64},{128,160},{160,128},{192,224},{224,1... | collective-permute-start | bytes 6291464 | tf_op jit(solution)/shard_map/ppermute | solution.py:135
  120.3 48.0 %all-to-all-start.3 = ((bf16[32,16,1024]{2,1,0:T(8,128)(2,1)}), bf16[32,16,1024]{2,1,0:T(8,128)(2,1)S(1)}, u32[]{:S(2)}, u32[]{:S(2)}) async-start(bf16[32,16,1024]{2,1,0:T(8,128)(2,1)} %bitcast.10), calls=%async_computation.3 | async-start | bytes 2097152 | tf_op jit(solution)/shard_map/all_to_all | solution.py:125
  133.8 15.1 %collective-permute-start.16 = (bf16[512,512]{1,0:T(8,128)(2,1)S(1)}, bf16[512,512]{1,0:T(8,128)(2,1)S(1)}, u32[]{:S(2)}, u32[]{:S(2)}) collective-permute-start(bf16[512,512]{1,0:T(8,128)(2,1)S(1)} %get-tuple-element.26), channel_id=1, source_target_pairs={{0,192},{32,224},{64,128},{96,160},{128,64},{160,96},{192,0},{224,... | collective-permute-start | bytes 1572872 | tf_op jit(solution)/shard_map/ppermute | solution.py:135
  135.7 16.3 %collective-permute-start.14 = (bf16[512,512]{1,0:T(8,128)(2,1)S(1)}, bf16[512,512]{1,0:T(8,128)(2,1)S(1)}, u32[]{:S(2)}, u32[]{:S(2)}) collective-permute-start(bf16[512,512]{1,0:T(8,128)(2,1)S(1)} %get-tuple-element.27), channel_id=1, source_target_pairs={{0,64},{32,96},{64,0},{96,32},{128,192},{160,224},{192,128},{224,1... | collective-permute-start | bytes 1572872 | tf_op jit(solution)/shard_map/ppermute | solution.py:135
  141.7 18.4 %collective-permute-start.11 = (bf16[512,512]{1,0:T(8,128)(2,1)S(1)}, bf16[512,512]{1,0:T(8,128)(2,1)S(1)}, u32[]{:S(2)}, u32[]{:S(2)}) collective-permute-start(bf16[512,512]{1,0:T(8,128)(2,1)S(1)} %get-tuple-element.30), channel_id=1, source_target_pairs={{0,192},{32,224},{64,128},{96,160},{128,64},{160,96},{192,0},{224,... | collective-permute-start | bytes 1572872 | tf_op jit(solution)/shard_map/ppermute | solution.py:135
  141.8 21.3 %collective-permute-start.9 = (bf16[512,512]{1,0:T(8,128)(2,1)S(1)}, bf16[512,512]{1,0:T(8,128)(2,1)S(1)}, u32[]{:S(2)}, u32[]{:S(2)}) collective-permute-start(bf16[512,512]{1,0:T(8,128)(2,1)S(1)} %get-tuple-element.31), channel_id=1, source_target_pairs={{0,64},{32,96},{64,0},{96,32},{128,192},{160,224},{192,128},{224,1... | collective-permute-start | bytes 1572872 | tf_op jit(solution)/shard_map/ppermute | solution.py:135
  153.0 16.3 %collective-permute-start.17 = (bf16[256,512]{1,0:T(8,128)(2,1)}, bf16[256,512]{1,0:T(8,128)(2,1)}, u32[]{:S(2)}, u32[]{:S(2)}) collective-permute-start(bf16[256,512]{1,0:T(8,128)(2,1)} %get-tuple-element.16), channel_id=1, source_target_pairs={{0,64},{32,96},{64,0},{96,32},{128,192},{160,224},{192,128},{224,1... | collective-permute-start | bytes 786440 | tf_op jit(solution)/shard_map/ppermute | solution.py:135
  155.0 14.3 %collective-permute-start.15 = (bf16[256,512]{1,0:T(8,128)(2,1)}, bf16[256,512]{1,0:T(8,128)(2,1)}, u32[]{:S(2)}, u32[]{:S(2)}) collective-permute-start(bf16[256,512]{1,0:T(8,128)(2,1)} %get-tuple-element.25), channel_id=1, source_target_pairs={{0,192},{32,224},{64,128},{96,160},{128,64},{160,96},{192,0},{224,... | collective-permute-start | bytes 786440 | tf_op jit(solution)/shard_map/ppermute | solution.py:135
  164.5 7.8 %collective-permute-start.12 = (bf16[256,512]{1,0:T(8,128)(2,1)}, bf16[256,512]{1,0:T(8,128)(2,1)}, u32[]{:S(2)}, u32[]{:S(2)}) collective-permute-start(bf16[256,512]{1,0:T(8,128)(2,1)} %get-tuple-element.20), channel_id=1, source_target_pairs={{0,64},{32,96},{64,0},{96,32},{128,192},{160,224},{192,128},{224,1... | collective-permute-start | bytes 786440 | tf_op jit(solution)/shard_map/ppermute | solution.py:135
  166.5 6.7 %collective-permute-start.10 = (bf16[256,512]{1,0:T(8,128)(2,1)}, bf16[256,512]{1,0:T(8,128)(2,1)}, u32[]{:S(2)}, u32[]{:S(2)}) collective-permute-start(bf16[256,512]{1,0:T(8,128)(2,1)} %get-tuple-element.29), channel_id=1, source_target_pairs={{0,192},{32,224},{64,128},{96,160},{128,64},{160,96},{192,0},{224,... | collective-permute-start | bytes 786440 | tf_op jit(solution)/shard_map/ppermute | solution.py:135
  (13 other events, 55.0 us)

commit v3 on v1

v3 whole, which is shorter than its diff:
```python
import functools

import jax
import jax.numpy as jnp
from jax import lax
from jax.experimental import pallas as pl
from jax.experimental.pallas import tpu as pltpu
from jax.sharding import PartitionSpec as P


PAIR_A = [(2 * y + c, 2 * (y ^ 1) + c) for y in range(4) for c in range(2)]
PAIR_B = [(2 * y + c, 2 * (3 - y) + c) for y in range(4) for c in range(2)]
PAIR_C = [(f, f ^ 1) for f in range(8)]
F32 = jnp.float32
BF16 = jnp.bfloat16
GELU_SCALE = 0.7978845608028654
GELU_CUBIC = 0.044715


def dot_t(a, b):
    return lax.dot_general(a, b, (((1,), (1,)), ((), ())), preferred_element_type=F32)


def dot_0(a, b):
    return lax.dot_general(a, b, (((0,), (0,)), ((), ())), preferred_element_type=F32)


def dot(a, b):
    return jnp.dot(a, b, preferred_element_type=F32)


def cells_of(experts, capacity, ids_ref):
    n = ids_ref.shape[1]
    ids0, ids1 = ids_ref[0:1, :], ids_ref[1:2, :]
    label = lax.broadcasted_iota(jnp.int32, (experts, n), 0)
    oh0, oh1 = ids0 == label, ids1 == label
    hit = jnp.where(oh0 | oh1, 1.0, 0.0).astype(BF16)
    before = lax.broadcasted_iota(jnp.int32, (n, n), 0) < lax.broadcasted_iota(jnp.int32, (n, n), 1)
    earlier = dot(hit, jnp.where(before, 1.0, 0.0).astype(BF16))
    slot0 = jnp.sum(jnp.where(oh0, earlier, 0.0), axis=0, keepdims=True).astype(jnp.int32)
    slot1 = jnp.sum(jnp.where(oh1, earlier, 0.0), axis=0, keepdims=True).astype(jnp.int32)
    cell = lax.broadcasted_iota(jnp.int32, (experts * capacity, n), 0)
    return cell == ids0 * capacity + slot0, cell == ids1 * capacity + slot1


def place_kernel(*refs):
    hbm, out_hbm, local, cells_ref, sems = refs[:4], refs[4], refs[5:9], refs[9], refs[10]
    copies = [pltpu.make_async_copy(a, b, sems.at[i]) for i, (a, b) in enumerate(zip(hbm, local))]
    for copy in copies:
        copy.start()
    ids_ref, gate_ref, tok_ref, cot_ref = local
    experts, slots, width = cells_ref.shape
    capacity = slots // 2
    outs = [
        pltpu.make_async_copy(cells_ref.at[:, part, :], out_hbm.at[:, part, :], sems.at[4 + i])
        for i, part in enumerate((pl.ds(0, capacity), pl.ds(capacity, capacity)))
    ]
    copies[0].wait()
    at0, at1 = cells_of(experts, capacity, ids_ref)
    place = jnp.where(at0 | at1, 1.0, 0.0).astype(BF16)
    copies[2].wait()
    cells_ref[:, :capacity, :] = dot(place, tok_ref[...]).astype(BF16).reshape(experts, capacity, width)
    outs[0].start()
    copies[1].wait()
    gate = jnp.where(at0, gate_ref[0:1, :], 0.0) + jnp.where(at1, gate_ref[1:2, :], 0.0)
    hi = gate.astype(BF16)
    lo = (gate - hi.astype(F32)).astype(BF16)
    copies[3].wait()
    cot = cot_ref[...]
    cells_ref[:, capacity:, :] = (
        (dot(hi, cot) + dot(lo, cot)).astype(BF16).reshape(experts, capacity, width)
    )
    outs[1].start()
    outs[0].wait()
    outs[1].wait()


def weights_kernel(experts, ids_ref, gate_ref, place_ref, hi_ref, lo_ref):
    at0, at1 = cells_of(experts, place_ref.shape[1] // experts, ids_ref)
    place_ref[...] = jnp.transpose(jnp.where(at0 | at1, 1.0, 0.0)).astype(BF16)
    gate = jnp.where(at0, gate_ref[0:1, :], 0.0) + jnp.where(at1, gate_ref[1:2, :], 0.0)
    gate = jnp.transpose(gate)
    hi = gate.astype(BF16)
    hi_ref[...] = hi
    lo_ref[...] = (gate - hi.astype(F32)).astype(BF16)


def expert_kernel(unit, rows_hbm, *refs):
    in_a, in_b, in_ca, in_cb, out_a, out_b, out_ca, out_cb = refs[:8]
    back_hbm, hid_hbm, act_hbm = refs[8:11]
    rows_ref, back_ref, hid_ref, act_ref, full_in, full_out, sems, row_sem, out_sems, back_sems = refs[11:]
    sources, slots, width = rows_ref.shape
    capacity = slots // 2
    count = sources * capacity
    tile = count // 2
    per = sources // 2
    row_copies = [
        pltpu.make_async_copy(
            rows_hbm.at[pl.ds(r * per, per)], rows_ref.at[pl.ds(r * per, per)], row_sem.at[r]
        )
        for r in range(2)
    ]
    order = []
    for first, second, first_out, second_out in [(in_a, in_b, out_a, out_b), (in_ca, in_cb, out_ca, out_cb)]:
        order.append(((first, 0), (first_out, 0)))
        order.append(((first, 1), (second_out, 0)))
        order.append(((second, 1), (second_out, 1)))
        order.append(((second, 0), (first_out, 1)))
    for c, pair in enumerate(order):
        for w, ((ref, row), full) in enumerate(zip(pair, (full_in, full_out))):
            pltpu.make_async_copy(
                ref.at[pl.ds(row * unit, unit)], full.at[pl.ds(c * unit, unit)], sems.at[w, c]
            ).start()
        if c == 0:
            for copy in row_copies:
                copy.start()
    for copy in row_copies:
        copy.wait()

    @pl.loop(0, 8)
    def _(c):
        at = pl.multiple_of(c * unit, unit)
        for w, full in enumerate((full_in, full_out)):
            pltpu.make_async_copy(in_a.at[pl.ds(0, unit)], full.at[pl.ds(at, unit)], sems.at[w, c]).wait()
        w_in, w_out = full_in[pl.ds(at, unit), :], full_out[pl.ds(at, unit), :]
        for r in range(2):
            x = rows_ref[r * per : (r + 1) * per, :capacity, :].reshape(tile, width)
            dy = rows_ref[r * per : (r + 1) * per, capacity:, :].reshape(tile, width)
            pre = dot_t(x, w_in)
            up = dot_t(dy, w_out)
            square = pre * pre
            t = jnp.tanh(GELU_SCALE * pre * (1.0 + GELU_CUBIC * square))
            half = 0.5 * (1.0 + t)
            slope = half + (0.5 * GELU_SCALE) * pre * (1.0 - t * t) * (1.0 + 3.0 * GELU_CUBIC * square)
            hid_ref[r * tile : (r + 1) * tile, pl.ds(at, unit)] = (pre * half).astype(BF16)
            act_ref[r * tile : (r + 1) * tile, pl.ds(at, unit)] = (up * slope).astype(BF16)

    outs = [
        pltpu.make_async_copy(a, b, out_sems.at[i])
        for i, (a, b) in enumerate([(hid_ref, hid_hbm), (act_ref, act_hbm)])
    ]
    for copy in outs:
        copy.start()
    columns = 256

    def back_copy(c, at):
        cut = pl.ds(at, columns)
        return pltpu.make_async_copy(back_ref.at[:, :, cut], back_hbm.at[:, :, cut], back_sems.at[c])

    @pl.loop(0, width // columns)
    def _(c):
        at = pl.multiple_of(c * columns, columns)
        for part, (a_ref, full) in enumerate([(hid_ref, full_out), (act_ref, full_in)]):
            w = full[:, pl.ds(at, columns)]
            for r in range(2):
                got = dot(a_ref[r * tile : (r + 1) * tile, :], w).astype(BF16)
                back_ref[
                    r * per : (r + 1) * per, part * capacity : (part + 1) * capacity, pl.ds(at, columns)
                ] = got.reshape(per, capacity, columns)
        back_copy(c, at).start()

    for c in range(width // columns):
        back_copy(c, c * columns).wait()
    for copy in outs:
        copy.wait()


def grad_kernel(part, unit, acts_ref, rows_ref, keep_ref, send_ref, held_ref):
    _, slots, _ = rows_ref.shape
    capacity = slots // 2
    held_ref[...] = rows_ref[:, part * capacity : (part + 1) * capacity, :].reshape(held_ref.shape)
    for half, ref in ((4, send_ref), (0, keep_ref)):

        @pl.loop(0, 4)
        def _(c):
            at = pl.multiple_of((half + c) * unit, unit)
            got = dot_0(acts_ref[:, pl.ds(at, unit)], held_ref[...]).astype(BF16)
            ref[pl.ds(pl.multiple_of(c * unit, unit), unit), :] = got


def combine_kernel(place_ref, hi_ref, lo_ref, rows_ref, out_ref, grad_ref):
    sources, slots, width = rows_ref.shape
    capacity = slots // 2
    rows = rows_ref[:, :capacity, :].reshape(sources * capacity, width)
    out_ref[...] = (dot(hi_ref[...], rows) + dot(lo_ref[...], rows)).astype(BF16)
    rows = rows_ref[:, capacity:, :].reshape(sources * capacity, width)
    grad_ref[...] = dot(place_ref[...], rows).astype(BF16)


def finish_kernel(own_l_ref, got_l_ref, own_r_ref, got_r_ref, out_ref):
    half = own_l_ref.shape[1]
    out_ref[:, :half] = own_l_ref[...] + got_l_ref[...].astype(F32)
    out_ref[:, half:] = own_r_ref[...] + got_r_ref[...].astype(F32)


def call(kernel, outs, *args, flops=3e8, moved=4 << 20, specs=None, scratch=(), limit=None):
    shapes = [jax.ShapeDtypeStruct(s, d) for s, d in outs]
    vmem = pl.BlockSpec(memory_space=pltpu.VMEM)
    in_specs, out_specs = specs or ([vmem] * len(args), [vmem] * len(shapes))
    single = len(shapes) == 1
    return pl.pallas_call(
        kernel,
        out_shape=shapes[0] if single else shapes,
        in_specs=in_specs,
        out_specs=out_specs[0] if single else out_specs,
        scratch_shapes=list(scratch),
        cost_estimate=pl.CostEstimate(flops=int(flops), bytes_accessed=moved, transcendentals=0),
        compiler_params=pltpu.CompilerParams(vmem_limit_bytes=limit),
    )(*args)


def exchange(cells):
    return lax.all_to_all(cells, "expert", split_axis=0, concat_axis=0, tiled=True)


def permute(x, pairs):
    return lax.ppermute(x, "fsdp", pairs)


def gather(shard, first, second):
    got = permute(shard, first)
    two = jnp.concatenate([shard, got], axis=0)
    other = permute(two, second)
    core_two = permute(two, PAIR_C)
    core_other = permute(other, PAIR_C)
    return two, other, core_two, core_other


def scatter(keep, send, unit):
    got = permute(send, PAIR_C)
    total = (keep.astype(F32) + got.astype(F32)).astype(BF16)
    half = total.shape[1] // 2
    left, right = total[:, :half], total[:, half:]
    got_l = permute(left[unit : 3 * unit], PAIR_A)
    got_r = permute(right[2 * unit :], PAIR_B)
    own_l = left[:unit].astype(F32) + got_l[:unit].astype(F32)
    next_l = left[3 * unit :].astype(F32) + got_l[unit:].astype(F32)
    own_r = right[:unit].astype(F32) + got_r[unit:].astype(F32)
    next_r = right[unit : 2 * unit].astype(F32) + got_r[:unit].astype(F32)
    got_l = permute(next_l.astype(BF16), PAIR_B)
    got_r = permute(next_r.astype(BF16), PAIR_A)
    return call(finish_kernel, [((unit, 2 * half), F32)], own_l, got_l, own_r, got_r, limit=16 << 20)


def layer(tokens, expert_ids, gate_weights, weight_in, weight_out, cotangent):
    n, width = tokens.shape
    experts = lax.axis_size("expert")
    cells = 4 * n
    capacity = cells // experts
    unit = weight_in.shape[1]
    in_pieces = gather(weight_in[0], PAIR_A, PAIR_B)
    out_pieces = gather(weight_out[0], PAIR_B, PAIR_A)

    anywhere = pl.BlockSpec(memory_space=pl.ANY)
    shape = (experts, 2 * capacity, width)
    sent = call(
        place_kernel,
        [(shape, BF16)],
        expert_ids.T,
        gate_weights.T,
        tokens,
        cotangent,
        specs=([anywhere] * 4, [anywhere]),
        scratch=[
            pltpu.VMEM((2, n), jnp.int32),
            pltpu.VMEM((2, n), F32),
            pltpu.VMEM(tokens.shape, BF16),
            pltpu.VMEM(tokens.shape, BF16),
            pltpu.VMEM(shape, BF16),
            pltpu.SemaphoreType.DMA((6,)),
        ],
    )
    rows = exchange(sent)
    place, hi, lo = call(
        functools.partial(weights_kernel, experts),
        [((n, cells), BF16)] * 3,
        expert_ids.T,
        gate_weights.T,
    )
    answer, hidden, grad_act = call(
        functools.partial(expert_kernel, unit),
        [(shape, BF16)] + [((cells, 8 * unit), BF16)] * 2,
        rows,
        *in_pieces,
        *out_pieces,
        flops=8 * cells * width * 8 * unit,
        moved=16 << 20,
        specs=([anywhere] * 9, [anywhere] * 3),
        scratch=[
            pltpu.VMEM(shape, BF16),
            pltpu.VMEM(shape, BF16),
            pltpu.VMEM((cells, 8 * unit), BF16),
            pltpu.VMEM((cells, 8 * unit), BF16),
            pltpu.VMEM((8 * unit, width), BF16),
            pltpu.VMEM((8 * unit, width), BF16),
            pltpu.SemaphoreType.DMA((2, 8)),
            pltpu.SemaphoreType.DMA((2,)),
            pltpu.SemaphoreType.DMA((2,)),
            pltpu.SemaphoreType.DMA((4,)),
        ],
    )
    returned = exchange(answer)

    grads = []
    for part, acts in ((1, hidden), (0, grad_act)):
        keep, send = call(
            functools.partial(grad_kernel, part, unit),
            [((4 * unit, width), BF16)] * 2,
            acts,
            rows,
            flops=2 * cells * width * 8 * unit,
            moved=8 << 20,
            scratch=[pltpu.VMEM((cells, width), BF16)],
        )
        grads.append(scatter(keep, send, unit))
    grad_out, grad_in = grads

    layer_out, token_grad = call(
        combine_kernel, [((n, width), BF16)] * 2, place, hi, lo, returned, limit=16 << 20
    )
    return (layer_out, token_grad, grad_in[None], grad_out[None])


def solution(mesh):
    rows = P(("fsdp", "expert"), None)
    weights = P("expert", "fsdp", None)
    return jax.shard_map(
        layer,
        mesh=mesh,
        in_specs=(rows, rows, rows, weights, weights, rows),
        out_specs=(rows, rows, weights, weights),
        check_vma=False,
    )
```

time: 191 us -> 153 us (0.80)
  Pallas kernels: 5.63 us -> 43.5 us
  matrix products: 32.3 us -> 0 us
  local copies, waits for them, and re-layouts: 22 us -> 3.05 us
  waiting for transfers between devices: 74.8 us -> 61.3 us
  other arithmetic: 14.8 us -> 8.72 us
  starting transfers between devices: 37.6 us -> 33.2 us
    pallas_call x4 -> x8, Pallas kernels: 5.63 us -> 43.5 us  [call(): pl.pallas_call(kernel, out_shape=shapes[0] if single else shapes, in_spec...]
    dot_general x6 -> x0, matrix products: 32.3 us -> none  [the longest x2 12.4 us: dot_t(): lax.dot_general(a, b, (((1,), (1,)), ((), ())), preferred_element_type=F32)]
    all_to_all x4 -> x2, waiting for transfers between devices: 27.1 us -> 7.3 us  [exchange(): lax.all_to_all(cells, 'expert', split_axis=0, concat_axis=0, tiled=True)]
    unnamed x47 -> x30, local copies, waits for them, and re-layouts: 17.3 us -> 2.9 us
    all_to_all x4 -> x2, starting transfers between devices: 29.2 us -> 17.6 us  [exchange(): lax.all_to_all(cells, 'expert', split_axis=0, concat_axis=0, tiled=True)]
    ppermute x14 -> x18, starting transfers between devices: 8.33 us -> 15.6 us  [permute(): return lax.ppermute(x, 'fsdp', pairs)]
    ppermute x14 -> x18, waiting for transfers between devices: 47.7 us -> 54 us  [permute(): return lax.ppermute(x, 'fsdp', pairs)]
    slice x6 -> x2, local copies, waits for them, and re-layouts: 4.6 us -> 0.15 us  [scatter(): got_r = permute(right[2 * unit:], PAIR_B)]
  transfers between devices with their start and end apart: 18 -> 20, of which waited for: 9 -> 10; matrix products, arithmetic and copies ran while one was open for 26% -> 6% of each run, Pallas kernels for 2% -> 9%
where the time goes in v3:
time: 153 us; the launch traced here: 151 us
  waiting for transfers between devices  61.3 us (40%)
  Pallas kernels  43.5 us (28%)
  starting transfers between devices  33.2 us (22%)
  other arithmetic  8.72 us (6%)
  local copies, waits for them, and re-layouts  3.05 us (2%)
    ppermute x18, waiting for transfers between devices, permute(): return lax.ppermute(x, 'fsdp', pairs)  54 us
    pallas_call x8, Pallas kernels, call(): pl.pallas_call(kernel, out_shape=shapes[0] if single else shapes, in_spec...  43.5 us
    all_to_all x2, starting transfers between devices, exchange(): lax.all_to_all(cells, 'expert', split_axis=0, concat_axis=0, tiled=True)  17.6 us
    ppermute x18, starting transfers between devices, permute(): return lax.ppermute(x, 'fsdp', pairs)  15.6 us
    all_to_all x2, waiting for transfers between devices, exchange(): lax.all_to_all(cells, 'expert', split_axis=0, concat_axis=0, tiled=True)  7.3 us
    convert_element_type x2, other arithmetic, scatter(): total = (keep.astype(F32) + got.astype(F32)).astype(BF16)  4.15 us
  transfers between devices with their start and end apart: 20, of which 10 were waited for; matrix products, arithmetic and copies ran while one was open for 6% of the time, Pallas kernels for 9%

profile of v3, /device:TPU:16, one launch (start us, length us, event | category | flops | bytes accessed | tf_op | source)
XLA Modules:
  0.0 150.6 jit_solution(504184365071213624)
XLA Ops:
  0.6 3.3 %shard_map.94 = bf16[32,32,1024]{2,1,0:T(8,128)(2,1)} custom-call(s32[2,128]{1,0:T(2,128)} %bitcast.10, f32[2,128]{1,0:T(2,128)} %bitcast.12, bf16[128,1024]{1,0:T(8,128)(2,1)} %refs_2_.1, bf16[128,1024]{1,0:T(8,128)(2,1)} %refs_3_.1), custom_call_target="tpu_custom_call" | custom-call | flops 300000000 | bytes 4194304 | tf_op jit(solution)/shard_map/pallas_call | solution.py:201
  3.9 11.4 %all-to-all-start = ((bf16[32,32,1024]{2,1,0:T(8,128)(2,1)}), bf16[32,32,1024]{2,1,0:T(8,128)(2,1)S(1)}, u32[]{:S(2)}, u32[]{:S(2)}) async-start(bf16[32,32,1024]{2,1,0:T(8,128)(2,1)} %shard_map.94), calls=%async_computation | async-start | bytes 4194304 | tf_op jit(solution)/shard_map/all_to_all | solution.py:213
  15.4 1.4 collective-permute-start
  16.7 12.1 %collective-permute-done = bf16[256,1024]{1,0:T(8,128)(2,1)S(1)} collective-permute-done((bf16[256,1024]{1,0:T(8,128)(2,1)S(1)}, bf16[256,1024]{1,0:T(8,128)(2,1)S(1)}, u32[]{:S(2)}, u32[]{:S(2)}) %collective-permute-start) | collective-permute-done | bytes 524320 | tf_op jit(solution)/shard_map/ppermute | solution.py:217
  31.6 1.6 %collective-permute-start.5 = (bf16[512,1024]{1,0:T(8,128)(2,1)S(1)}, bf16[512,1024]{1,0:T(8,128)(2,1)S(1)}, u32[]{:S(2)}, u32[]{:S(2)}) collective-permute-start(bf16[512,1024]{1,0:T(8,128)(2,1)S(1)} %pad_maximum_fusion.1.refs_4_), channel_id=1, source_target_pairs={{0,64},{32,96},{64,0},{96,32},{128,192},{160,224},{192,128},{224,1... | collective-permute-start | bytes 3145736 | tf_op jit(solution)/shard_map/ppermute | solution.py:217
  33.7 20.1 %collective-permute-done.1.refs_1_ = bf16[512,1024]{1,0:T(8,128)(2,1)S(1)} collective-permute-done((bf16[512,1024]{1,0:T(8,128)(2,1)S(1)}, bf16[512,1024]{1,0:T(8,128)(2,1)S(1)}, u32[]{:S(2)}, u32[]{:S(2)}) %collective-permute-start.1) | collective-permute-done | bytes 1048608 | tf_op jit(solution)/shard_map/ppermute | solution.py:217
  53.8 1.5 collective-permute-done.5.refs_5_
  58.1 7.3 %all-to-all-done.rows_hbm.rows_ref = bf16[32,32,1024]{2,1,0:T(8,128)(2,1)S(1)} async-done(((bf16[32,32,1024]{2,1,0:T(8,128)(2,1)}), bf16[32,32,1024]{2,1,0:T(8,128)(2,1)S(1)}, u32[]{:S(2)}, u32[]{:S(2)}) %all-to-all-start) | async-done | bytes 2097184 | tf_op jit(solution)/shard_map/all_to_all | solution.py:213
  66.7 17.7 %shard_map.95 = (bf16[32,32,1024]{2,1,0:T(8,128)(2,1)}, bf16[512,2048]{1,0:T(8,128)(2,1)}, bf16[512,2048]{1,0:T(8,128)(2,1)}) custom-call(bf16[32,32,1024]{2,1,0:T(8,128)(2,1)} %copy-done.6, bf16[512,1024]{1,0:T(8,128)(2,1)} %copy-done.7, bf16[512,1024]{1,0:T(8,128)(2,1)} %copy-done.10, bf16[512,1024]{1,0:T(8,128)(2,1)} %copy-done.12, ...), custom_call_target="tpu_custom_call" | custom-call | flops 8589934592 | bytes 16777216 | tf_op jit(solution)/shard_map/pallas_call | solution.py:201
  84.4 7.7 %shard_map.99 = (bf16[1024,1024]{1,0:T(8,128)(2,1)}, bf16[1024,1024]{1,0:T(8,128)(2,1)}) custom-call(bf16[512,2048]{1,0:T(8,128)(2,1)} %get-tuple-element.25.acts_ref, bf16[32,32,1024]{2,1,0:T(8,128)(2,1)} %copy-done.6), custom_call_target="tpu_custom_call" | custom-call | flops 2147483648 | bytes 8388608 | tf_op jit(solution)/shard_map/pallas_call | solution.py:201
  92.1 6.1 %all-to-all-start.1 = ((bf16[32,32,1024]{2,1,0:T(8,128)(2,1)}), bf16[32,32,1024]{2,1,0:T(8,128)(2,1)S(1)}, u32[]{:S(2)}, u32[]{:S(2)}) async-start(bf16[32,32,1024]{2,1,0:T(8,128)(2,1)} %get-tuple-element.19), calls=%async_computation.1 | async-start | bytes 4194304 | tf_op jit(solution)/shard_map/all_to_all | solution.py:213
  98.2 7.7 %shard_map.97 = (bf16[1024,1024]{1,0:T(8,128)(2,1)}, bf16[1024,1024]{1,0:T(8,128)(2,1)}) custom-call(bf16[512,2048]{1,0:T(8,128)(2,1)} %get-tuple-element.22.acts_ref, bf16[32,32,1024]{2,1,0:T(8,128)(2,1)} %copy-done.6), custom_call_target="tpu_custom_call" | custom-call | flops 2147483648 | bytes 8388608 | tf_op jit(solution)/shard_map/pallas_call | solution.py:201
  106.1 3.2 %add_convert_fusion = bf16[1024,1024]{1,0:T(8,128)(2,1)S(1)} fusion(bf16[1024,1024]{1,0:T(8,128)(2,1)} %collective-permute-done.13, bf16[1024,1024]{1,0:T(8,128)(2,1)} %get-tuple-element.26), kind=kLoop, calls=%fused_computation | loop fusion | flops 4194304 | bytes 6291456 | tf_op jit(solution)/shard_map/convert_element_type | solution.py:231
  109.4 1.4 collective-permute-start.14
  111.9 2.0 %collective-permute-start.11 = (bf16[512,512]{1,0:T(8,128)(2,1)S(1)}, bf16[512,512]{1,0:T(8,128)(2,1)S(1)}, u32[]{:S(2)}, u32[]{:S(2)}) collective-permute-start(bf16[512,512]{1,0:T(8,128)(2,1)S(1)} %get-tuple-element.42), channel_id=1, source_target_pairs={{0,192},{32,224},{64,128},{96,160},{128,64},{160,96},{192,0},{224,... | collective-permute-start | bytes 1572872 | tf_op jit(solution)/shard_map/ppermute | solution.py:217
  113.9 2.0 %collective-permute-start.9 = (bf16[512,512]{1,0:T(8,128)(2,1)S(1)}, bf16[512,512]{1,0:T(8,128)(2,1)S(1)}, u32[]{:S(2)}, u32[]{:S(2)}) collective-permute-start(bf16[512,512]{1,0:T(8,128)(2,1)S(1)} %get-tuple-element.43), channel_id=1, source_target_pairs={{0,64},{32,96},{64,0},{96,32},{128,192},{160,224},{192,128},{224,1... | collective-permute-start | bytes 1572872 | tf_op jit(solution)/shard_map/ppermute | solution.py:217
  115.9 8.4 %collective-permute-done.14 = bf16[512,512]{1,0:T(8,128)(2,1)S(1)} collective-permute-done((bf16[512,512]{1,0:T(8,128)(2,1)S(1)}, bf16[512,512]{1,0:T(8,128)(2,1)S(1)}, u32[]{:S(2)}, u32[]{:S(2)}) %collective-permute-start.14) | collective-permute-done | bytes 524320 | tf_op jit(solution)/shard_map/ppermute | solution.py:217
  126.7 3.0 %collective-permute-start.17 = (bf16[256,512]{1,0:T(8,128)(2,1)}, bf16[256,512]{1,0:T(8,128)(2,1)}, u32[]{:S(2)}, u32[]{:S(2)}) collective-permute-start(bf16[256,512]{1,0:T(8,128)(2,1)} %get-tuple-element.28), channel_id=1, source_target_pairs={{0,64},{32,96},{64,0},{96,32},{128,192},{160,224},{192,128},{224,1... | collective-permute-start | bytes 786440 | tf_op jit(solution)/shard_map/ppermute | solution.py:217
  129.7 7.1 %collective-permute-done.11 = bf16[512,512]{1,0:T(8,128)(2,1)S(1)} collective-permute-done((bf16[512,512]{1,0:T(8,128)(2,1)S(1)}, bf16[512,512]{1,0:T(8,128)(2,1)S(1)}, u32[]{:S(2)}, u32[]{:S(2)}) %collective-permute-start.11) | collective-permute-done | bytes 524320 | tf_op jit(solution)/shard_map/ppermute | solution.py:217
  138.1 3.0 %collective-permute-start.12 = (bf16[256,512]{1,0:T(8,128)(2,1)}, bf16[256,512]{1,0:T(8,128)(2,1)}, u32[]{:S(2)}, u32[]{:S(2)}) collective-permute-start(bf16[256,512]{1,0:T(8,128)(2,1)} %get-tuple-element.32), channel_id=1, source_target_pairs={{0,64},{32,96},{64,0},{96,32},{128,192},{160,224},{192,128},{224,1... | collective-permute-start | bytes 786440 | tf_op jit(solution)/shard_map/ppermute | solution.py:217
  141.1 1.8 %shard_map.93 = (bf16[128,512]{1,0:T(8,128)(2,1)}, bf16[128,512]{1,0:T(8,128)(2,1)}, bf16[128,512]{1,0:T(8,128)(2,1)}) custom-call(s32[2,128]{1,0:T(2,128)} %bitcast.11, f32[2,128]{1,0:T(2,128)} %bitcast.13), custom_call_target="tpu_custom_call" | custom-call | flops 300000000 | bytes 4194304 | tf_op jit(solution)/shard_map/pallas_call | solution.py:201
  142.9 2.1 %shard_map.100 = f32[256,1024]{1,0:T(8,128)} custom-call(f32[256,512]{1,0:T(8,128)S(1)} %get-tuple-element.36.own_l_ref, bf16[256,512]{1,0:T(8,128)(2,1)S(1)} %collective-permute-done.15.got_l_ref, f32[256,512]{1,0:T(8,128)S(1)} %get-tuple-element.29.own_r_ref, bf16[256,512]{1,0:T(8,128)(2,1)} %collective-permute-done.17.got_r_ref), custom_call_target="tpu_custom_call" | custom-call | flops 300000000 | bytes 4194304 | tf_op jit(solution)/shard_map/pallas_call | solution.py:201
  145.0 2.2 %collective-permute-done.10.got_l_ref = bf16[256,512]{1,0:T(8,128)(2,1)} collective-permute-done((bf16[256,512]{1,0:T(8,128)(2,1)}, bf16[256,512]{1,0:T(8,128)(2,1)}, u32[]{:S(2)}, u32[]{:S(2)}) %collective-permute-start.10) | collective-permute-done | bytes 262176 | tf_op jit(solution)/shard_map/ppermute | solution.py:217
  147.2 2.1 %shard_map.98 = f32[256,1024]{1,0:T(8,128)} custom-call(f32[256,512]{1,0:T(8,128)S(1)} %copy-done.1, bf16[256,512]{1,0:T(8,128)(2,1)} %collective-permute-done.10.got_l_ref, f32[256,512]{1,0:T(8,128)S(1)} %copy-done, bf16[256,512]{1,0:T(8,128)(2,1)} %collective-permute-done.12.got_r_ref), custom_call_target="tpu_custom_call" | custom-call | flops 300000000 | bytes 4194304 | tf_op jit(solution)/shard_map/pallas_call | solution.py:201
  (62 shorter events, 13.8 us)
Async XLA Ops:
  3.9 11.5 %copy-start.9 = (bf16[1,256,1024]{2,1,0:T(8,128)(2,1)S(1)}, bf16[1,256,1024]{2,1,0:T(8,128)(2,1)}, u32[]{:S(2)}) copy-start(bf16[1,256,1024]{2,1,0:T(8,128)(2,1)} %param.9) | copy-start | bytes 1572868
  3.9 61.5 %all-to-all-start = ((bf16[32,32,1024]{2,1,0:T(8,128)(2,1)}), bf16[32,32,1024]{2,1,0:T(8,128)(2,1)S(1)}, u32[]{:S(2)}, u32[]{:S(2)}) async-start(bf16[32,32,1024]{2,1,0:T(8,128)(2,1)} %shard_map.94), calls=%async_computation | async-start | bytes 4194304 | tf_op jit(solution)/shard_map/all_to_all | solution.py:213
  15.4 13.5 %collective-permute-start = (bf16[256,1024]{1,0:T(8,128)(2,1)S(1)}, bf16[256,1024]{1,0:T(8,128)(2,1)S(1)}, u32[]{:S(2)}, u32[]{:S(2)}) collective-permute-start(bf16[256,1024]{1,0:T(8,128)(2,1)S(1)} %bitcast.9), channel_id=1, source_target_pairs={{0,64},{32,96},{64,0},{96,32},{128,192},{160,224},{192,128},{224,1... | collective-permute-start | bytes 1572872 | tf_op jit(solution)/shard_map/ppermute | solution.py:217
  16.7 13.8 %collective-permute-start.4 = (bf16[256,1024]{1,0:T(8,128)(2,1)}, bf16[256,1024]{1,0:T(8,128)(2,1)S(1)}, u32[]{:S(2)}, u32[]{:S(2)}) collective-permute-start(bf16[256,1024]{1,0:T(8,128)(2,1)} %bitcast.3), channel_id=1, source_target_pairs={{0,192},{32,224},{64,128},{96,160},{128,64},{160,96},{192,0},{224,... | collective-permute-start | bytes 1572872 | tf_op jit(solution)/shard_map/ppermute | solution.py:217
  29.9 35.5 %copy-start.7 = (bf16[512,1024]{1,0:T(8,128)(2,1)}, bf16[512,1024]{1,0:T(8,128)(2,1)S(1)}, u32[]{:S(2)}) copy-start(bf16[512,1024]{1,0:T(8,128)(2,1)S(1)} %pad_maximum_fusion.refs_0_) | copy-start | bytes 3145732
  30.0 23.8 %collective-permute-start.1 = (bf16[512,1024]{1,0:T(8,128)(2,1)S(1)}, bf16[512,1024]{1,0:T(8,128)(2,1)S(1)}, u32[]{:S(2)}, u32[]{:S(2)}) collective-permute-start(bf16[512,1024]{1,0:T(8,128)(2,1)S(1)} %pad_maximum_fusion.refs_0_), channel_id=1, source_target_pairs={{0,192},{32,224},{64,128},{96,160},{128,64},{160,96},{192,0},{224,... | collective-permute-start | bytes 3145736 | tf_op jit(solution)/shard_map/ppermute | solution.py:217
  31.6 24.9 %copy-start.8 = (bf16[512,1024]{1,0:T(8,128)(2,1)}, bf16[512,1024]{1,0:T(8,128)(2,1)S(1)}, u32[]{:S(2)}) copy-start(bf16[512,1024]{1,0:T(8,128)(2,1)S(1)} %pad_maximum_fusion.1.refs_4_) | copy-start | bytes 3145732
  31.6 23.7 %collective-permute-start.5 = (bf16[512,1024]{1,0:T(8,128)(2,1)S(1)}, bf16[512,1024]{1,0:T(8,128)(2,1)S(1)}, u32[]{:S(2)}, u32[]{:S(2)}) collective-permute-start(bf16[512,1024]{1,0:T(8,128)(2,1)S(1)} %pad_maximum_fusion.1.refs_4_), channel_id=1, source_target_pairs={{0,64},{32,96},{64,0},{96,32},{128,192},{160,224},{192,128},{224,1... | collective-permute-start | bytes 3145736 | tf_op jit(solution)/shard_map/ppermute | solution.py:217
  33.2 22.1 %collective-permute-start.2 = (bf16[512,1024]{1,0:T(8,128)(2,1)S(1)}, bf16[512,1024]{1,0:T(8,128)(2,1)S(1)}, u32[]{:S(2)}, u32[]{:S(2)}) collective-permute-start(bf16[512,1024]{1,0:T(8,128)(2,1)S(1)} %pad_maximum_fusion.refs_0_), channel_id=1, source_target_pairs={{0,32},{32,0},{64,96},{96,64},{128,160},{160,128},{192,224},{224,1... | collective-permute-start | bytes 3145736 | tf_op jit(solution)/shard_map/ppermute | solution.py:217
  33.2 22.1 %collective-permute-start.6 = (bf16[512,1024]{1,0:T(8,128)(2,1)S(1)}, bf16[512,1024]{1,0:T(8,128)(2,1)S(1)}, u32[]{:S(2)}, u32[]{:S(2)}) collective-permute-start(bf16[512,1024]{1,0:T(8,128)(2,1)S(1)} %pad_maximum_fusion.1.refs_4_), channel_id=1, source_target_pairs={{0,32},{32,0},{64,96},{96,64},{128,160},{160,128},{192,224},{224,1... | collective-permute-start | bytes 3145736 | tf_op jit(solution)/shard_map/ppermute | solution.py:217
  53.8 2.7 %collective-permute-start.3 = (bf16[512,1024]{1,0:T(8,128)(2,1)S(1)}, bf16[512,1024]{1,0:T(8,128)(2,1)S(1)}, u32[]{:S(2)}, u32[]{:S(2)}) collective-permute-start(bf16[512,1024]{1,0:T(8,128)(2,1)S(1)} %collective-permute-done.1.refs_1_), channel_id=1, source_target_pairs={{0,32},{32,0},{64,96},{96,64},{128,160},{160,128},{192,224},{224,1... | collective-permute-start | bytes 3145736 | tf_op jit(solution)/shard_map/ppermute | solution.py:217
  55.3 2.8 %collective-permute-start.7 = (bf16[512,1024]{1,0:T(8,128)(2,1)S(1)}, bf16[512,1024]{1,0:T(8,128)(2,1)}, u32[]{:S(2)}, u32[]{:S(2)}) collective-permute-start(bf16[512,1024]{1,0:T(8,128)(2,1)S(1)} %collective-permute-done.5.refs_5_), channel_id=1, source_target_pairs={{0,32},{32,0},{64,96},{96,64},{128,160},{160,128},{192,224},{224,1... | collective-permute-start | bytes 3145736 | tf_op jit(solution)/shard_map/ppermute | solution.py:217
  92.1 14.0 %collective-permute-start.13 = (bf16[1024,1024]{1,0:T(8,128)(2,1)}, bf16[1024,1024]{1,0:T(8,128)(2,1)}, u32[]{:S(2)}, u32[]{:S(2)}) collective-permute-start(bf16[1024,1024]{1,0:T(8,128)(2,1)} %get-tuple-element.27), channel_id=1, source_target_pairs={{0,32},{32,0},{64,96},{96,64},{128,160},{160,128},{192,224},{224,1... | collective-permute-start | bytes 6291464 | tf_op jit(solution)/shard_map/ppermute | solution.py:217
  92.1 57.2 %all-to-all-start.1 = ((bf16[32,32,1024]{2,1,0:T(8,128)(2,1)}), bf16[32,32,1024]{2,1,0:T(8,128)(2,1)S(1)}, u32[]{:S(2)}, u32[]{:S(2)}) async-start(bf16[32,32,1024]{2,1,0:T(8,128)(2,1)} %get-tuple-element.19), calls=%async_computation.1 | async-start | bytes 4194304 | tf_op jit(solution)/shard_map/all_to_all | solution.py:213
  105.9 4.9 %collective-permute-start.8 = (bf16[1024,1024]{1,0:T(8,128)(2,1)}, bf16[1024,1024]{1,0:T(8,128)(2,1)S(1)}, u32[]{:S(2)}, u32[]{:S(2)}) collective-permute-start(bf16[1024,1024]{1,0:T(8,128)(2,1)} %get-tuple-element.24), channel_id=1, source_target_pairs={{0,32},{32,0},{64,96},{96,64},{128,160},{160,128},{192,224},{224,1... | collective-permute-start | bytes 6291464 | tf_op jit(solution)/shard_map/ppermute | solution.py:217
  109.4 14.9 %collective-permute-start.14 = (bf16[512,512]{1,0:T(8,128)(2,1)S(1)}, bf16[512,512]{1,0:T(8,128)(2,1)S(1)}, u32[]{:S(2)}, u32[]{:S(2)}) collective-permute-start(bf16[512,512]{1,0:T(8,128)(2,1)S(1)} %get-tuple-element.39), channel_id=1, source_target_pairs={{0,64},{32,96},{64,0},{96,32},{128,192},{160,224},{192,128},{224,1... | collective-permute-start | bytes 1572872 | tf_op jit(solution)/shard_map/ppermute | solution.py:217
  110.8 14.8 %collective-permute-start.16 = (bf16[512,512]{1,0:T(8,128)(2,1)S(1)}, bf16[512,512]{1,0:T(8,128)(2,1)S(1)}, u32[]{:S(2)}, u32[]{:S(2)}) collective-permute-start(bf16[512,512]{1,0:T(8,128)(2,1)S(1)} %get-tuple-element.38), channel_id=1, source_target_pairs={{0,192},{32,224},{64,128},{96,160},{128,64},{160,96},{192,0},{224,... | collective-permute-start | bytes 1572872 | tf_op jit(solution)/shard_map/ppermute | solution.py:217
  111.9 24.8 %collective-permute-start.11 = (bf16[512,512]{1,0:T(8,128)(2,1)S(1)}, bf16[512,512]{1,0:T(8,128)(2,1)S(1)}, u32[]{:S(2)}, u32[]{:S(2)}) collective-permute-start(bf16[512,512]{1,0:T(8,128)(2,1)S(1)} %get-tuple-element.42), channel_id=1, source_target_pairs={{0,192},{32,224},{64,128},{96,160},{128,64},{160,96},{192,0},{224,... | collective-permute-start | bytes 1572872 | tf_op jit(solution)/shard_map/ppermute | solution.py:217
  113.9 22.8 %collective-permute-start.9 = (bf16[512,512]{1,0:T(8,128)(2,1)S(1)}, bf16[512,512]{1,0:T(8,128)(2,1)S(1)}, u32[]{:S(2)}, u32[]{:S(2)}) collective-permute-start(bf16[512,512]{1,0:T(8,128)(2,1)S(1)} %get-tuple-element.43), channel_id=1, source_target_pairs={{0,64},{32,96},{64,0},{96,32},{128,192},{160,224},{192,128},{224,1... | collective-permute-start | bytes 1572872 | tf_op jit(solution)/shard_map/ppermute | solution.py:217
  126.7 16.2 %collective-permute-start.15 = (bf16[256,512]{1,0:T(8,128)(2,1)}, bf16[256,512]{1,0:T(8,128)(2,1)S(1)}, u32[]{:S(2)}, u32[]{:S(2)}) collective-permute-start(bf16[256,512]{1,0:T(8,128)(2,1)} %get-tuple-element.37), channel_id=1, source_target_pairs={{0,192},{32,224},{64,128},{96,160},{128,64},{160,96},{192,0},{224,... | collective-permute-start | bytes 786440 | tf_op jit(solution)/shard_map/ppermute | solution.py:217
  126.7 16.2 %collective-permute-start.17 = (bf16[256,512]{1,0:T(8,128)(2,1)}, bf16[256,512]{1,0:T(8,128)(2,1)}, u32[]{:S(2)}, u32[]{:S(2)}) collective-permute-start(bf16[256,512]{1,0:T(8,128)(2,1)} %get-tuple-element.28), channel_id=1, source_target_pairs={{0,64},{32,96},{64,0},{96,32},{128,192},{160,224},{192,128},{224,1... | collective-permute-start | bytes 786440 | tf_op jit(solution)/shard_map/ppermute | solution.py:217
  138.1 9.1 %collective-permute-start.10 = (bf16[256,512]{1,0:T(8,128)(2,1)}, bf16[256,512]{1,0:T(8,128)(2,1)}, u32[]{:S(2)}, u32[]{:S(2)}) collective-permute-start(bf16[256,512]{1,0:T(8,128)(2,1)} %get-tuple-element.41), channel_id=1, source_target_pairs={{0,192},{32,224},{64,128},{96,160},{128,64},{160,96},{192,0},{224,... | collective-permute-start | bytes 786440 | tf_op jit(solution)/shard_map/ppermute | solution.py:217
  138.1 9.1 %collective-permute-start.12 = (bf16[256,512]{1,0:T(8,128)(2,1)}, bf16[256,512]{1,0:T(8,128)(2,1)}, u32[]{:S(2)}, u32[]{:S(2)}) collective-permute-start(bf16[256,512]{1,0:T(8,128)(2,1)} %get-tuple-element.32), channel_id=1, source_target_pairs={{0,64},{32,96},{64,0},{96,32},{128,192},{160,224},{192,128},{224,1... | collective-permute-start | bytes 786440 | tf_op jit(solution)/shard_map/ppermute | solution.py:217
  142.9 6.4 %copy-start.2 = (bf16[128,512]{1,0:T(8,128)(2,1)S(1)}, bf16[128,512]{1,0:T(8,128)(2,1)}, u32[]{:S(2)}) copy-start(bf16[128,512]{1,0:T(8,128)(2,1)} %get-tuple-element.16.place_ref) | copy-start | bytes 393220
  (11 other events, 28.0 us)

commit v4 on v3

--- a/solution.py
+++ b/solution.py
@@ -106,19 +106,35 @@
         order.append(((first, 1), (second_out, 0)))
         order.append(((second, 1), (second_out, 1)))
         order.append(((second, 0), (first_out, 1)))
-    for c, pair in enumerate(order):
-        for w, ((ref, row), full) in enumerate(zip(pair, (full_in, full_out))):
+
+    def fetch(c):
+        for w, ((ref, row), full) in enumerate(zip(order[c], (full_in, full_out))):
             pltpu.make_async_copy(
                 ref.at[pl.ds(row * unit, unit)], full.at[pl.ds(c * unit, unit)], sems.at[w, c]
             ).start()
-        if c == 0:
-            for copy in row_copies:
-                copy.start()
+
+    for copy in row_copies:
+        copy.start()
+    fetch(0)
     for copy in row_copies:
         copy.wait()
+    fetch(1)
+
+    def act_copies(c, at):
+        cut = pl.ds(at, unit)
+        return [
+            pltpu.make_async_copy(ref.at[:, cut], hbm.at[:, cut], out_sems.at[i, c])
+            for i, (ref, hbm) in enumerate([(hid_ref, hid_hbm), (act_ref, act_hbm)])
+        ]
 
     @pl.loop(0, 8)
     def _(c):
+        for ahead in range(2, 8):
+
+            @pl.when(c == ahead - 2)
+            def _():
+                fetch(ahead)
+
         at = pl.multiple_of(c * unit, unit)
         for w, full in enumerate((full_in, full_out)):
             pltpu.make_async_copy(in_a.at[pl.ds(0, unit)], full.at[pl.ds(at, unit)], sems.at[w, c]).wait()
@@ -129,18 +145,14 @@
             pre = dot_t(x, w_in)
             up = dot_t(dy, w_out)
             square = pre * pre
-            t = jnp.tanh(GELU_SCALE * pre * (1.0 + GELU_CUBIC * square))
-            half = 0.5 * (1.0 + t)
-            slope = half + (0.5 * GELU_SCALE) * pre * (1.0 - t * t) * (1.0 + 3.0 * GELU_CUBIC * square)
-            hid_ref[r * tile : (r + 1) * tile, pl.ds(at, unit)] = (pre * half).astype(BF16)
+            half = 0.5 + 0.5 * jnp.tanh(pre * (GELU_SCALE + (GELU_SCALE * GELU_CUBIC) * square))
+            hid = pre * half
+            slope = half + hid * (1.0 - half) * (2.0 * GELU_SCALE + (6.0 * GELU_SCALE * GELU_CUBIC) * square)
+            hid_ref[r * tile : (r + 1) * tile, pl.ds(at, unit)] = hid.astype(BF16)
             act_ref[r * tile : (r + 1) * tile, pl.ds(at, unit)] = (up * slope).astype(BF16)
-
-    outs = [
-        pltpu.make_async_copy(a, b, out_sems.at[i])
-        for i, (a, b) in enumerate([(hid_ref, hid_hbm), (act_ref, act_hbm)])
-    ]
-    for copy in outs:
-        copy.start()
+        for copy in act_copies(c, at):
+            copy.start()
+
     columns = 256
 
     def back_copy(c, at):
@@ -161,21 +173,41 @@
 
     for c in range(width // columns):
         back_copy(c, c * columns).wait()
-    for copy in outs:
-        copy.wait()
-
-
-def grad_kernel(part, unit, acts_ref, rows_ref, keep_ref, send_ref, held_ref):
-    _, slots, _ = rows_ref.shape
-    capacity = slots // 2
-    held_ref[...] = rows_ref[:, part * capacity : (part + 1) * capacity, :].reshape(held_ref.shape)
-    for half, ref in ((4, send_ref), (0, keep_ref)):
-
-        @pl.loop(0, 4)
-        def _(c):
-            at = pl.multiple_of((half + c) * unit, unit)
-            got = dot_0(acts_ref[:, pl.ds(at, unit)], held_ref[...]).astype(BF16)
-            ref[pl.ds(pl.multiple_of(c * unit, unit), unit), :] = got
+    for c in range(8):
+        for copy in act_copies(c, c * unit):
+            copy.wait()
+
+
+def grad_kernel(part, first, unit, acts_hbm, rows_hbm, out_hbm, acts_ref, rows_ref, out_ref, sems):
+    width = out_ref.shape[1]
+    sources, capacity, _ = rows_ref.shape
+    chunks = out_ref.shape[0] // unit
+    rows_copy = pltpu.make_async_copy(
+        rows_hbm.at[:, pl.ds(part * capacity, capacity), :], rows_ref, sems.at[2 * chunks]
+    )
+    rows_copy.start()
+    loads = [
+        pltpu.make_async_copy(
+            acts_hbm.at[:, pl.ds((first + c) * unit, unit)], acts_ref.at[c], sems.at[c]
+        )
+        for c in range(chunks)
+    ]
+    for load in loads:
+        load.start()
+    stores = [
+        pltpu.make_async_copy(
+            out_ref.at[pl.ds(c * unit, unit)], out_hbm.at[pl.ds(c * unit, unit)], sems.at[chunks + c]
+        )
+        for c in range(chunks)
+    ]
+    rows_copy.wait()
+    rows = rows_ref[...].reshape(sources * capacity, width)
+    for c in range(chunks):
+        loads[c].wait()
+        out_ref[c * unit : (c + 1) * unit, :] = dot_0(acts_ref[c], rows).astype(BF16)
+        stores[c].start()
+    for store in stores:
+        store.wait()
 
 
 def combine_kernel(place_ref, hi_ref, lo_ref, rows_ref, out_ref, grad_ref):
@@ -295,23 +327,34 @@
             pltpu.VMEM((8 * unit, width), BF16),
             pltpu.SemaphoreType.DMA((2, 8)),
             pltpu.SemaphoreType.DMA((2,)),
-            pltpu.SemaphoreType.DMA((2,)),
+            pltpu.SemaphoreType.DMA((2, 8)),
             pltpu.SemaphoreType.DMA((4,)),
         ],
+        limit=48 << 20,
     )
     returned = exchange(answer)
 
     grads = []
     for part, acts in ((1, hidden), (0, grad_act)):
-        keep, send = call(
-            functools.partial(grad_kernel, part, unit),
-            [((4 * unit, width), BF16)] * 2,
-            acts,
-            rows,
-            flops=2 * cells * width * 8 * unit,
-            moved=8 << 20,
-            scratch=[pltpu.VMEM((cells, width), BF16)],
-        )
+        halves = []
+        for first in (4, 0):
+            halves.append(
+                call(
+                    functools.partial(grad_kernel, part, first, unit),
+                    [((4 * unit, width), BF16)],
+                    acts,
+                    rows,
+                    flops=cells * width * 8 * unit,
+                    specs=([anywhere] * 2, [anywhere]),
+                    scratch=[
+                        pltpu.VMEM((4, cells, unit), BF16),
+                        pltpu.VMEM((experts, capacity, width), BF16),
+                        pltpu.VMEM((4 * unit, width), BF16),
+                        pltpu.SemaphoreType.DMA((9,)),
+                    ],
+                )
+            )
+        send, keep = halves
         grads.append(scatter(keep, send, unit))
     grad_out, grad_in = grads
 

time: 153 us -> 153 us (level)
  local copies, waits for them, and re-layouts: 3.05 us -> 5 us
    concatenate x2, other arithmetic: 2.22 us -> 0.14 us  [gather(): two = jnp.concatenate([shard, got], axis=0)]
    unnamed x30, local copies, waits for them, and re-layouts: 2.9 us -> 4.84 us
    ppermute x18, waiting for transfers between devices: 54 us -> 52.3 us  [permute(): return lax.ppermute(x, 'fsdp', pairs)]
    convert_element_type x2, other arithmetic: 4.15 us -> 5.75 us  [scatter(): total = (keep.astype(F32) + got.astype(F32)).astype(BF16)]
    pallas_call x8 -> x10, Pallas kernels: 43.5 us -> 42.2 us  [call(): pl.pallas_call(kernel, out_shape=shapes[0] if single else shapes, in_spec...]
  transfers between devices with their start and end apart: 20 -> 20, of which waited for: 10 -> 11; matrix products, arithmetic and copies ran while one was open for 6% -> 6% of each run, Pallas kernels for 9% -> 12%
where the time goes in v4:
time: 153 us; the launch traced here: 151 us
  waiting for transfers between devices  60.5 us (40%)
  Pallas kernels  42.2 us (28%)
  starting transfers between devices  34.1 us (22%)
  other arithmetic  8.23 us (5%)
  local copies, waits for them, and re-layouts  5 us (3%)
    ppermute x18, waiting for transfers between devices, permute(): return lax.ppermute(x, 'fsdp', pairs)  52.3 us
    pallas_call x10, Pallas kernels, call(): pl.pallas_call(kernel, out_shape=shapes[0] if single else shapes, in_spec...  42.2 us
    all_to_all x2, starting transfers between devices, exchange(): lax.all_to_all(cells, 'expert', split_axis=0, concat_axis=0, tiled=True)  17.7 us
    ppermute x18, starting transfers between devices, permute(): return lax.ppermute(x, 'fsdp', pairs)  16.4 us
    all_to_all x2, waiting for transfers between devices, exchange(): lax.all_to_all(cells, 'expert', split_axis=0, concat_axis=0, tiled=True)  8.21 us
    convert_element_type x2, other arithmetic, scatter(): total = (keep.astype(F32) + got.astype(F32)).astype(BF16)  5.75 us
    unnamed x30, local copies, waits for them, and re-layouts  4.84 us
  transfers between devices with their start and end apart: 20, of which 11 were waited for; matrix products, arithmetic and copies ran while one was open for 6% of the time, Pallas kernels for 12%

profile of v4, /device:TPU:16, one launch (start us, length us, event | category | flops | bytes accessed | tf_op | source)
XLA Modules:
  0.0 151.0 jit_solution(14688476462981296692)
XLA Ops:
  0.6 3.3 %shard_map.94 = bf16[32,32,1024]{2,1,0:T(8,128)(2,1)} custom-call(s32[2,128]{1,0:T(2,128)} %bitcast.12, f32[2,128]{1,0:T(2,128)} %bitcast.14, bf16[128,1024]{1,0:T(8,128)(2,1)} %refs_2_.1, bf16[128,1024]{1,0:T(8,128)(2,1)} %refs_3_.1), custom_call_target="tpu_custom_call" | custom-call | flops 300000000 | bytes 4194304 | tf_op jit(solution)/shard_map/pallas_call | solution.py:233
  3.9 11.6 %all-to-all-start = ((bf16[32,32,1024]{2,1,0:T(8,128)(2,1)}), bf16[32,32,1024]{2,1,0:T(8,128)(2,1)}, u32[]{:S(2)}, u32[]{:S(2)}) async-start(bf16[32,32,1024]{2,1,0:T(8,128)(2,1)} %shard_map.94), calls=%async_computation | async-start | bytes 4194304 | tf_op jit(solution)/shard_map/all_to_all | solution.py:245
  16.9 12.1 %collective-permute-done = bf16[256,1024]{1,0:T(8,128)(2,1)S(1)} collective-permute-done((bf16[256,1024]{1,0:T(8,128)(2,1)S(1)}, bf16[256,1024]{1,0:T(8,128)(2,1)S(1)}, u32[]{:S(2)}, u32[]{:S(2)}) %collective-permute-start) | collective-permute-done | bytes 524320 | tf_op jit(solution)/shard_map/ppermute | solution.py:249
  30.1 2.0 %collective-permute-start.5 = (bf16[512,1024]{1,0:T(8,128)(2,1)S(1)}, bf16[512,1024]{1,0:T(8,128)(2,1)S(1)}, u32[]{:S(2)}, u32[]{:S(2)}) collective-permute-start(bf16[512,1024]{1,0:T(8,128)(2,1)S(1)} %pad_maximum_fusion.1.refs_4_), channel_id=1, source_target_pairs={{0,64},{32,96},{64,0},{96,32},{128,192},{160,224},{192,128},{224,1... | collective-permute-start | bytes 3145736 | tf_op jit(solution)/shard_map/ppermute | solution.py:249
  32.7 20.4 %collective-permute-done.1.refs_1_ = bf16[512,1024]{1,0:T(8,128)(2,1)S(1)} collective-permute-done((bf16[512,1024]{1,0:T(8,128)(2,1)S(1)}, bf16[512,1024]{1,0:T(8,128)(2,1)S(1)}, u32[]{:S(2)}, u32[]{:S(2)}) %collective-permute-start.1) | collective-permute-done | bytes 1048608 | tf_op jit(solution)/shard_map/ppermute | solution.py:249
  57.3 8.2 %all-to-all-done.rows_hbm = bf16[32,32,1024]{2,1,0:T(8,128)(2,1)} async-done(((bf16[32,32,1024]{2,1,0:T(8,128)(2,1)}), bf16[32,32,1024]{2,1,0:T(8,128)(2,1)}, u32[]{:S(2)}, u32[]{:S(2)}) %all-to-all-start) | async-done | bytes 2097184 | tf_op jit(solution)/shard_map/all_to_all | solution.py:245
  68.0 15.6 %shard_map.95 = (bf16[32,32,1024]{2,1,0:T(8,128)(2,1)}, bf16[512,2048]{1,0:T(8,128)(2,1)}, bf16[512,2048]{1,0:T(8,128)(2,1)}) custom-call(bf16[32,32,1024]{2,1,0:T(8,128)(2,1)} %all-to-all-done.rows_hbm, bf16[512,1024]{1,0:T(8,128)(2,1)S(1)} %pad_maximum_fusion.refs_0_, bf16[512,1024]{1,0:T(8,128)(2,1)S(1)} %collective-permute-done.1.refs_1_, ...), custom_call_target="tpu_custom_call" | custom-call | flops 8589934592 | bytes 16777216 | tf_op jit(solution)/shard_map/pallas_call | solution.py:233
  83.6 4.0 %shard_map.101 = bf16[1024,1024]{1,0:T(8,128)(2,1)} custom-call(bf16[512,2048]{1,0:T(8,128)(2,1)} %get-tuple-element.19.acts_hbm, bf16[32,32,1024]{2,1,0:T(8,128)(2,1)} %all-to-all-done.rows_hbm), custom_call_target="tpu_custom_call" | custom-call | flops 1073741824 | bytes 4194304 | tf_op jit(solution)/shard_map/pallas_call | solution.py:233
  87.7 6.1 %all-to-all-start.1 = ((bf16[32,32,1024]{2,1,0:T(8,128)(2,1)}), bf16[32,32,1024]{2,1,0:T(8,128)(2,1)S(1)}, u32[]{:S(2)}, u32[]{:S(2)}) async-start(bf16[32,32,1024]{2,1,0:T(8,128)(2,1)} %get-tuple-element.15), calls=%async_computation.1 | async-start | bytes 4194304 | tf_op jit(solution)/shard_map/all_to_all | solution.py:245
  93.9 4.0 %shard_map.98 = bf16[1024,1024]{1,0:T(8,128)(2,1)} custom-call(bf16[512,2048]{1,0:T(8,128)(2,1)} %get-tuple-element.18.acts_hbm, bf16[32,32,1024]{2,1,0:T(8,128)(2,1)} %all-to-all-done.rows_hbm), custom_call_target="tpu_custom_call" | custom-call | flops 1073741824 | bytes 4194304 | tf_op jit(solution)/shard_map/pallas_call | solution.py:233
  98.4 4.0 %shard_map.100 = bf16[1024,1024]{1,0:T(8,128)(2,1)} custom-call(bf16[512,2048]{1,0:T(8,128)(2,1)} %get-tuple-element.19.acts_hbm, bf16[32,32,1024]{2,1,0:T(8,128)(2,1)} %all-to-all-done.rows_hbm), custom_call_target="tpu_custom_call" | custom-call | flops 1073741824 | bytes 4194304 | tf_op jit(solution)/shard_map/pallas_call | solution.py:233
  102.4 4.0 %shard_map.97 = bf16[1024,1024]{1,0:T(8,128)(2,1)} custom-call(bf16[512,2048]{1,0:T(8,128)(2,1)} %get-tuple-element.18.acts_hbm, bf16[32,32,1024]{2,1,0:T(8,128)(2,1)} %all-to-all-done.rows_hbm), custom_call_target="tpu_custom_call" | custom-call | flops 1073741824 | bytes 4194304 | tf_op jit(solution)/shard_map/pallas_call | solution.py:233
  106.5 3.2 %add_convert_fusion = bf16[1024,1024]{1,0:T(8,128)(2,1)S(1)} fusion(bf16[1024,1024]{1,0:T(8,128)(2,1)} %collective-permute-done.13, bf16[1024,1024]{1,0:T(8,128)(2,1)} %shard_map.100), kind=kLoop, calls=%fused_computation | loop fusion | flops 4194304 | bytes 6291456 | tf_op jit(solution)/shard_map/convert_element_type | solution.py:263
  111.3 2.6 %add_convert_fusion.1 = bf16[1024,1024]{1,0:T(8,128)(2,1)S(1)} fusion(bf16[1024,1024]{1,0:T(8,128)(2,1)} %collective-permute-done.8, bf16[1024,1024]{1,0:T(8,128)(2,1)S(1)} %copy-done.9), kind=kLoop, calls=%fused_computation.1 | loop fusion | flops 4194304 | bytes 6291456 | tf_op jit(solution)/shard_map/convert_element_type | solution.py:263
  113.9 2.0 %collective-permute-start.11 = (bf16[512,512]{1,0:T(8,128)(2,1)S(1)}, bf16[512,512]{1,0:T(8,128)(2,1)S(1)}, u32[]{:S(2)}, u32[]{:S(2)}) collective-permute-start(bf16[512,512]{1,0:T(8,128)(2,1)S(1)} %get-tuple-element.34), channel_id=1, source_target_pairs={{0,192},{32,224},{64,128},{96,160},{128,64},{160,96},{192,0},{224,... | collective-permute-start | bytes 1572872 | tf_op jit(solution)/shard_map/ppermute | solution.py:249
  115.9 2.0 %collective-permute-start.9 = (bf16[512,512]{1,0:T(8,128)(2,1)S(1)}, bf16[512,512]{1,0:T(8,128)(2,1)S(1)}, u32[]{:S(2)}, u32[]{:S(2)}) collective-permute-start(bf16[512,512]{1,0:T(8,128)(2,1)S(1)} %get-tuple-element.35), channel_id=1, source_target_pairs={{0,64},{32,96},{64,0},{96,32},{128,192},{160,224},{192,128},{224,1... | collective-permute-start | bytes 1572872 | tf_op jit(solution)/shard_map/ppermute | solution.py:249
  117.9 6.8 %collective-permute-done.14 = bf16[512,512]{1,0:T(8,128)(2,1)S(1)} collective-permute-done((bf16[512,512]{1,0:T(8,128)(2,1)S(1)}, bf16[512,512]{1,0:T(8,128)(2,1)S(1)}, u32[]{:S(2)}, u32[]{:S(2)}) %collective-permute-start.14) | collective-permute-done | bytes 524320 | tf_op jit(solution)/shard_map/ppermute | solution.py:249
  127.0 3.0 %collective-permute-start.17 = (bf16[256,512]{1,0:T(8,128)(2,1)}, bf16[256,512]{1,0:T(8,128)(2,1)}, u32[]{:S(2)}, u32[]{:S(2)}) collective-permute-start(bf16[256,512]{1,0:T(8,128)(2,1)} %get-tuple-element.20), channel_id=1, source_target_pairs={{0,64},{32,96},{64,0},{96,32},{128,192},{160,224},{192,128},{224,1... | collective-permute-start | bytes 786440 | tf_op jit(solution)/shard_map/ppermute | solution.py:249
  130.0 7.1 %collective-permute-done.11 = bf16[512,512]{1,0:T(8,128)(2,1)S(1)} collective-permute-done((bf16[512,512]{1,0:T(8,128)(2,1)S(1)}, bf16[512,512]{1,0:T(8,128)(2,1)S(1)}, u32[]{:S(2)}, u32[]{:S(2)}) %collective-permute-start.11) | collective-permute-done | bytes 524320 | tf_op jit(solution)/shard_map/ppermute | solution.py:249
  138.4 3.0 %collective-permute-start.12 = (bf16[256,512]{1,0:T(8,128)(2,1)}, bf16[256,512]{1,0:T(8,128)(2,1)}, u32[]{:S(2)}, u32[]{:S(2)}) collective-permute-start(bf16[256,512]{1,0:T(8,128)(2,1)} %get-tuple-element.24), channel_id=1, source_target_pairs={{0,64},{32,96},{64,0},{96,32},{128,192},{160,224},{192,128},{224,1... | collective-permute-start | bytes 786440 | tf_op jit(solution)/shard_map/ppermute | solution.py:249
  141.4 1.8 %shard_map.93 = (bf16[128,512]{1,0:T(8,128)(2,1)}, bf16[128,512]{1,0:T(8,128)(2,1)}, bf16[128,512]{1,0:T(8,128)(2,1)}) custom-call(s32[2,128]{1,0:T(2,128)} %bitcast.13, f32[2,128]{1,0:T(2,128)} %bitcast.15), custom_call_target="tpu_custom_call" | custom-call | flops 300000000 | bytes 4194304 | tf_op jit(solution)/shard_map/pallas_call | solution.py:233
  143.2 2.1 %shard_map.102 = f32[256,1024]{1,0:T(8,128)} custom-call(f32[256,512]{1,0:T(8,128)S(1)} %get-tuple-element.28.own_l_ref, bf16[256,512]{1,0:T(8,128)(2,1)S(1)} %collective-permute-done.15.got_l_ref, f32[256,512]{1,0:T(8,128)S(1)} %get-tuple-element.21.own_r_ref, bf16[256,512]{1,0:T(8,128)(2,1)} %collective-permute-done.17.got_r_ref), custom_call_target="tpu_custom_call" | custom-call | flops 300000000 | bytes 4194304 | tf_op jit(solution)/shard_map/pallas_call | solution.py:233
  145.3 2.2 %collective-permute-done.10.got_l_ref = bf16[256,512]{1,0:T(8,128)(2,1)} collective-permute-done((bf16[256,512]{1,0:T(8,128)(2,1)}, bf16[256,512]{1,0:T(8,128)(2,1)}, u32[]{:S(2)}, u32[]{:S(2)}) %collective-permute-start.10) | collective-permute-done | bytes 262176 | tf_op jit(solution)/shard_map/ppermute | solution.py:249
  147.6 2.1 %shard_map.99 = f32[256,1024]{1,0:T(8,128)} custom-call(f32[256,512]{1,0:T(8,128)S(1)} %copy-done.1, bf16[256,512]{1,0:T(8,128)(2,1)} %collective-permute-done.10.got_l_ref, f32[256,512]{1,0:T(8,128)S(1)} %copy-done, bf16[256,512]{1,0:T(8,128)(2,1)} %collective-permute-done.12.got_r_ref), custom_call_target="tpu_custom_call" | custom-call | flops 300000000 | bytes 4194304 | tf_op jit(solution)/shard_map/pallas_call | solution.py:233
  (64 shorter events, 16.9 us)
Async XLA Ops:
  3.9 11.6 %copy-start.10 = (bf16[1,256,1024]{2,1,0:T(8,128)(2,1)S(1)}, bf16[1,256,1024]{2,1,0:T(8,128)(2,1)}, u32[]{:S(2)}) copy-start(bf16[1,256,1024]{2,1,0:T(8,128)(2,1)} %param.9) | copy-start | bytes 1572868
  3.9 13.0 %copy-start.11 = (bf16[1,256,1024]{2,1,0:T(8,128)(2,1)S(1)}, bf16[1,256,1024]{2,1,0:T(8,128)(2,1)}, u32[]{:S(2)}) copy-start(bf16[1,256,1024]{2,1,0:T(8,128)(2,1)} %param.10) | copy-start | bytes 1572868
  3.9 61.6 %all-to-all-start = ((bf16[32,32,1024]{2,1,0:T(8,128)(2,1)}), bf16[32,32,1024]{2,1,0:T(8,128)(2,1)}, u32[]{:S(2)}, u32[]{:S(2)}) async-start(bf16[32,32,1024]{2,1,0:T(8,128)(2,1)} %shard_map.94), calls=%async_computation | async-start | bytes 4194304 | tf_op jit(solution)/shard_map/all_to_all | solution.py:245
  15.5 14.5 %copy-start.12 = (bf16[1,256,1024]{2,1,0:T(8,128)(2,1)S(1)}, bf16[1,256,1024]{2,1,0:T(8,128)(2,1)}, u32[]{:S(2)}) copy-start(bf16[1,256,1024]{2,1,0:T(8,128)(2,1)} %param.10) | copy-start | bytes 1572868
  15.6 13.5 %collective-permute-start = (bf16[256,1024]{1,0:T(8,128)(2,1)S(1)}, bf16[256,1024]{1,0:T(8,128)(2,1)S(1)}, u32[]{:S(2)}, u32[]{:S(2)}) collective-permute-start(bf16[256,1024]{1,0:T(8,128)(2,1)S(1)} %bitcast.8), channel_id=1, source_target_pairs={{0,64},{32,96},{64,0},{96,32},{128,192},{160,224},{192,128},{224,1... | collective-permute-start | bytes 1572872 | tf_op jit(solution)/shard_map/ppermute | solution.py:249
  16.9 13.1 %collective-permute-start.4 = (bf16[256,1024]{1,0:T(8,128)(2,1)S(1)}, bf16[256,1024]{1,0:T(8,128)(2,1)S(1)}, u32[]{:S(2)}, u32[]{:S(2)}) collective-permute-start(bf16[256,1024]{1,0:T(8,128)(2,1)S(1)} %bitcast.10), channel_id=1, source_target_pairs={{0,192},{32,224},{64,128},{96,160},{128,64},{160,96},{192,0},{224,... | collective-permute-start | bytes 1572872 | tf_op jit(solution)/shard_map/ppermute | solution.py:249
  29.1 24.0 %collective-permute-start.1 = (bf16[512,1024]{1,0:T(8,128)(2,1)S(1)}, bf16[512,1024]{1,0:T(8,128)(2,1)S(1)}, u32[]{:S(2)}, u32[]{:S(2)}) collective-permute-start(bf16[512,1024]{1,0:T(8,128)(2,1)S(1)} %pad_maximum_fusion.refs_0_), channel_id=1, source_target_pairs={{0,192},{32,224},{64,128},{96,160},{128,64},{160,96},{192,0},{224,... | collective-permute-start | bytes 3145736 | tf_op jit(solution)/shard_map/ppermute | solution.py:249
  30.1 23.9 %collective-permute-start.5 = (bf16[512,1024]{1,0:T(8,128)(2,1)S(1)}, bf16[512,1024]{1,0:T(8,128)(2,1)S(1)}, u32[]{:S(2)}, u32[]{:S(2)}) collective-permute-start(bf16[512,1024]{1,0:T(8,128)(2,1)S(1)} %pad_maximum_fusion.1.refs_4_), channel_id=1, source_target_pairs={{0,64},{32,96},{64,0},{96,32},{128,192},{160,224},{192,128},{224,1... | collective-permute-start | bytes 3145736 | tf_op jit(solution)/shard_map/ppermute | solution.py:249
  32.1 21.9 %collective-permute-start.2 = (bf16[512,1024]{1,0:T(8,128)(2,1)S(1)}, bf16[512,1024]{1,0:T(8,128)(2,1)S(1)}, u32[]{:S(2)}, u32[]{:S(2)}) collective-permute-start(bf16[512,1024]{1,0:T(8,128)(2,1)S(1)} %pad_maximum_fusion.refs_0_), channel_id=1, source_target_pairs={{0,32},{32,0},{64,96},{96,64},{128,160},{160,128},{192,224},{224,1... | collective-permute-start | bytes 3145736 | tf_op jit(solution)/shard_map/ppermute | solution.py:249
  32.1 22.9 %collective-permute-start.6 = (bf16[512,1024]{1,0:T(8,128)(2,1)S(1)}, bf16[512,1024]{1,0:T(8,128)(2,1)S(1)}, u32[]{:S(2)}, u32[]{:S(2)}) collective-permute-start(bf16[512,1024]{1,0:T(8,128)(2,1)S(1)} %pad_maximum_fusion.1.refs_4_), channel_id=1, source_target_pairs={{0,32},{32,0},{64,96},{96,64},{128,160},{160,128},{192,224},{224,1... | collective-permute-start | bytes 3145736 | tf_op jit(solution)/shard_map/ppermute | solution.py:249
  53.0 2.7 %collective-permute-start.3 = (bf16[512,1024]{1,0:T(8,128)(2,1)S(1)}, bf16[512,1024]{1,0:T(8,128)(2,1)S(1)}, u32[]{:S(2)}, u32[]{:S(2)}) collective-permute-start(bf16[512,1024]{1,0:T(8,128)(2,1)S(1)} %collective-permute-done.1.refs_1_), channel_id=1, source_target_pairs={{0,32},{32,0},{64,96},{96,64},{128,160},{160,128},{192,224},{224,1... | collective-permute-start | bytes 3145736 | tf_op jit(solution)/shard_map/ppermute | solution.py:249
  54.0 3.3 %collective-permute-start.7 = (bf16[512,1024]{1,0:T(8,128)(2,1)S(1)}, bf16[512,1024]{1,0:T(8,128)(2,1)}, u32[]{:S(2)}, u32[]{:S(2)}) collective-permute-start(bf16[512,1024]{1,0:T(8,128)(2,1)S(1)} %collective-permute-done.5.refs_5_), channel_id=1, source_target_pairs={{0,32},{32,0},{64,96},{96,64},{128,160},{160,128},{192,224},{224,1... | collective-permute-start | bytes 3145736 | tf_op jit(solution)/shard_map/ppermute | solution.py:249
  87.6 18.8 %collective-permute-start.13 = (bf16[1024,1024]{1,0:T(8,128)(2,1)}, bf16[1024,1024]{1,0:T(8,128)(2,1)}, u32[]{:S(2)}, u32[]{:S(2)}) collective-permute-start(bf16[1024,1024]{1,0:T(8,128)(2,1)} %shard_map.101), channel_id=1, source_target_pairs={{0,32},{32,0},{64,96},{96,64},{128,160},{160,128},{192,224},{224,1... | collective-permute-start | bytes 6291464 | tf_op jit(solution)/shard_map/ppermute | solution.py:249
  87.7 61.9 %all-to-all-start.1 = ((bf16[32,32,1024]{2,1,0:T(8,128)(2,1)}), bf16[32,32,1024]{2,1,0:T(8,128)(2,1)S(1)}, u32[]{:S(2)}, u32[]{:S(2)}) async-start(bf16[32,32,1024]{2,1,0:T(8,128)(2,1)} %get-tuple-element.15), calls=%async_computation.1 | async-start | bytes 4194304 | tf_op jit(solution)/shard_map/all_to_all | solution.py:245
  97.9 13.2 %collective-permute-start.8 = (bf16[1024,1024]{1,0:T(8,128)(2,1)}, bf16[1024,1024]{1,0:T(8,128)(2,1)}, u32[]{:S(2)}, u32[]{:S(2)}) collective-permute-start(bf16[1024,1024]{1,0:T(8,128)(2,1)} %shard_map.98), channel_id=1, source_target_pairs={{0,32},{32,0},{64,96},{96,64},{128,160},{160,128},{192,224},{224,1... | collective-permute-start | bytes 6291464 | tf_op jit(solution)/shard_map/ppermute | solution.py:249
  109.8 14.9 %collective-permute-start.14 = (bf16[512,512]{1,0:T(8,128)(2,1)S(1)}, bf16[512,512]{1,0:T(8,128)(2,1)S(1)}, u32[]{:S(2)}, u32[]{:S(2)}) collective-permute-start(bf16[512,512]{1,0:T(8,128)(2,1)S(1)} %get-tuple-element.31), channel_id=1, source_target_pairs={{0,64},{32,96},{64,0},{96,32},{128,192},{160,224},{192,128},{224,1... | collective-permute-start | bytes 1572872 | tf_op jit(solution)/shard_map/ppermute | solution.py:249
  111.1 14.8 %collective-permute-start.16 = (bf16[512,512]{1,0:T(8,128)(2,1)S(1)}, bf16[512,512]{1,0:T(8,128)(2,1)S(1)}, u32[]{:S(2)}, u32[]{:S(2)}) collective-permute-start(bf16[512,512]{1,0:T(8,128)(2,1)S(1)} %get-tuple-element.30), channel_id=1, source_target_pairs={{0,192},{32,224},{64,128},{96,160},{128,64},{160,96},{192,0},{224,... | collective-permute-start | bytes 1572872 | tf_op jit(solution)/shard_map/ppermute | solution.py:249
  113.9 23.2 %collective-permute-start.11 = (bf16[512,512]{1,0:T(8,128)(2,1)S(1)}, bf16[512,512]{1,0:T(8,128)(2,1)S(1)}, u32[]{:S(2)}, u32[]{:S(2)}) collective-permute-start(bf16[512,512]{1,0:T(8,128)(2,1)S(1)} %get-tuple-element.34), channel_id=1, source_target_pairs={{0,192},{32,224},{64,128},{96,160},{128,64},{160,96},{192,0},{224,... | collective-permute-start | bytes 1572872 | tf_op jit(solution)/shard_map/ppermute | solution.py:249
  115.9 21.3 %collective-permute-start.9 = (bf16[512,512]{1,0:T(8,128)(2,1)S(1)}, bf16[512,512]{1,0:T(8,128)(2,1)S(1)}, u32[]{:S(2)}, u32[]{:S(2)}) collective-permute-start(bf16[512,512]{1,0:T(8,128)(2,1)S(1)} %get-tuple-element.35), channel_id=1, source_target_pairs={{0,64},{32,96},{64,0},{96,32},{128,192},{160,224},{192,128},{224,1... | collective-permute-start | bytes 1572872 | tf_op jit(solution)/shard_map/ppermute | solution.py:249
  127.0 16.2 %collective-permute-start.15 = (bf16[256,512]{1,0:T(8,128)(2,1)}, bf16[256,512]{1,0:T(8,128)(2,1)S(1)}, u32[]{:S(2)}, u32[]{:S(2)}) collective-permute-start(bf16[256,512]{1,0:T(8,128)(2,1)} %get-tuple-element.29), channel_id=1, source_target_pairs={{0,192},{32,224},{64,128},{96,160},{128,64},{160,96},{192,0},{224,... | collective-permute-start | bytes 786440 | tf_op jit(solution)/shard_map/ppermute | solution.py:249
  127.0 16.2 %collective-permute-start.17 = (bf16[256,512]{1,0:T(8,128)(2,1)}, bf16[256,512]{1,0:T(8,128)(2,1)}, u32[]{:S(2)}, u32[]{:S(2)}) collective-permute-start(bf16[256,512]{1,0:T(8,128)(2,1)} %get-tuple-element.20), channel_id=1, source_target_pairs={{0,64},{32,96},{64,0},{96,32},{128,192},{160,224},{192,128},{224,1... | collective-permute-start | bytes 786440 | tf_op jit(solution)/shard_map/ppermute | solution.py:249
  138.4 9.1 %collective-permute-start.10 = (bf16[256,512]{1,0:T(8,128)(2,1)}, bf16[256,512]{1,0:T(8,128)(2,1)}, u32[]{:S(2)}, u32[]{:S(2)}) collective-permute-start(bf16[256,512]{1,0:T(8,128)(2,1)} %get-tuple-element.33), channel_id=1, source_target_pairs={{0,192},{32,224},{64,128},{96,160},{128,64},{160,96},{192,0},{224,... | collective-permute-start | bytes 786440 | tf_op jit(solution)/shard_map/ppermute | solution.py:249
  138.4 9.1 %collective-permute-start.12 = (bf16[256,512]{1,0:T(8,128)(2,1)}, bf16[256,512]{1,0:T(8,128)(2,1)}, u32[]{:S(2)}, u32[]{:S(2)}) collective-permute-start(bf16[256,512]{1,0:T(8,128)(2,1)} %get-tuple-element.24), channel_id=1, source_target_pairs={{0,64},{32,96},{64,0},{96,32},{128,192},{160,224},{192,128},{224,1... | collective-permute-start | bytes 786440 | tf_op jit(solution)/shard_map/ppermute | solution.py:249
  143.2 6.4 %copy-start.2 = (bf16[128,512]{1,0:T(8,128)(2,1)S(1)}, bf16[128,512]{1,0:T(8,128)(2,1)}, u32[]{:S(2)}) copy-start(bf16[128,512]{1,0:T(8,128)(2,1)} %get-tuple-element.12.place_ref) | copy-start | bytes 393220
  (11 other events, 26.0 us)

commit v5 on v4

--- a/solution.py
+++ b/solution.py
@@ -19,10 +19,6 @@
 
 def dot_t(a, b):
     return lax.dot_general(a, b, (((1,), (1,)), ((), ())), preferred_element_type=F32)
-
-
-def dot_0(a, b):
-    return lax.dot_general(a, b, (((0,), (0,)), ((), ())), preferred_element_type=F32)
 
 
 def dot(a, b):
@@ -178,36 +174,64 @@
             copy.wait()
 
 
-def grad_kernel(part, first, unit, acts_hbm, rows_hbm, out_hbm, acts_ref, rows_ref, out_ref, sems):
-    width = out_ref.shape[1]
-    sources, capacity, _ = rows_ref.shape
-    chunks = out_ref.shape[0] // unit
-    rows_copy = pltpu.make_async_copy(
-        rows_hbm.at[:, pl.ds(part * capacity, capacity), :], rows_ref, sems.at[2 * chunks]
-    )
-    rows_copy.start()
-    loads = [
-        pltpu.make_async_copy(
-            acts_hbm.at[:, pl.ds((first + c) * unit, unit)], acts_ref.at[c], sems.at[c]
+def grad_kernel(part, first, unit, acts_hbm, rows_hbm, *refs):
+    last = first == 0
+    if last:
+        got_hbm, outs_hbm, (acts_ref, rows_ref, turned_ref, got_ref), outs, sems = (
+            refs[0], refs[1:6], refs[6:10], refs[10:15], refs[15]
         )
-        for c in range(chunks)
+    else:
+        outs_hbm, (acts_ref, rows_ref, turned_ref), outs, sems = refs[:1], refs[1:4], refs[4:5], refs[5]
+    sources, capacity, width = rows_ref.shape
+    columns = 256
+    chunks = width // columns
+    copies = [
+        pltpu.make_async_copy(acts_hbm.at[:, pl.ds(first * unit, 4 * unit)], acts_ref, sems.at[0]),
+        pltpu.make_async_copy(rows_hbm.at[:, pl.ds(part * capacity, capacity), :], rows_ref, sems.at[1]),
     ]
-    for load in loads:
-        load.start()
-    stores = [
-        pltpu.make_async_copy(
-            out_ref.at[pl.ds(c * unit, unit)], out_hbm.at[pl.ds(c * unit, unit)], sems.at[chunks + c]
-        )
-        for c in range(chunks)
-    ]
-    rows_copy.wait()
-    rows = rows_ref[...].reshape(sources * capacity, width)
+    if last:
+        copies.append(pltpu.make_async_copy(got_hbm, got_ref, sems.at[2]))
+    for copy in copies:
+        copy.start()
+    copies[0].wait()
+    for c in range(4):
+        turned_ref[c * unit : (c + 1) * unit, :] = jnp.transpose(acts_ref[:, c * unit : (c + 1) * unit])
+    for copy in copies[1:]:
+        copy.wait()
+    stores = []
+
+    def store(at, ref, hbm):
+        stores.append(pltpu.make_async_copy(ref, hbm, sems.at[at]))
+        stores[-1].start()
+
     for c in range(chunks):
-        loads[c].wait()
-        out_ref[c * unit : (c + 1) * unit, :] = dot_0(acts_ref[c], rows).astype(BF16)
-        stores[c].start()
-    for store in stores:
-        store.wait()
+        cut = slice(c * columns, (c + 1) * columns)
+        rows = rows_ref[:, :, cut].reshape(sources * capacity, columns)
+        got = dot(turned_ref[...], rows)
+        if not last:
+            outs[0][:, cut] = got.astype(BF16)
+            window = pl.ds(c * columns, columns)
+            store(3 + c, outs[0].at[:, window], outs_hbm[0].at[:, window])
+            continue
+        got = got + got_ref[:, cut].astype(F32)
+        own_ref, left_ref, right_ref, next_l_ref, next_r_ref = outs
+        own_ref[:, cut] = got[:unit]
+        side = slice((c % (chunks // 2)) * columns, (c % (chunks // 2) + 1) * columns)
+        if c < chunks // 2:
+            left_ref[:, side] = got[unit : 3 * unit].astype(BF16)
+            next_l_ref[:, side] = got[3 * unit :]
+        else:
+            right_ref[:, side] = got[2 * unit :].astype(BF16)
+            next_r_ref[:, side] = got[unit : 2 * unit]
+        if c == chunks // 2 - 1:
+            store(3, left_ref, outs_hbm[1])
+            store(4, next_l_ref, outs_hbm[3])
+    if last:
+        store(5, right_ref, outs_hbm[2])
+        store(6, next_r_ref, outs_hbm[4])
+        store(7, own_ref, outs_hbm[0])
+    for copy in stores:
+        copy.wait()
 
 
 def combine_kernel(place_ref, hi_ref, lo_ref, rows_ref, out_ref, grad_ref):
@@ -219,10 +243,11 @@
     grad_ref[...] = dot(place_ref[...], rows).astype(BF16)
 
 
-def finish_kernel(own_l_ref, got_l_ref, own_r_ref, got_r_ref, out_ref):
-    half = own_l_ref.shape[1]
-    out_ref[:, :half] = own_l_ref[...] + got_l_ref[...].astype(F32)
-    out_ref[:, half:] = own_r_ref[...] + got_r_ref[...].astype(F32)
+def finish_kernel(own_ref, first_l_ref, got_l_ref, first_r_ref, got_r_ref, out_ref):
+    half = got_l_ref.shape[1]
+    unit = out_ref.shape[0]
+    out_ref[:, :half] = own_ref[:, :half] + first_l_ref[:unit, :].astype(F32) + got_l_ref[...].astype(F32)
+    out_ref[:, half:] = own_ref[:, half:] + first_r_ref[unit:, :].astype(F32) + got_r_ref[...].astype(F32)
 
 
 def call(kernel, outs, *args, flops=3e8, moved=4 << 20, specs=None, scratch=(), limit=None):
@@ -258,20 +283,47 @@
     return two, other, core_two, core_other
 
 
-def scatter(keep, send, unit):
+def scatter(acts, rows, part, unit):
+    cells = acts.shape[0]
+    sources, slots, width = rows.shape
+    anywhere = pl.BlockSpec(memory_space=pl.ANY)
+
+    def product(first, outs, *more):
+        return call(
+            functools.partial(grad_kernel, part, first, unit),
+            outs,
+            acts,
+            rows,
+            *more,
+            flops=cells * width * 8 * unit,
+            specs=([anywhere] * (2 + len(more)), [anywhere] * len(outs)),
+            scratch=[
+                pltpu.VMEM((cells, 4 * unit), BF16),
+                pltpu.VMEM((sources, slots // 2, width), BF16),
+                pltpu.VMEM((4 * unit, cells), BF16),
+            ]
+            + [pltpu.VMEM(m.shape, m.dtype) for m in more]
+            + [pltpu.VMEM(s, d) for s, d in outs]
+            + [pltpu.SemaphoreType.DMA((8,))],
+        )
+
+    half = width // 2
+    send = product(4, [((4 * unit, width), BF16)])
     got = permute(send, PAIR_C)
-    total = (keep.astype(F32) + got.astype(F32)).astype(BF16)
-    half = total.shape[1] // 2
-    left, right = total[:, :half], total[:, half:]
-    got_l = permute(left[unit : 3 * unit], PAIR_A)
-    got_r = permute(right[2 * unit :], PAIR_B)
-    own_l = left[:unit].astype(F32) + got_l[:unit].astype(F32)
-    next_l = left[3 * unit :].astype(F32) + got_l[unit:].astype(F32)
-    own_r = right[:unit].astype(F32) + got_r[unit:].astype(F32)
-    next_r = right[unit : 2 * unit].astype(F32) + got_r[:unit].astype(F32)
-    got_l = permute(next_l.astype(BF16), PAIR_B)
-    got_r = permute(next_r.astype(BF16), PAIR_A)
-    return call(finish_kernel, [((unit, 2 * half), F32)], own_l, got_l, own_r, got_r, limit=16 << 20)
+    own, left, right, next_l, next_r = product(
+        0,
+        [((unit, width), F32)] + [((2 * unit, half), BF16)] * 2 + [((unit, half), F32)] * 2,
+        got,
+    )
+    first_l = permute(left, PAIR_A)
+    first_r = permute(right, PAIR_B)
+    next_l = (next_l + first_l[unit:].astype(F32)).astype(BF16)
+    next_r = (next_r + first_r[:unit].astype(F32)).astype(BF16)
+    got_l = permute(next_l, PAIR_B)
+    got_r = permute(next_r, PAIR_A)
+    return call(
+        finish_kernel, [((unit, width), F32)], own, first_l, got_l, first_r, got_r, limit=16 << 20
+    )
 
 
 def layer(tokens, expert_ids, gate_weights, weight_in, weight_out, cotangent):
@@ -334,29 +386,8 @@
     )
     returned = exchange(answer)
 
-    grads = []
-    for part, acts in ((1, hidden), (0, grad_act)):
-        halves = []
-        for first in (4, 0):
-            halves.append(
-                call(
-                    functools.partial(grad_kernel, part, first, unit),
-                    [((4 * unit, width), BF16)],
-                    acts,
-                    rows,
-                    flops=cells * width * 8 * unit,
-                    specs=([anywhere] * 2, [anywhere]),
-                    scratch=[
-                        pltpu.VMEM((4, cells, unit), BF16),
-                        pltpu.VMEM((experts, capacity, width), BF16),
-                        pltpu.VMEM((4 * unit, width), BF16),
-                        pltpu.SemaphoreType.DMA((9,)),
-                    ],
-                )
-            )
-        send, keep = halves
-        grads.append(scatter(keep, send, unit))
-    grad_out, grad_in = grads
+    grad_out = scatter(hidden, rows, 1, unit)
+    grad_in = scatter(grad_act, rows, 0, unit)
 
     layer_out, token_grad = call(
         combine_kernel, [((n, width), BF16)] * 2, place, hi, lo, returned, limit=16 << 20

time: 153 us -> 147 us (0.961)
  waiting for transfers between devices: 60.5 us -> 55 us
  other arithmetic: 8.23 us -> 5.33 us
  local copies, waits for them, and re-layouts: 5 us -> 7.66 us
  Pallas kernels: 42.2 us -> 43.9 us
    ppermute x18, waiting for transfers between devices: 52.3 us -> 46.8 us  [permute(): return lax.ppermute(x, 'fsdp', pairs)]
    convert_element_type x4, other arithmetic: 8.09 us -> 5.19 us  [the longest x2 2.62 us: scatter(): next_r = (next_r + first_r[:unit].astype(F32)).astype(BF16)]
    unnamed x30 -> x40, local copies, waits for them, and re-layouts: 4.84 us -> 7.66 us
    pallas_call x10, Pallas kernels: 42.2 us -> 43.9 us  [call(): pl.pallas_call(kernel, out_shape=shapes[0] if single else shapes, in_spec...]
  transfers between devices with their start and end apart: 20 -> 20, of which waited for: 11 -> 10; matrix products, arithmetic and copies ran while one was open for 6% -> 4% of each run, Pallas kernels for 12% -> 16%
where the time goes in v5:
time: 147 us; the launch traced here: 146 us
  waiting for transfers between devices  55 us (37%)
  Pallas kernels  43.9 us (30%)
  starting transfers between devices  32.9 us (22%)
  local copies, waits for them, and re-layouts  7.66 us (5%)
  other arithmetic  5.33 us (4%)
    ppermute x18, waiting for transfers between devices, permute(): return lax.ppermute(x, 'fsdp', pairs)  46.8 us
    pallas_call x10, Pallas kernels, call(): pl.pallas_call(kernel, out_shape=shapes[0] if single else shapes, in_spec...  43.9 us
    all_to_all x2, starting transfers between devices, exchange(): lax.all_to_all(cells, 'expert', split_axis=0, concat_axis=0, tiled=True)  17.7 us
    ppermute x18, starting transfers between devices, permute(): return lax.ppermute(x, 'fsdp', pairs)  15.1 us
    all_to_all x2, waiting for transfers between devices, exchange(): lax.all_to_all(cells, 'expert', split_axis=0, concat_axis=0, tiled=True)  8.21 us
    unnamed x40, local copies, waits for them, and re-layouts  7.66 us
  transfers between devices with their start and end apart: 20, of which 10 were waited for; matrix products, arithmetic and copies ran while one was open for 4% of the time, Pallas kernels for 16%

profile of v5, /device:TPU:16, one launch (start us, length us, event | category | flops | bytes accessed | tf_op | source)
XLA Modules:
  0.0 145.6 jit_solution(10684976179296714590)
XLA Ops:
  0.6 3.3 %shard_map.94 = bf16[32,32,1024]{2,1,0:T(8,128)(2,1)} custom-call(s32[2,128]{1,0:T(2,128)} %bitcast.12, f32[2,128]{1,0:T(2,128)} %bitcast.14, bf16[128,1024]{1,0:T(8,128)(2,1)} %refs_2_.1, bf16[128,1024]{1,0:T(8,128)(2,1)} %refs_3_.1), custom_call_target="tpu_custom_call" | custom-call | flops 300000000 | bytes 4194304 | tf_op jit(solution)/shard_map/pallas_call | solution.py:258
  4.0 11.6 %all-to-all-start = ((bf16[32,32,1024]{2,1,0:T(8,128)(2,1)}), bf16[32,32,1024]{2,1,0:T(8,128)(2,1)}, u32[]{:S(2)}, u32[]{:S(2)}) async-start(bf16[32,32,1024]{2,1,0:T(8,128)(2,1)} %shard_map.94), calls=%async_computation | async-start | bytes 4194304 | tf_op jit(solution)/shard_map/all_to_all | solution.py:270
  15.6 1.4 collective-permute-start
  16.9 12.1 %collective-permute-done = bf16[256,1024]{1,0:T(8,128)(2,1)S(1)} collective-permute-done((bf16[256,1024]{1,0:T(8,128)(2,1)S(1)}, bf16[256,1024]{1,0:T(8,128)(2,1)S(1)}, u32[]{:S(2)}, u32[]{:S(2)}) %collective-permute-start) | collective-permute-done | bytes 524320 | tf_op jit(solution)/shard_map/ppermute | solution.py:274
  30.1 2.0 %collective-permute-start.5 = (bf16[512,1024]{1,0:T(8,128)(2,1)S(1)}, bf16[512,1024]{1,0:T(8,128)(2,1)S(1)}, u32[]{:S(2)}, u32[]{:S(2)}) collective-permute-start(bf16[512,1024]{1,0:T(8,128)(2,1)S(1)} %pad_maximum_fusion.1.refs_4_), channel_id=1, source_target_pairs={{0,64},{32,96},{64,0},{96,32},{128,192},{160,224},{192,128},{224,1... | collective-permute-start | bytes 3145736 | tf_op jit(solution)/shard_map/ppermute | solution.py:274
  32.7 20.4 %collective-permute-done.1.refs_1_ = bf16[512,1024]{1,0:T(8,128)(2,1)S(1)} collective-permute-done((bf16[512,1024]{1,0:T(8,128)(2,1)S(1)}, bf16[512,1024]{1,0:T(8,128)(2,1)S(1)}, u32[]{:S(2)}, u32[]{:S(2)}) %collective-permute-start.1) | collective-permute-done | bytes 1048608 | tf_op jit(solution)/shard_map/ppermute | solution.py:274
  57.4 8.2 %all-to-all-done.rows_hbm = bf16[32,32,1024]{2,1,0:T(8,128)(2,1)} async-done(((bf16[32,32,1024]{2,1,0:T(8,128)(2,1)}), bf16[32,32,1024]{2,1,0:T(8,128)(2,1)}, u32[]{:S(2)}, u32[]{:S(2)}) %all-to-all-start) | async-done | bytes 2097184 | tf_op jit(solution)/shard_map/all_to_all | solution.py:270
  68.0 15.6 %shard_map.95 = (bf16[32,32,1024]{2,1,0:T(8,128)(2,1)}, bf16[512,2048]{1,0:T(8,128)(2,1)}, bf16[512,2048]{1,0:T(8,128)(2,1)}) custom-call(bf16[32,32,1024]{2,1,0:T(8,128)(2,1)} %all-to-all-done.rows_hbm, bf16[512,1024]{1,0:T(8,128)(2,1)S(1)} %pad_maximum_fusion.refs_0_, bf16[512,1024]{1,0:T(8,128)(2,1)S(1)} %collective-permute-done.1.refs_1_, ...), custom_call_target="tpu_custom_call" | custom-call | flops 8589934592 | bytes 16777216 | tf_op jit(solution)/shard_map/pallas_call | solution.py:258
  83.6 6.1 %all-to-all-start.1 = ((bf16[32,32,1024]{2,1,0:T(8,128)(2,1)}), bf16[32,32,1024]{2,1,0:T(8,128)(2,1)S(1)}, u32[]{:S(2)}, u32[]{:S(2)}) async-start(bf16[32,32,1024]{2,1,0:T(8,128)(2,1)} %get-tuple-element.25), calls=%async_computation.1 | async-start | bytes 4194304 | tf_op jit(solution)/shard_map/all_to_all | solution.py:270
  89.8 4.0 %shard_map.100 = bf16[1024,1024]{1,0:T(8,128)(2,1)} custom-call(bf16[512,2048]{1,0:T(8,128)(2,1)} %get-tuple-element.34.acts_hbm, bf16[32,32,1024]{2,1,0:T(8,128)(2,1)} %all-to-all-done.rows_hbm), custom_call_target="tpu_custom_call" | custom-call | flops 1073741824 | bytes 4194304 | tf_op jit(solution)/shard_map/pallas_call | solution.py:258
  93.8 4.0 %shard_map.97 = bf16[1024,1024]{1,0:T(8,128)(2,1)} custom-call(bf16[512,2048]{1,0:T(8,128)(2,1)} %get-tuple-element.28.acts_hbm, bf16[32,32,1024]{2,1,0:T(8,128)(2,1)} %all-to-all-done.rows_hbm), custom_call_target="tpu_custom_call" | custom-call | flops 1073741824 | bytes 4194304 | tf_op jit(solution)/shard_map/pallas_call | solution.py:258
  98.6 4.9 %shard_map.101 = (f32[256,1024]{1,0:T(8,128)}, bf16[512,512]{1,0:T(8,128)(2,1)}, bf16[512,512]{1,0:T(8,128)(2,1)}, f32[256,512]{1,0:T(8,128)}, f32[256,512]{1,0:T(8,128)}) custom-call(bf16[512,2048]{1,0:T(8,128)(2,1)} %get-tuple-element.34.acts_hbm, bf16[32,32,1024]{2,1,0:T(8,128)(2,1)} %all-to-all-done.rows_hbm, ...), custom_call_target="tpu_custom_call" | custom-call | flops 1073741824 | bytes 4194304 | tf_op jit(solution)/shard_map/pallas_call | solution.py:258
  105.1 4.9 %shard_map.98 = (f32[256,1024]{1,0:T(8,128)}, bf16[512,512]{1,0:T(8,128)(2,1)}, bf16[512,512]{1,0:T(8,128)(2,1)}, f32[256,512]{1,0:T(8,128)}, f32[256,512]{1,0:T(8,128)}) custom-call(bf16[512,2048]{1,0:T(8,128)(2,1)} %get-tuple-element.28.acts_hbm, bf16[32,32,1024]{2,1,0:T(8,128)(2,1)} %all-to-all-done.rows_hbm, ...), custom_call_target="tpu_custom_call" | custom-call | flops 1073741824 | bytes 4194304 | tf_op jit(solution)/shard_map/pallas_call | solution.py:258
  110.0 2.5 %collective-permute-start.11 = (bf16[512,512]{1,0:T(8,128)(2,1)}, bf16[512,512]{1,0:T(8,128)(2,1)S(1)}, u32[]{:S(2)}, u32[]{:S(2)}) collective-permute-start(bf16[512,512]{1,0:T(8,128)(2,1)} %get-tuple-element.32), channel_id=1, source_target_pairs={{0,192},{32,224},{64,128},{96,160},{128,64},{160,96},{192,0},{224,... | collective-permute-start | bytes 1572872 | tf_op jit(solution)/shard_map/ppermute | solution.py:274
  113.2 5.4 %collective-permute-done.16.first_r_ref = bf16[512,512]{1,0:T(8,128)(2,1)S(1)} collective-permute-done((bf16[512,512]{1,0:T(8,128)(2,1)}, bf16[512,512]{1,0:T(8,128)(2,1)S(1)}, u32[]{:S(2)}, u32[]{:S(2)}) %collective-permute-start.16) | collective-permute-done | bytes 524320 | tf_op jit(solution)/shard_map/ppermute | solution.py:274
  118.6 1.8 %add_convert_fusion = bf16[256,512]{1,0:T(8,128)(2,1)} fusion(f32[256,512]{1,0:T(8,128)} %get-tuple-element.39, bf16[512,512]{1,0:T(8,128)(2,1)S(1)} %collective-permute-done.16.first_r_ref), kind=kLoop, calls=%fused_computation.2 | loop fusion | flops 393216 | bytes 1048576 | tf_op jit(solution)/shard_map/convert_element_type | solution.py:321
  120.4 2.5 %collective-permute-start.17 = (bf16[256,512]{1,0:T(8,128)(2,1)}, bf16[256,512]{1,0:T(8,128)(2,1)S(1)}, u32[]{:S(2)}, u32[]{:S(2)}) collective-permute-start(bf16[256,512]{1,0:T(8,128)(2,1)} %add_convert_fusion), channel_id=1, source_target_pairs={{0,64},{32,96},{64,0},{96,32},{128,192},{160,224},{192,128},{224,1... | collective-permute-start | bytes 786440 | tf_op jit(solution)/shard_map/ppermute | solution.py:274
  122.9 1.8 %add_convert_fusion.1 = bf16[256,512]{1,0:T(8,128)(2,1)} fusion(f32[256,512]{1,0:T(8,128)} %get-tuple-element.37, bf16[512,512]{1,0:T(8,128)(2,1)S(1)} %collective-permute-done.14.first_l_ref), kind=kLoop, calls=%fused_computation.3 | loop fusion | flops 393216 | bytes 1048576 | tf_op jit(solution)/shard_map/convert_element_type | solution.py:320
  124.7 5.1 %collective-permute-done.11.first_r_ref = bf16[512,512]{1,0:T(8,128)(2,1)S(1)} collective-permute-done((bf16[512,512]{1,0:T(8,128)(2,1)}, bf16[512,512]{1,0:T(8,128)(2,1)S(1)}, u32[]{:S(2)}, u32[]{:S(2)}) %collective-permute-start.11) | collective-permute-done | bytes 524320 | tf_op jit(solution)/shard_map/ppermute | solution.py:274
  131.4 2.5 %collective-permute-start.12 = (bf16[256,512]{1,0:T(8,128)(2,1)}, bf16[256,512]{1,0:T(8,128)(2,1)}, u32[]{:S(2)}, u32[]{:S(2)}) collective-permute-start(bf16[256,512]{1,0:T(8,128)(2,1)} %add_convert_fusion.2), channel_id=1, source_target_pairs={{0,64},{32,96},{64,0},{96,32},{128,192},{160,224},{192,128},{224,1... | collective-permute-start | bytes 786440 | tf_op jit(solution)/shard_map/ppermute | solution.py:274
  135.5 1.8 %shard_map.93 = (bf16[128,512]{1,0:T(8,128)(2,1)}, bf16[128,512]{1,0:T(8,128)(2,1)}, bf16[128,512]{1,0:T(8,128)(2,1)}) custom-call(s32[2,128]{1,0:T(2,128)} %bitcast.13, f32[2,128]{1,0:T(2,128)} %bitcast.15), custom_call_target="tpu_custom_call" | custom-call | flops 300000000 | bytes 4194304 | tf_op jit(solution)/shard_map/pallas_call | solution.py:258
  138.6 2.1 %shard_map.102 = f32[256,1024]{1,0:T(8,128)} custom-call(f32[256,1024]{1,0:T(8,128)S(1)} %copy-done.4, bf16[512,512]{1,0:T(8,128)(2,1)S(1)} %collective-permute-done.14.first_l_ref, bf16[256,512]{1,0:T(8,128)(2,1)} %collective-permute-done.15.got_l_ref, bf16[512,512]{1,0:T(8,128)(2,1)S(1)} %collective-permute-done.16.first_r_ref, ...), custom_call_target="tpu_custom_call" | custom-call | flops 300000000 | bytes 4194304 | tf_op jit(solution)/shard_map/pallas_call | solution.py:258
  140.7 1.4 collective-permute-done.10.got_l_ref
  142.1 2.1 %shard_map.99 = f32[256,1024]{1,0:T(8,128)} custom-call(f32[256,1024]{1,0:T(8,128)S(1)} %copy-done.5, bf16[512,512]{1,0:T(8,128)(2,1)S(1)} %copy-done.3, bf16[256,512]{1,0:T(8,128)(2,1)} %collective-permute-done.10.got_l_ref, bf16[512,512]{1,0:T(8,128)(2,1)S(1)} %copy-done.1, bf16[256,512]{1,0:T(8,128)(2,1)} %collective-permute-done.12.got_r_ref), custom_call_target="tpu_custom_call" | custom-call | flops 300000000 | bytes 4194304 | tf_op jit(solution)/shard_map/pallas_call | solution.py:258
  (72 shorter events, 17.3 us)
Async XLA Ops:
  3.9 13.0 %copy-start.16 = (bf16[1,256,1024]{2,1,0:T(8,128)(2,1)S(1)}, bf16[1,256,1024]{2,1,0:T(8,128)(2,1)}, u32[]{:S(2)}) copy-start(bf16[1,256,1024]{2,1,0:T(8,128)(2,1)} %param.10) | copy-start | bytes 1572868
  4.0 61.6 %all-to-all-start = ((bf16[32,32,1024]{2,1,0:T(8,128)(2,1)}), bf16[32,32,1024]{2,1,0:T(8,128)(2,1)}, u32[]{:S(2)}, u32[]{:S(2)}) async-start(bf16[32,32,1024]{2,1,0:T(8,128)(2,1)} %shard_map.94), calls=%async_computation | async-start | bytes 4194304 | tf_op jit(solution)/shard_map/all_to_all | solution.py:270
  15.5 14.5 %copy-start.17 = (bf16[1,256,1024]{2,1,0:T(8,128)(2,1)S(1)}, bf16[1,256,1024]{2,1,0:T(8,128)(2,1)}, u32[]{:S(2)}) copy-start(bf16[1,256,1024]{2,1,0:T(8,128)(2,1)} %param.10) | copy-start | bytes 1572868
  15.6 13.5 %collective-permute-start = (bf16[256,1024]{1,0:T(8,128)(2,1)S(1)}, bf16[256,1024]{1,0:T(8,128)(2,1)S(1)}, u32[]{:S(2)}, u32[]{:S(2)}) collective-permute-start(bf16[256,1024]{1,0:T(8,128)(2,1)S(1)} %bitcast.8), channel_id=1, source_target_pairs={{0,64},{32,96},{64,0},{96,32},{128,192},{160,224},{192,128},{224,1... | collective-permute-start | bytes 1572872 | tf_op jit(solution)/shard_map/ppermute | solution.py:274
  16.9 13.1 %collective-permute-start.4 = (bf16[256,1024]{1,0:T(8,128)(2,1)S(1)}, bf16[256,1024]{1,0:T(8,128)(2,1)S(1)}, u32[]{:S(2)}, u32[]{:S(2)}) collective-permute-start(bf16[256,1024]{1,0:T(8,128)(2,1)S(1)} %bitcast.10), channel_id=1, source_target_pairs={{0,192},{32,224},{64,128},{96,160},{128,64},{160,96},{192,0},{224,... | collective-permute-start | bytes 1572872 | tf_op jit(solution)/shard_map/ppermute | solution.py:274
  29.1 24.0 %collective-permute-start.1 = (bf16[512,1024]{1,0:T(8,128)(2,1)S(1)}, bf16[512,1024]{1,0:T(8,128)(2,1)S(1)}, u32[]{:S(2)}, u32[]{:S(2)}) collective-permute-start(bf16[512,1024]{1,0:T(8,128)(2,1)S(1)} %pad_maximum_fusion.refs_0_), channel_id=1, source_target_pairs={{0,192},{32,224},{64,128},{96,160},{128,64},{160,96},{192,0},{224,... | collective-permute-start | bytes 3145736 | tf_op jit(solution)/shard_map/ppermute | solution.py:274
  30.1 23.9 %collective-permute-start.5 = (bf16[512,1024]{1,0:T(8,128)(2,1)S(1)}, bf16[512,1024]{1,0:T(8,128)(2,1)S(1)}, u32[]{:S(2)}, u32[]{:S(2)}) collective-permute-start(bf16[512,1024]{1,0:T(8,128)(2,1)S(1)} %pad_maximum_fusion.1.refs_4_), channel_id=1, source_target_pairs={{0,64},{32,96},{64,0},{96,32},{128,192},{160,224},{192,128},{224,1... | collective-permute-start | bytes 3145736 | tf_op jit(solution)/shard_map/ppermute | solution.py:274
  32.2 21.9 %collective-permute-start.2 = (bf16[512,1024]{1,0:T(8,128)(2,1)S(1)}, bf16[512,1024]{1,0:T(8,128)(2,1)S(1)}, u32[]{:S(2)}, u32[]{:S(2)}) collective-permute-start(bf16[512,1024]{1,0:T(8,128)(2,1)S(1)} %pad_maximum_fusion.refs_0_), channel_id=1, source_target_pairs={{0,32},{32,0},{64,96},{96,64},{128,160},{160,128},{192,224},{224,1... | collective-permute-start | bytes 3145736 | tf_op jit(solution)/shard_map/ppermute | solution.py:274
  32.2 22.9 %collective-permute-start.6 = (bf16[512,1024]{1,0:T(8,128)(2,1)S(1)}, bf16[512,1024]{1,0:T(8,128)(2,1)S(1)}, u32[]{:S(2)}, u32[]{:S(2)}) collective-permute-start(bf16[512,1024]{1,0:T(8,128)(2,1)S(1)} %pad_maximum_fusion.1.refs_4_), channel_id=1, source_target_pairs={{0,32},{32,0},{64,96},{96,64},{128,160},{160,128},{192,224},{224,1... | collective-permute-start | bytes 3145736 | tf_op jit(solution)/shard_map/ppermute | solution.py:274
  53.1 2.7 %collective-permute-start.3 = (bf16[512,1024]{1,0:T(8,128)(2,1)S(1)}, bf16[512,1024]{1,0:T(8,128)(2,1)S(1)}, u32[]{:S(2)}, u32[]{:S(2)}) collective-permute-start(bf16[512,1024]{1,0:T(8,128)(2,1)S(1)} %collective-permute-done.1.refs_1_), channel_id=1, source_target_pairs={{0,32},{32,0},{64,96},{96,64},{128,160},{160,128},{192,224},{224,1... | collective-permute-start | bytes 3145736 | tf_op jit(solution)/shard_map/ppermute | solution.py:274
  54.0 3.3 %collective-permute-start.7 = (bf16[512,1024]{1,0:T(8,128)(2,1)S(1)}, bf16[512,1024]{1,0:T(8,128)(2,1)}, u32[]{:S(2)}, u32[]{:S(2)}) collective-permute-start(bf16[512,1024]{1,0:T(8,128)(2,1)S(1)} %collective-permute-done.5.refs_5_), channel_id=1, source_target_pairs={{0,32},{32,0},{64,96},{96,64},{128,160},{160,128},{192,224},{224,1... | collective-permute-start | bytes 3145736 | tf_op jit(solution)/shard_map/ppermute | solution.py:274
  83.6 60.7 %all-to-all-start.1 = ((bf16[32,32,1024]{2,1,0:T(8,128)(2,1)}), bf16[32,32,1024]{2,1,0:T(8,128)(2,1)S(1)}, u32[]{:S(2)}, u32[]{:S(2)}) async-start(bf16[32,32,1024]{2,1,0:T(8,128)(2,1)} %get-tuple-element.25), calls=%async_computation.1 | async-start | bytes 4194304 | tf_op jit(solution)/shard_map/all_to_all | solution.py:270
  93.7 4.8 %collective-permute-start.13 = (bf16[1024,1024]{1,0:T(8,128)(2,1)}, bf16[1024,1024]{1,0:T(8,128)(2,1)}, u32[]{:S(2)}, u32[]{:S(2)}) collective-permute-start(bf16[1024,1024]{1,0:T(8,128)(2,1)} %shard_map.100), channel_id=1, source_target_pairs={{0,32},{32,0},{64,96},{96,64},{128,160},{160,128},{192,224},{224,1... | collective-permute-start | bytes 6291464 | tf_op jit(solution)/shard_map/ppermute | solution.py:274
  97.8 7.2 %collective-permute-start.8 = (bf16[1024,1024]{1,0:T(8,128)(2,1)}, bf16[1024,1024]{1,0:T(8,128)(2,1)}, u32[]{:S(2)}, u32[]{:S(2)}) collective-permute-start(bf16[1024,1024]{1,0:T(8,128)(2,1)} %shard_map.97), channel_id=1, source_target_pairs={{0,32},{32,0},{64,96},{96,64},{128,160},{160,128},{192,224},{224,1... | collective-permute-start | bytes 6291464 | tf_op jit(solution)/shard_map/ppermute | solution.py:274
  103.5 15.1 %collective-permute-start.16 = (bf16[512,512]{1,0:T(8,128)(2,1)}, bf16[512,512]{1,0:T(8,128)(2,1)S(1)}, u32[]{:S(2)}, u32[]{:S(2)}) collective-permute-start(bf16[512,512]{1,0:T(8,128)(2,1)} %get-tuple-element.38), channel_id=1, source_target_pairs={{0,192},{32,224},{64,128},{96,160},{128,64},{160,96},{192,0},{224,... | collective-permute-start | bytes 1572872 | tf_op jit(solution)/shard_map/ppermute | solution.py:274
  104.0 18.9 %collective-permute-start.14 = (bf16[512,512]{1,0:T(8,128)(2,1)}, bf16[512,512]{1,0:T(8,128)(2,1)S(1)}, u32[]{:S(2)}, u32[]{:S(2)}) collective-permute-start(bf16[512,512]{1,0:T(8,128)(2,1)} %get-tuple-element.36), channel_id=1, source_target_pairs={{0,64},{32,96},{64,0},{96,32},{128,192},{160,224},{192,128},{224,1... | collective-permute-start | bytes 1572872 | tf_op jit(solution)/shard_map/ppermute | solution.py:274
  109.9 19.8 %copy-start.14 = (f32[256,512]{1,0:T(8,128)S(1)}, f32[256,512]{1,0:T(8,128)}, u32[]{:S(2)}) copy-start(f32[256,512]{1,0:T(8,128)} %get-tuple-element.33) | copy-start | bytes 1572868
  110.0 23.9 %copy-start.13 = (f32[256,512]{1,0:T(8,128)S(1)}, f32[256,512]{1,0:T(8,128)}, u32[]{:S(2)}) copy-start(f32[256,512]{1,0:T(8,128)} %get-tuple-element.31) | copy-start | bytes 1572868
  110.0 19.8 %collective-permute-start.11 = (bf16[512,512]{1,0:T(8,128)(2,1)}, bf16[512,512]{1,0:T(8,128)(2,1)S(1)}, u32[]{:S(2)}, u32[]{:S(2)}) collective-permute-start(bf16[512,512]{1,0:T(8,128)(2,1)} %get-tuple-element.32), channel_id=1, source_target_pairs={{0,192},{32,224},{64,128},{96,160},{128,64},{160,96},{192,0},{224,... | collective-permute-start | bytes 1572872 | tf_op jit(solution)/shard_map/ppermute | solution.py:274
  112.4 21.4 %collective-permute-start.9 = (bf16[512,512]{1,0:T(8,128)(2,1)}, bf16[512,512]{1,0:T(8,128)(2,1)S(1)}, u32[]{:S(2)}, u32[]{:S(2)}) collective-permute-start(bf16[512,512]{1,0:T(8,128)(2,1)} %get-tuple-element.30), channel_id=1, source_target_pairs={{0,64},{32,96},{64,0},{96,32},{128,192},{160,224},{192,128},{224,1... | collective-permute-start | bytes 1572872 | tf_op jit(solution)/shard_map/ppermute | solution.py:274
  120.4 16.8 %collective-permute-start.17 = (bf16[256,512]{1,0:T(8,128)(2,1)}, bf16[256,512]{1,0:T(8,128)(2,1)S(1)}, u32[]{:S(2)}, u32[]{:S(2)}) collective-permute-start(bf16[256,512]{1,0:T(8,128)(2,1)} %add_convert_fusion), channel_id=1, source_target_pairs={{0,64},{32,96},{64,0},{96,32},{128,192},{160,224},{192,128},{224,1... | collective-permute-start | bytes 786440 | tf_op jit(solution)/shard_map/ppermute | solution.py:274
  124.7 12.5 %collective-permute-start.15 = (bf16[256,512]{1,0:T(8,128)(2,1)}, bf16[256,512]{1,0:T(8,128)(2,1)}, u32[]{:S(2)}, u32[]{:S(2)}) collective-permute-start(bf16[256,512]{1,0:T(8,128)(2,1)} %add_convert_fusion.1), channel_id=1, source_target_pairs={{0,192},{32,224},{64,128},{96,160},{128,64},{160,96},{192,0},{224,... | collective-permute-start | bytes 786440 | tf_op jit(solution)/shard_map/ppermute | solution.py:274
  131.4 9.3 %collective-permute-start.12 = (bf16[256,512]{1,0:T(8,128)(2,1)}, bf16[256,512]{1,0:T(8,128)(2,1)}, u32[]{:S(2)}, u32[]{:S(2)}) collective-permute-start(bf16[256,512]{1,0:T(8,128)(2,1)} %add_convert_fusion.2), channel_id=1, source_target_pairs={{0,64},{32,96},{64,0},{96,32},{128,192},{160,224},{192,128},{224,1... | collective-permute-start | bytes 786440 | tf_op jit(solution)/shard_map/ppermute | solution.py:274
  135.5 6.7 %collective-permute-start.10 = (bf16[256,512]{1,0:T(8,128)(2,1)}, bf16[256,512]{1,0:T(8,128)(2,1)}, u32[]{:S(2)}, u32[]{:S(2)}) collective-permute-start(bf16[256,512]{1,0:T(8,128)(2,1)} %add_convert_fusion.3), channel_id=1, source_target_pairs={{0,192},{32,224},{64,128},{96,160},{128,64},{160,96},{192,0},{224,... | collective-permute-start | bytes 786440 | tf_op jit(solution)/shard_map/ppermute | solution.py:274
  (16 other events, 45.8 us)

commit v6 on v5

--- a/solution.py
+++ b/solution.py
@@ -19,6 +19,10 @@
 
 def dot_t(a, b):
     return lax.dot_general(a, b, (((1,), (1,)), ((), ())), preferred_element_type=F32)
+
+
+def dot_0(a, b):
+    return lax.dot_general(a, b, (((0,), (0,)), ((), ())), preferred_element_type=F32)
 
 
 def dot(a, b):
@@ -83,8 +87,9 @@
 
 def expert_kernel(unit, rows_hbm, *refs):
     in_a, in_b, in_ca, in_cb, out_a, out_b, out_ca, out_cb = refs[:8]
-    back_hbm, hid_hbm, act_hbm = refs[8:11]
-    rows_ref, back_ref, hid_ref, act_ref, full_in, full_out, sems, row_sem, out_sems, back_sems = refs[11:]
+    back_hbm, hid_hbm, act_hbm, send_out_hbm, send_in_hbm = refs[8:13]
+    rows_ref, back_ref, hid_ref, act_ref, send_out_ref, send_in_ref, full_in, full_out = refs[13:21]
+    sems, row_sem, out_sems, send_sems, back_sems = refs[21:]
     sources, slots, width = rows_ref.shape
     capacity = slots // 2
     count = sources * capacity
@@ -146,10 +151,27 @@
             slope = half + hid * (1.0 - half) * (2.0 * GELU_SCALE + (6.0 * GELU_SCALE * GELU_CUBIC) * square)
             hid_ref[r * tile : (r + 1) * tile, pl.ds(at, unit)] = hid.astype(BF16)
             act_ref[r * tile : (r + 1) * tile, pl.ds(at, unit)] = (up * slope).astype(BF16)
-        for copy in act_copies(c, at):
-            copy.start()
+
+        @pl.when(c < 4)
+        def _():
+            for copy in act_copies(c, at):
+                copy.start()
 
     columns = 256
+    sends = [(1, hid_ref, send_out_ref, send_out_hbm), (0, act_ref, send_in_ref, send_in_hbm)]
+
+    def send_copy(i, c, at):
+        cut = pl.ds(at, columns)
+        return pltpu.make_async_copy(sends[i][2].at[:, cut], sends[i][3].at[:, cut], send_sems.at[i, c])
+
+    @pl.loop(0, width // columns)
+    def _(c):
+        at = pl.multiple_of(c * columns, columns)
+        for i, (part, a_ref, ref, _) in enumerate(sends):
+            rows = rows_ref[:, part * capacity : (part + 1) * capacity, pl.ds(at, columns)]
+            got = dot_0(a_ref[:, 4 * unit :], rows.reshape(count, columns))
+            ref[:, pl.ds(at, columns)] = got.astype(BF16)
+            send_copy(i, c, at).start()
 
     def back_copy(c, at):
         cut = pl.ds(at, columns)
@@ -169,34 +191,27 @@
 
     for c in range(width // columns):
         back_copy(c, c * columns).wait()
-    for c in range(8):
+    for c in range(4):
         for copy in act_copies(c, c * unit):
             copy.wait()
-
-
-def grad_kernel(part, first, unit, acts_hbm, rows_hbm, *refs):
-    last = first == 0
-    if last:
-        got_hbm, outs_hbm, (acts_ref, rows_ref, turned_ref, got_ref), outs, sems = (
-            refs[0], refs[1:6], refs[6:10], refs[10:15], refs[15]
-        )
-    else:
-        outs_hbm, (acts_ref, rows_ref, turned_ref), outs, sems = refs[:1], refs[1:4], refs[4:5], refs[5]
+    for c in range(width // columns):
+        for i in range(2):
+            send_copy(i, c, c * columns).wait()
+
+
+def grad_kernel(part, unit, acts_hbm, rows_hbm, got_hbm, *refs):
+    outs_hbm, (acts_ref, rows_ref, got_ref), outs, sems = refs[:5], refs[5:8], refs[8:13], refs[13]
     sources, capacity, width = rows_ref.shape
     columns = 256
     chunks = width // columns
     copies = [
-        pltpu.make_async_copy(acts_hbm.at[:, pl.ds(first * unit, 4 * unit)], acts_ref, sems.at[0]),
+        pltpu.make_async_copy(acts_hbm, acts_ref, sems.at[0]),
         pltpu.make_async_copy(rows_hbm.at[:, pl.ds(part * capacity, capacity), :], rows_ref, sems.at[1]),
+        pltpu.make_async_copy(got_hbm, got_ref, sems.at[2]),
     ]
-    if last:
-        copies.append(pltpu.make_async_copy(got_hbm, got_ref, sems.at[2]))
     for copy in copies:
         copy.start()
-    copies[0].wait()
-    for c in range(4):
-        turned_ref[c * unit : (c + 1) * unit, :] = jnp.transpose(acts_ref[:, c * unit : (c + 1) * unit])
-    for copy in copies[1:]:
+    for copy in copies:
         copy.wait()
     stores = []
 
@@ -204,17 +219,11 @@
         stores.append(pltpu.make_async_copy(ref, hbm, sems.at[at]))
         stores[-1].start()
 
+    own_ref, left_ref, right_ref, next_l_ref, next_r_ref = outs
     for c in range(chunks):
         cut = slice(c * columns, (c + 1) * columns)
-        rows = rows_ref[:, :, cut].reshape(sources * capacity, columns)
-        got = dot(turned_ref[...], rows)
-        if not last:
-            outs[0][:, cut] = got.astype(BF16)
-            window = pl.ds(c * columns, columns)
-            store(3 + c, outs[0].at[:, window], outs_hbm[0].at[:, window])
-            continue
+        got = dot_0(acts_ref[...], rows_ref[:, :, cut].reshape(sources * capacity, columns))
         got = got + got_ref[:, cut].astype(F32)
-        own_ref, left_ref, right_ref, next_l_ref, next_r_ref = outs
         own_ref[:, cut] = got[:unit]
         side = slice((c % (chunks // 2)) * columns, (c % (chunks // 2) + 1) * columns)
         if c < chunks // 2:
@@ -226,10 +235,9 @@
         if c == chunks // 2 - 1:
             store(3, left_ref, outs_hbm[1])
             store(4, next_l_ref, outs_hbm[3])
-    if last:
-        store(5, right_ref, outs_hbm[2])
-        store(6, next_r_ref, outs_hbm[4])
-        store(7, own_ref, outs_hbm[0])
+    store(5, right_ref, outs_hbm[2])
+    store(6, next_r_ref, outs_hbm[4])
+    store(7, own_ref, outs_hbm[0])
     for copy in stores:
         copy.wait()
 
@@ -283,37 +291,28 @@
     return two, other, core_two, core_other
 
 
-def scatter(acts, rows, part, unit):
+def scatter(send, acts, rows, part, unit):
     cells = acts.shape[0]
     sources, slots, width = rows.shape
+    half = width // 2
     anywhere = pl.BlockSpec(memory_space=pl.ANY)
-
-    def product(first, outs, *more):
-        return call(
-            functools.partial(grad_kernel, part, first, unit),
-            outs,
-            acts,
-            rows,
-            *more,
-            flops=cells * width * 8 * unit,
-            specs=([anywhere] * (2 + len(more)), [anywhere] * len(outs)),
-            scratch=[
-                pltpu.VMEM((cells, 4 * unit), BF16),
-                pltpu.VMEM((sources, slots // 2, width), BF16),
-                pltpu.VMEM((4 * unit, cells), BF16),
-            ]
-            + [pltpu.VMEM(m.shape, m.dtype) for m in more]
-            + [pltpu.VMEM(s, d) for s, d in outs]
-            + [pltpu.SemaphoreType.DMA((8,))],
-        )
-
-    half = width // 2
-    send = product(4, [((4 * unit, width), BF16)])
+    outs = [((unit, width), F32)] + [((2 * unit, half), BF16)] * 2 + [((unit, half), F32)] * 2
     got = permute(send, PAIR_C)
-    own, left, right, next_l, next_r = product(
-        0,
-        [((unit, width), F32)] + [((2 * unit, half), BF16)] * 2 + [((unit, half), F32)] * 2,
+    own, left, right, next_l, next_r = call(
+        functools.partial(grad_kernel, part, unit),
+        outs,
+        acts,
+        rows,
         got,
+        flops=cells * width * 8 * unit,
+        specs=([anywhere] * 3, [anywhere] * 5),
+        scratch=[
+            pltpu.VMEM(acts.shape, BF16),
+            pltpu.VMEM((sources, slots // 2, width), BF16),
+            pltpu.VMEM(got.shape, BF16),
+        ]
+        + [pltpu.VMEM(s, d) for s, d in outs]
+        + [pltpu.SemaphoreType.DMA((8,))],
     )
     first_l = permute(left, PAIR_A)
     first_r = permute(right, PAIR_B)
@@ -361,33 +360,36 @@
         expert_ids.T,
         gate_weights.T,
     )
-    answer, hidden, grad_act = call(
+    answer, hidden, grad_act, send_out, send_in = call(
         functools.partial(expert_kernel, unit),
-        [(shape, BF16)] + [((cells, 8 * unit), BF16)] * 2,
+        [(shape, BF16)] + [((cells, 4 * unit), BF16)] * 2 + [((4 * unit, width), BF16)] * 2,
         rows,
         *in_pieces,
         *out_pieces,
-        flops=8 * cells * width * 8 * unit,
+        flops=10 * cells * width * 8 * unit,
         moved=16 << 20,
-        specs=([anywhere] * 9, [anywhere] * 3),
+        specs=([anywhere] * 9, [anywhere] * 5),
         scratch=[
             pltpu.VMEM(shape, BF16),
             pltpu.VMEM(shape, BF16),
             pltpu.VMEM((cells, 8 * unit), BF16),
             pltpu.VMEM((cells, 8 * unit), BF16),
+            pltpu.VMEM((4 * unit, width), BF16),
+            pltpu.VMEM((4 * unit, width), BF16),
             pltpu.VMEM((8 * unit, width), BF16),
             pltpu.VMEM((8 * unit, width), BF16),
             pltpu.SemaphoreType.DMA((2, 8)),
             pltpu.SemaphoreType.DMA((2,)),
-            pltpu.SemaphoreType.DMA((2, 8)),
+            pltpu.SemaphoreType.DMA((2, 4)),
+            pltpu.SemaphoreType.DMA((2, 4)),
             pltpu.SemaphoreType.DMA((4,)),
         ],
         limit=48 << 20,
     )
     returned = exchange(answer)
 
-    grad_out = scatter(hidden, rows, 1, unit)
-    grad_in = scatter(grad_act, rows, 0, unit)
+    grad_out = scatter(send_out, hidden, rows, 1, unit)
+    grad_in = scatter(send_in, grad_act, rows, 0, unit)
 
     layer_out, token_grad = call(
         combine_kernel, [((n, width), BF16)] * 2, place, hi, lo, returned, limit=16 << 20

time: 147 us -> 146 us (level)
  waiting for transfers between devices: 55 us -> 60.2 us
  Pallas kernels: 43.9 us -> 39.5 us
  local copies, waits for them, and re-layouts: 7.66 us -> 5.88 us
    ppermute x18, waiting for transfers between devices: 46.8 us -> 52 us  [permute(): return lax.ppermute(x, 'fsdp', pairs)]
    pallas_call x10 -> x8, Pallas kernels: 43.9 us -> 39.5 us  [call(): pl.pallas_call(kernel, out_shape=shapes[0] if single else shapes, in_spec...]
    unnamed x40 -> x38, local copies, waits for them, and re-layouts: 7.66 us -> 5.88 us
  transfers between devices with their start and end apart: 20 -> 20, of which waited for: 10 -> 11; matrix products, arithmetic and copies ran while one was open for 4% -> 4% of each run, Pallas kernels for 16% -> 11%
where the time goes in v6:
time: 146 us; the launch traced here: 145 us
  waiting for transfers between devices  60.2 us (41%)
  Pallas kernels  39.5 us (27%)
  starting transfers between devices  32.8 us (22%)
  local copies, waits for them, and re-layouts  5.88 us (4%)
  other arithmetic  5.32 us (4%)
    ppermute x18, waiting for transfers between devices, permute(): return lax.ppermute(x, 'fsdp', pairs)  52 us
    pallas_call x8, Pallas kernels, call(): pl.pallas_call(kernel, out_shape=shapes[0] if single else shapes, in_spec...  39.5 us
    all_to_all x2, starting transfers between devices, exchange(): lax.all_to_all(cells, 'expert', split_axis=0, concat_axis=0, tiled=True)  17.7 us
    ppermute x18, starting transfers between devices, permute(): return lax.ppermute(x, 'fsdp', pairs)  15.1 us
    all_to_all x2, waiting for transfers between devices, exchange(): lax.all_to_all(cells, 'expert', split_axis=0, concat_axis=0, tiled=True)  8.23 us
    unnamed x38, local copies, waits for them, and re-layouts  5.88 us
  transfers between devices with their start and end apart: 20, of which 11 were waited for; matrix products, arithmetic and copies ran while one was open for 4% of the time, Pallas kernels for 11%

profile of v6, /device:TPU:16, one launch (start us, length us, event | category | flops | bytes accessed | tf_op | source)
XLA Modules:
  0.0 144.5 jit_solution(1639242448499694308)
XLA Ops:
  0.6 3.3 %shard_map.94 = bf16[32,32,1024]{2,1,0:T(8,128)(2,1)} custom-call(s32[2,128]{1,0:T(2,128)} %bitcast.12, f32[2,128]{1,0:T(2,128)} %bitcast.14, bf16[128,1024]{1,0:T(8,128)(2,1)} %refs_2_.1, bf16[128,1024]{1,0:T(8,128)(2,1)} %refs_3_.1), custom_call_target="tpu_custom_call" | custom-call | flops 300000000 | bytes 4194304 | tf_op jit(solution)/shard_map/pallas_call | solution.py:266
  3.9 11.6 %all-to-all-start = ((bf16[32,32,1024]{2,1,0:T(8,128)(2,1)}), bf16[32,32,1024]{2,1,0:T(8,128)(2,1)}, u32[]{:S(2)}, u32[]{:S(2)}) async-start(bf16[32,32,1024]{2,1,0:T(8,128)(2,1)} %shard_map.94), calls=%async_computation | async-start | bytes 4194304 | tf_op jit(solution)/shard_map/all_to_all | solution.py:278
  15.5 1.4 collective-permute-start
  16.9 12.1 %collective-permute-done = bf16[256,1024]{1,0:T(8,128)(2,1)S(1)} collective-permute-done((bf16[256,1024]{1,0:T(8,128)(2,1)S(1)}, bf16[256,1024]{1,0:T(8,128)(2,1)S(1)}, u32[]{:S(2)}, u32[]{:S(2)}) %collective-permute-start) | collective-permute-done | bytes 524320 | tf_op jit(solution)/shard_map/ppermute | solution.py:282
  30.1 2.0 %collective-permute-start.5 = (bf16[512,1024]{1,0:T(8,128)(2,1)S(1)}, bf16[512,1024]{1,0:T(8,128)(2,1)S(1)}, u32[]{:S(2)}, u32[]{:S(2)}) collective-permute-start(bf16[512,1024]{1,0:T(8,128)(2,1)S(1)} %pad_maximum_fusion.1.refs_4_), channel_id=1, source_target_pairs={{0,64},{32,96},{64,0},{96,32},{128,192},{160,224},{192,128},{224,1... | collective-permute-start | bytes 3145736 | tf_op jit(solution)/shard_map/ppermute | solution.py:282
  32.6 20.4 %collective-permute-done.1.refs_1_ = bf16[512,1024]{1,0:T(8,128)(2,1)S(1)} collective-permute-done((bf16[512,1024]{1,0:T(8,128)(2,1)S(1)}, bf16[512,1024]{1,0:T(8,128)(2,1)S(1)}, u32[]{:S(2)}, u32[]{:S(2)}) %collective-permute-start.1) | collective-permute-done | bytes 1048608 | tf_op jit(solution)/shard_map/ppermute | solution.py:282
  54.0 1.7 %collective-permute-done.3.refs_3_ = bf16[512,1024]{1,0:T(8,128)(2,1)S(1)} collective-permute-done((bf16[512,1024]{1,0:T(8,128)(2,1)S(1)}, bf16[512,1024]{1,0:T(8,128)(2,1)S(1)}, u32[]{:S(2)}, u32[]{:S(2)}) %collective-permute-start.3) | collective-permute-done | bytes 1048608 | tf_op jit(solution)/shard_map/ppermute | solution.py:282
  57.3 8.2 %all-to-all-done.rows_hbm = bf16[32,32,1024]{2,1,0:T(8,128)(2,1)} async-done(((bf16[32,32,1024]{2,1,0:T(8,128)(2,1)}), bf16[32,32,1024]{2,1,0:T(8,128)(2,1)}, u32[]{:S(2)}, u32[]{:S(2)}) %all-to-all-start) | async-done | bytes 2097184 | tf_op jit(solution)/shard_map/all_to_all | solution.py:278
  65.5 19.0 %shard_map.95 = (bf16[32,32,1024]{2,1,0:T(8,128)(2,1)}, bf16[512,1024]{1,0:T(8,128)(2,1)S(1)}, bf16[512,1024]{1,0:T(8,128)(2,1)S(1)}, bf16[1024,1024]{1,0:T(8,128)(2,1)}, bf16[1024,1024]{1,0:T(8,128)(2,1)}) custom-call(bf16[32,32,1024]{2,1,0:T(8,128)(2,1)} %all-to-all-done.rows_hbm, bf16[512,1024]{1,0:T(8,128)(2,1)S(1)} %pad_maximum_fusion.refs_0_, ...), custom_call_target="tpu_custom_call" | custom-call | flops 10737418240 | bytes 16777216 | tf_op jit(solution)/shard_map/pallas_call | solution.py:266
  86.5 6.1 %all-to-all-start.1 = ((bf16[32,32,1024]{2,1,0:T(8,128)(2,1)}), bf16[32,32,1024]{2,1,0:T(8,128)(2,1)S(1)}, u32[]{:S(2)}, u32[]{:S(2)}) async-start(bf16[32,32,1024]{2,1,0:T(8,128)(2,1)} %get-tuple-element.27), calls=%async_computation.1 | async-start | bytes 4194304 | tf_op jit(solution)/shard_map/all_to_all | solution.py:278
  93.3 4.0 %collective-permute-done.13.got_hbm = bf16[1024,1024]{1,0:T(8,128)(2,1)} collective-permute-done((bf16[1024,1024]{1,0:T(8,128)(2,1)}, bf16[1024,1024]{1,0:T(8,128)(2,1)}, u32[]{:S(2)}, u32[]{:S(2)}) %collective-permute-start.13) | collective-permute-done | bytes 2097184 | tf_op jit(solution)/shard_map/ppermute | solution.py:282
  97.3 4.9 %shard_map.99 = (f32[256,1024]{1,0:T(8,128)}, bf16[512,512]{1,0:T(8,128)(2,1)}, bf16[512,512]{1,0:T(8,128)(2,1)}, f32[256,512]{1,0:T(8,128)}, f32[256,512]{1,0:T(8,128)}) custom-call(bf16[512,1024]{1,0:T(8,128)(2,1)} %copy-done.7, bf16[32,32,1024]{2,1,0:T(8,128)(2,1)} %all-to-all-done.rows_hbm, bf16[1024,1024]{1,0:T(8,128)(2,1)} %collective-permute-done.13.got_hbm), custom_call_target="tpu_custom_call" | custom-call | flops 1073741824 | bytes 4194304 | tf_op jit(solution)/shard_map/pallas_call | solution.py:266
  104.0 4.9 %shard_map.97 = (f32[256,1024]{1,0:T(8,128)}, bf16[512,512]{1,0:T(8,128)(2,1)}, bf16[512,512]{1,0:T(8,128)(2,1)}, f32[256,512]{1,0:T(8,128)}, f32[256,512]{1,0:T(8,128)}) custom-call(bf16[512,1024]{1,0:T(8,128)(2,1)} %copy-done.6, bf16[32,32,1024]{2,1,0:T(8,128)(2,1)} %all-to-all-done.rows_hbm, bf16[1024,1024]{1,0:T(8,128)(2,1)} %collective-permute-done.8.got_hbm), custom_call_target="tpu_custom_call" | custom-call | flops 1073741824 | bytes 4194304 | tf_op jit(solution)/shard_map/pallas_call | solution.py:266
  108.9 2.5 %collective-permute-start.11 = (bf16[512,512]{1,0:T(8,128)(2,1)}, bf16[512,512]{1,0:T(8,128)(2,1)S(1)}, u32[]{:S(2)}, u32[]{:S(2)}) collective-permute-start(bf16[512,512]{1,0:T(8,128)(2,1)} %get-tuple-element.35), channel_id=1, source_target_pairs={{0,192},{32,224},{64,128},{96,160},{128,64},{160,96},{192,0},{224,... | collective-permute-start | bytes 1572872 | tf_op jit(solution)/shard_map/ppermute | solution.py:282
  112.1 5.3 %collective-permute-done.16.first_r_ref = bf16[512,512]{1,0:T(8,128)(2,1)S(1)} collective-permute-done((bf16[512,512]{1,0:T(8,128)(2,1)}, bf16[512,512]{1,0:T(8,128)(2,1)S(1)}, u32[]{:S(2)}, u32[]{:S(2)}) %collective-permute-start.16) | collective-permute-done | bytes 524320 | tf_op jit(solution)/shard_map/ppermute | solution.py:282
  117.5 1.8 %add_convert_fusion = bf16[256,512]{1,0:T(8,128)(2,1)} fusion(f32[256,512]{1,0:T(8,128)} %get-tuple-element.43, bf16[512,512]{1,0:T(8,128)(2,1)S(1)} %collective-permute-done.16.first_r_ref), kind=kLoop, calls=%fused_computation.2 | loop fusion | flops 393216 | bytes 1048576 | tf_op jit(solution)/shard_map/convert_element_type | solution.py:320
  119.3 2.5 %collective-permute-start.17 = (bf16[256,512]{1,0:T(8,128)(2,1)}, bf16[256,512]{1,0:T(8,128)(2,1)S(1)}, u32[]{:S(2)}, u32[]{:S(2)}) collective-permute-start(bf16[256,512]{1,0:T(8,128)(2,1)} %add_convert_fusion), channel_id=1, source_target_pairs={{0,64},{32,96},{64,0},{96,32},{128,192},{160,224},{192,128},{224,1... | collective-permute-start | bytes 786440 | tf_op jit(solution)/shard_map/ppermute | solution.py:282
  121.8 1.8 %add_convert_fusion.1 = bf16[256,512]{1,0:T(8,128)(2,1)} fusion(f32[256,512]{1,0:T(8,128)} %get-tuple-element.41, bf16[512,512]{1,0:T(8,128)(2,1)S(1)} %collective-permute-done.14.first_l_ref), kind=kLoop, calls=%fused_computation.3 | loop fusion | flops 393216 | bytes 1048576 | tf_op jit(solution)/shard_map/convert_element_type | solution.py:319
  123.6 5.1 %collective-permute-done.11.first_r_ref = bf16[512,512]{1,0:T(8,128)(2,1)S(1)} collective-permute-done((bf16[512,512]{1,0:T(8,128)(2,1)}, bf16[512,512]{1,0:T(8,128)(2,1)S(1)}, u32[]{:S(2)}, u32[]{:S(2)}) %collective-permute-start.11) | collective-permute-done | bytes 524320 | tf_op jit(solution)/shard_map/ppermute | solution.py:282
  130.3 2.5 %collective-permute-start.12 = (bf16[256,512]{1,0:T(8,128)(2,1)}, bf16[256,512]{1,0:T(8,128)(2,1)}, u32[]{:S(2)}, u32[]{:S(2)}) collective-permute-start(bf16[256,512]{1,0:T(8,128)(2,1)} %add_convert_fusion.2), channel_id=1, source_target_pairs={{0,64},{32,96},{64,0},{96,32},{128,192},{160,224},{192,128},{224,1... | collective-permute-start | bytes 786440 | tf_op jit(solution)/shard_map/ppermute | solution.py:282
  134.4 1.8 %shard_map.93 = (bf16[128,512]{1,0:T(8,128)(2,1)}, bf16[128,512]{1,0:T(8,128)(2,1)}, bf16[128,512]{1,0:T(8,128)(2,1)}) custom-call(s32[2,128]{1,0:T(2,128)} %bitcast.13, f32[2,128]{1,0:T(2,128)} %bitcast.15), custom_call_target="tpu_custom_call" | custom-call | flops 300000000 | bytes 4194304 | tf_op jit(solution)/shard_map/pallas_call | solution.py:266
  137.5 2.1 %shard_map.100 = f32[256,1024]{1,0:T(8,128)} custom-call(f32[256,1024]{1,0:T(8,128)S(1)} %copy-done.4, bf16[512,512]{1,0:T(8,128)(2,1)S(1)} %collective-permute-done.14.first_l_ref, bf16[256,512]{1,0:T(8,128)(2,1)} %collective-permute-done.15.got_l_ref, bf16[512,512]{1,0:T(8,128)(2,1)S(1)} %collective-permute-done.16.first_r_ref, ...), custom_call_target="tpu_custom_call" | custom-call | flops 300000000 | bytes 4194304 | tf_op jit(solution)/shard_map/pallas_call | solution.py:266
  139.6 1.4 collective-permute-done.10.got_l_ref
  141.1 2.1 %shard_map.98 = f32[256,1024]{1,0:T(8,128)} custom-call(f32[256,1024]{1,0:T(8,128)S(1)} %copy-done.5, bf16[512,512]{1,0:T(8,128)(2,1)S(1)} %copy-done.3, bf16[256,512]{1,0:T(8,128)(2,1)} %collective-permute-done.10.got_l_ref, bf16[512,512]{1,0:T(8,128)(2,1)S(1)} %copy-done.1, bf16[256,512]{1,0:T(8,128)(2,1)} %collective-permute-done.12.got_r_ref), custom_call_target="tpu_custom_call" | custom-call | flops 300000000 | bytes 4194304 | tf_op jit(solution)/shard_map/pallas_call | solution.py:266
  (68 shorter events, 15.0 us)
Async XLA Ops:
  3.9 13.0 %copy-start.15 = (bf16[1,256,1024]{2,1,0:T(8,128)(2,1)S(1)}, bf16[1,256,1024]{2,1,0:T(8,128)(2,1)}, u32[]{:S(2)}) copy-start(bf16[1,256,1024]{2,1,0:T(8,128)(2,1)} %param.10) | copy-start | bytes 1572868
  3.9 61.6 %all-to-all-start = ((bf16[32,32,1024]{2,1,0:T(8,128)(2,1)}), bf16[32,32,1024]{2,1,0:T(8,128)(2,1)}, u32[]{:S(2)}, u32[]{:S(2)}) async-start(bf16[32,32,1024]{2,1,0:T(8,128)(2,1)} %shard_map.94), calls=%async_computation | async-start | bytes 4194304 | tf_op jit(solution)/shard_map/all_to_all | solution.py:278
  15.5 13.5 %collective-permute-start = (bf16[256,1024]{1,0:T(8,128)(2,1)S(1)}, bf16[256,1024]{1,0:T(8,128)(2,1)S(1)}, u32[]{:S(2)}, u32[]{:S(2)}) collective-permute-start(bf16[256,1024]{1,0:T(8,128)(2,1)S(1)} %bitcast.8), channel_id=1, source_target_pairs={{0,64},{32,96},{64,0},{96,32},{128,192},{160,224},{192,128},{224,1... | collective-permute-start | bytes 1572872 | tf_op jit(solution)/shard_map/ppermute | solution.py:282
  16.9 13.1 %collective-permute-start.4 = (bf16[256,1024]{1,0:T(8,128)(2,1)S(1)}, bf16[256,1024]{1,0:T(8,128)(2,1)S(1)}, u32[]{:S(2)}, u32[]{:S(2)}) collective-permute-start(bf16[256,1024]{1,0:T(8,128)(2,1)S(1)} %bitcast.10), channel_id=1, source_target_pairs={{0,192},{32,224},{64,128},{96,160},{128,64},{160,96},{192,0},{224,... | collective-permute-start | bytes 1572872 | tf_op jit(solution)/shard_map/ppermute | solution.py:282
  29.1 24.0 %collective-permute-start.1 = (bf16[512,1024]{1,0:T(8,128)(2,1)S(1)}, bf16[512,1024]{1,0:T(8,128)(2,1)S(1)}, u32[]{:S(2)}, u32[]{:S(2)}) collective-permute-start(bf16[512,1024]{1,0:T(8,128)(2,1)S(1)} %pad_maximum_fusion.refs_0_), channel_id=1, source_target_pairs={{0,192},{32,224},{64,128},{96,160},{128,64},{160,96},{192,0},{224,... | collective-permute-start | bytes 3145736 | tf_op jit(solution)/shard_map/ppermute | solution.py:282
  30.1 25.6 %copy-start.11 = (bf16[512,1024]{1,0:T(8,128)(2,1)}, bf16[512,1024]{1,0:T(8,128)(2,1)S(1)}, u32[]{:S(2)}) copy-start(bf16[512,1024]{1,0:T(8,128)(2,1)S(1)} %pad_maximum_fusion.1.refs_4_) | copy-start | bytes 3145732
  30.1 23.9 %collective-permute-start.5 = (bf16[512,1024]{1,0:T(8,128)(2,1)S(1)}, bf16[512,1024]{1,0:T(8,128)(2,1)S(1)}, u32[]{:S(2)}, u32[]{:S(2)}) collective-permute-start(bf16[512,1024]{1,0:T(8,128)(2,1)S(1)} %pad_maximum_fusion.1.refs_4_), channel_id=1, source_target_pairs={{0,64},{32,96},{64,0},{96,32},{128,192},{160,224},{192,128},{224,1... | collective-permute-start | bytes 3145736 | tf_op jit(solution)/shard_map/ppermute | solution.py:282
  32.1 21.9 %collective-permute-start.2 = (bf16[512,1024]{1,0:T(8,128)(2,1)S(1)}, bf16[512,1024]{1,0:T(8,128)(2,1)S(1)}, u32[]{:S(2)}, u32[]{:S(2)}) collective-permute-start(bf16[512,1024]{1,0:T(8,128)(2,1)S(1)} %pad_maximum_fusion.refs_0_), channel_id=1, source_target_pairs={{0,32},{32,0},{64,96},{96,64},{128,160},{160,128},{192,224},{224,1... | collective-permute-start | bytes 3145736 | tf_op jit(solution)/shard_map/ppermute | solution.py:282
  32.1 21.9 %collective-permute-start.6 = (bf16[512,1024]{1,0:T(8,128)(2,1)S(1)}, bf16[512,1024]{1,0:T(8,128)(2,1)S(1)}, u32[]{:S(2)}, u32[]{:S(2)}) collective-permute-start(bf16[512,1024]{1,0:T(8,128)(2,1)S(1)} %pad_maximum_fusion.1.refs_4_), channel_id=1, source_target_pairs={{0,32},{32,0},{64,96},{96,64},{128,160},{160,128},{192,224},{224,1... | collective-permute-start | bytes 3145736 | tf_op jit(solution)/shard_map/ppermute | solution.py:282
  53.0 2.7 %collective-permute-start.3 = (bf16[512,1024]{1,0:T(8,128)(2,1)S(1)}, bf16[512,1024]{1,0:T(8,128)(2,1)S(1)}, u32[]{:S(2)}, u32[]{:S(2)}) collective-permute-start(bf16[512,1024]{1,0:T(8,128)(2,1)S(1)} %collective-permute-done.1.refs_1_), channel_id=1, source_target_pairs={{0,32},{32,0},{64,96},{96,64},{128,160},{160,128},{192,224},{224,1... | collective-permute-start | bytes 3145736 | tf_op jit(solution)/shard_map/ppermute | solution.py:282
  54.0 3.3 %collective-permute-start.7 = (bf16[512,1024]{1,0:T(8,128)(2,1)S(1)}, bf16[512,1024]{1,0:T(8,128)(2,1)}, u32[]{:S(2)}, u32[]{:S(2)}) collective-permute-start(bf16[512,1024]{1,0:T(8,128)(2,1)S(1)} %collective-permute-done.5.refs_5_), channel_id=1, source_target_pairs={{0,32},{32,0},{64,96},{96,64},{128,160},{160,128},{192,224},{224,1... | collective-permute-start | bytes 3145736 | tf_op jit(solution)/shard_map/ppermute | solution.py:282
  86.5 56.7 %all-to-all-start.1 = ((bf16[32,32,1024]{2,1,0:T(8,128)(2,1)}), bf16[32,32,1024]{2,1,0:T(8,128)(2,1)S(1)}, u32[]{:S(2)}, u32[]{:S(2)}) async-start(bf16[32,32,1024]{2,1,0:T(8,128)(2,1)} %get-tuple-element.27), calls=%async_computation.1 | async-start | bytes 4194304 | tf_op jit(solution)/shard_map/all_to_all | solution.py:278
  92.7 4.6 %collective-permute-start.13 = (bf16[1024,1024]{1,0:T(8,128)(2,1)}, bf16[1024,1024]{1,0:T(8,128)(2,1)}, u32[]{:S(2)}, u32[]{:S(2)}) collective-permute-start(bf16[1024,1024]{1,0:T(8,128)(2,1)} %get-tuple-element.38), channel_id=1, source_target_pairs={{0,32},{32,0},{64,96},{96,64},{128,160},{160,128},{192,224},{224,1... | collective-permute-start | bytes 6291464 | tf_op jit(solution)/shard_map/ppermute | solution.py:282
  92.8 11.2 %collective-permute-start.8 = (bf16[1024,1024]{1,0:T(8,128)(2,1)}, bf16[1024,1024]{1,0:T(8,128)(2,1)}, u32[]{:S(2)}, u32[]{:S(2)}) collective-permute-start(bf16[1024,1024]{1,0:T(8,128)(2,1)} %get-tuple-element.31), channel_id=1, source_target_pairs={{0,32},{32,0},{64,96},{96,64},{128,160},{160,128},{192,224},{224,1... | collective-permute-start | bytes 6291464 | tf_op jit(solution)/shard_map/ppermute | solution.py:282
  102.2 15.3 %collective-permute-start.16 = (bf16[512,512]{1,0:T(8,128)(2,1)}, bf16[512,512]{1,0:T(8,128)(2,1)S(1)}, u32[]{:S(2)}, u32[]{:S(2)}) collective-permute-start(bf16[512,512]{1,0:T(8,128)(2,1)} %get-tuple-element.42), channel_id=1, source_target_pairs={{0,192},{32,224},{64,128},{96,160},{128,64},{160,96},{192,0},{224,... | collective-permute-start | bytes 1572872 | tf_op jit(solution)/shard_map/ppermute | solution.py:282
  102.9 18.9 %collective-permute-start.14 = (bf16[512,512]{1,0:T(8,128)(2,1)}, bf16[512,512]{1,0:T(8,128)(2,1)S(1)}, u32[]{:S(2)}, u32[]{:S(2)}) collective-permute-start(bf16[512,512]{1,0:T(8,128)(2,1)} %get-tuple-element.40), channel_id=1, source_target_pairs={{0,64},{32,96},{64,0},{96,32},{128,192},{160,224},{192,128},{224,1... | collective-permute-start | bytes 1572872 | tf_op jit(solution)/shard_map/ppermute | solution.py:282
  108.9 19.8 %copy-start.13 = (f32[256,512]{1,0:T(8,128)S(1)}, f32[256,512]{1,0:T(8,128)}, u32[]{:S(2)}) copy-start(f32[256,512]{1,0:T(8,128)} %get-tuple-element.36) | copy-start | bytes 1572868
  108.9 23.9 %copy-start.12 = (f32[256,512]{1,0:T(8,128)S(1)}, f32[256,512]{1,0:T(8,128)}, u32[]{:S(2)}) copy-start(f32[256,512]{1,0:T(8,128)} %get-tuple-element.34) | copy-start | bytes 1572868
  108.9 19.8 %collective-permute-start.11 = (bf16[512,512]{1,0:T(8,128)(2,1)}, bf16[512,512]{1,0:T(8,128)(2,1)S(1)}, u32[]{:S(2)}, u32[]{:S(2)}) collective-permute-start(bf16[512,512]{1,0:T(8,128)(2,1)} %get-tuple-element.35), channel_id=1, source_target_pairs={{0,192},{32,224},{64,128},{96,160},{128,64},{160,96},{192,0},{224,... | collective-permute-start | bytes 1572872 | tf_op jit(solution)/shard_map/ppermute | solution.py:282
  111.4 21.4 %collective-permute-start.9 = (bf16[512,512]{1,0:T(8,128)(2,1)}, bf16[512,512]{1,0:T(8,128)(2,1)S(1)}, u32[]{:S(2)}, u32[]{:S(2)}) collective-permute-start(bf16[512,512]{1,0:T(8,128)(2,1)} %get-tuple-element.33), channel_id=1, source_target_pairs={{0,64},{32,96},{64,0},{96,32},{128,192},{160,224},{192,128},{224,1... | collective-permute-start | bytes 1572872 | tf_op jit(solution)/shard_map/ppermute | solution.py:282
  119.3 16.9 %collective-permute-start.17 = (bf16[256,512]{1,0:T(8,128)(2,1)}, bf16[256,512]{1,0:T(8,128)(2,1)S(1)}, u32[]{:S(2)}, u32[]{:S(2)}) collective-permute-start(bf16[256,512]{1,0:T(8,128)(2,1)} %add_convert_fusion), channel_id=1, source_target_pairs={{0,64},{32,96},{64,0},{96,32},{128,192},{160,224},{192,128},{224,1... | collective-permute-start | bytes 786440 | tf_op jit(solution)/shard_map/ppermute | solution.py:282
  123.6 12.6 %collective-permute-start.15 = (bf16[256,512]{1,0:T(8,128)(2,1)}, bf16[256,512]{1,0:T(8,128)(2,1)}, u32[]{:S(2)}, u32[]{:S(2)}) collective-permute-start(bf16[256,512]{1,0:T(8,128)(2,1)} %add_convert_fusion.1), channel_id=1, source_target_pairs={{0,192},{32,224},{64,128},{96,160},{128,64},{160,96},{192,0},{224,... | collective-permute-start | bytes 786440 | tf_op jit(solution)/shard_map/ppermute | solution.py:282
  130.3 9.4 %collective-permute-start.12 = (bf16[256,512]{1,0:T(8,128)(2,1)}, bf16[256,512]{1,0:T(8,128)(2,1)}, u32[]{:S(2)}, u32[]{:S(2)}) collective-permute-start(bf16[256,512]{1,0:T(8,128)(2,1)} %add_convert_fusion.2), channel_id=1, source_target_pairs={{0,64},{32,96},{64,0},{96,32},{128,192},{160,224},{192,128},{224,1... | collective-permute-start | bytes 786440 | tf_op jit(solution)/shard_map/ppermute | solution.py:282
  134.4 6.7 %collective-permute-start.10 = (bf16[256,512]{1,0:T(8,128)(2,1)}, bf16[256,512]{1,0:T(8,128)(2,1)}, u32[]{:S(2)}, u32[]{:S(2)}) collective-permute-start(bf16[256,512]{1,0:T(8,128)(2,1)} %add_convert_fusion.3), channel_id=1, source_target_pairs={{0,192},{32,224},{64,128},{96,160},{128,64},{160,96},{192,0},{224,... | collective-permute-start | bytes 786440 | tf_op jit(solution)/shard_map/ppermute | solution.py:282
  (15 other events, 45.1 us)

commit v7 on v5

--- a/solution.py
+++ b/solution.py
@@ -19,6 +19,10 @@
 
 def dot_t(a, b):
     return lax.dot_general(a, b, (((1,), (1,)), ((), ())), preferred_element_type=F32)
+
+
+def dot_0(a, b):
+    return lax.dot_general(a, b, (((0,), (0,)), ((), ())), preferred_element_type=F32)
 
 
 def dot(a, b):
@@ -83,8 +87,9 @@
 
 def expert_kernel(unit, rows_hbm, *refs):
     in_a, in_b, in_ca, in_cb, out_a, out_b, out_ca, out_cb = refs[:8]
-    back_hbm, hid_hbm, act_hbm = refs[8:11]
-    rows_ref, back_ref, hid_ref, act_ref, full_in, full_out, sems, row_sem, out_sems, back_sems = refs[11:]
+    back_hbm, hid_hbm, act_hbm, send_hbm = refs[8:12]
+    rows_ref, back_ref, hid_ref, act_ref, send_ref, full_in, full_out = refs[12:19]
+    sems, row_sem, out_sems, send_sems, back_sems = refs[19:]
     sources, slots, width = rows_ref.shape
     capacity = slots // 2
     count = sources * capacity
@@ -151,6 +156,17 @@
 
     columns = 256
 
+    def send_copy(c, at):
+        cut = pl.ds(at, columns)
+        return pltpu.make_async_copy(send_ref.at[:, cut], send_hbm.at[:, cut], send_sems.at[c])
+
+    @pl.loop(0, width // columns)
+    def _(c):
+        at = pl.multiple_of(c * columns, columns)
+        rows = rows_ref[:, capacity:, pl.ds(at, columns)].reshape(count, columns)
+        send_ref[:, pl.ds(at, columns)] = dot_0(hid_ref[:, 4 * unit :], rows).astype(BF16)
+        send_copy(c, at).start()
+
     def back_copy(c, at):
         cut = pl.ds(at, columns)
         return pltpu.make_async_copy(back_ref.at[:, :, cut], back_hbm.at[:, :, cut], back_sems.at[c])
@@ -172,6 +188,8 @@
     for c in range(8):
         for copy in act_copies(c, c * unit):
             copy.wait()
+    for c in range(width // columns):
+        send_copy(c, c * columns).wait()
 
 
 def grad_kernel(part, first, unit, acts_hbm, rows_hbm, *refs):
@@ -283,7 +301,7 @@
     return two, other, core_two, core_other
 
 
-def scatter(acts, rows, part, unit):
+def scatter(send, acts, rows, part, unit):
     cells = acts.shape[0]
     sources, slots, width = rows.shape
     anywhere = pl.BlockSpec(memory_space=pl.ANY)
@@ -308,7 +326,8 @@
         )
 
     half = width // 2
-    send = product(4, [((4 * unit, width), BF16)])
+    if send is None:
+        send = product(4, [((4 * unit, width), BF16)])
     got = permute(send, PAIR_C)
     own, left, right, next_l, next_r = product(
         0,
@@ -360,34 +379,37 @@
         [((n, cells), BF16)] * 3,
         expert_ids.T,
         gate_weights.T,
-    )
-    answer, hidden, grad_act = call(
+        limit=16 << 20,
+    )
+    answer, hidden, grad_act, send_out = call(
         functools.partial(expert_kernel, unit),
-        [(shape, BF16)] + [((cells, 8 * unit), BF16)] * 2,
+        [(shape, BF16)] + [((cells, 8 * unit), BF16)] * 2 + [((4 * unit, width), BF16)],
         rows,
         *in_pieces,
         *out_pieces,
-        flops=8 * cells * width * 8 * unit,
+        flops=9 * cells * width * 8 * unit,
         moved=16 << 20,
-        specs=([anywhere] * 9, [anywhere] * 3),
+        specs=([anywhere] * 9, [anywhere] * 4),
         scratch=[
             pltpu.VMEM(shape, BF16),
             pltpu.VMEM(shape, BF16),
             pltpu.VMEM((cells, 8 * unit), BF16),
             pltpu.VMEM((cells, 8 * unit), BF16),
+            pltpu.VMEM((4 * unit, width), BF16),
             pltpu.VMEM((8 * unit, width), BF16),
             pltpu.VMEM((8 * unit, width), BF16),
             pltpu.SemaphoreType.DMA((2, 8)),
             pltpu.SemaphoreType.DMA((2,)),
             pltpu.SemaphoreType.DMA((2, 8)),
             pltpu.SemaphoreType.DMA((4,)),
+            pltpu.SemaphoreType.DMA((4,)),
         ],
         limit=48 << 20,
     )
     returned = exchange(answer)
 
-    grad_out = scatter(hidden, rows, 1, unit)
-    grad_in = scatter(grad_act, rows, 0, unit)
+    grad_out = scatter(send_out, hidden, rows, 1, unit)
+    grad_in = scatter(None, grad_act, rows, 0, unit)
 
     layer_out, token_grad = call(
         combine_kernel, [((n, width), BF16)] * 2, place, hi, lo, returned, limit=16 << 20

time: 147 us -> 144 us (0.980)
  waiting for transfers between devices: 55 us -> 62.8 us
  Pallas kernels: 43.9 us -> 38.7 us
  local copies, waits for them, and re-layouts: 7.66 us -> 4.85 us
  other arithmetic: 5.33 us -> 2.63 us
    ppermute x18, waiting for transfers between devices: 46.8 us -> 52.4 us  [permute(): return lax.ppermute(x, 'fsdp', pairs)]
    pallas_call x10 -> x9, Pallas kernels: 43.9 us -> 38.7 us  [call(): pl.pallas_call(kernel, out_shape=shapes[0] if single else shapes, in_spec...]
    unnamed x40 -> x30, local copies, waits for them, and re-layouts: 7.66 us -> 4.85 us
    all_to_all x2, waiting for transfers between devices: 8.21 us -> 10.4 us  [exchange(): lax.all_to_all(cells, 'expert', split_axis=0, concat_axis=0, tiled=True)]
  transfers between devices with their start and end apart: 20 -> 20, of which waited for: 10 -> 12; matrix products, arithmetic and copies ran while one was open for 4% -> 2% of each run, Pallas kernels for 16% -> 11%
where the time goes in v7:
time: 144 us; the launch traced here: 143 us
  waiting for transfers between devices  62.8 us (44%)
  Pallas kernels  38.7 us (27%)
  starting transfers between devices  33.2 us (23%)
  local copies, waits for them, and re-layouts  4.85 us (3%)
  other arithmetic  2.63 us (2%)
    ppermute x18, waiting for transfers between devices, permute(): return lax.ppermute(x, 'fsdp', pairs)  52.4 us
    pallas_call x9, Pallas kernels, call(): pl.pallas_call(kernel, out_shape=shapes[0] if single else shapes, in_spec...  38.7 us
    all_to_all x2, starting transfers between devices, exchange(): lax.all_to_all(cells, 'expert', split_axis=0, concat_axis=0, tiled=True)  17.7 us
    ppermute x18, starting transfers between devices, permute(): return lax.ppermute(x, 'fsdp', pairs)  15.5 us
    all_to_all x2, waiting for transfers between devices, exchange(): lax.all_to_all(cells, 'expert', split_axis=0, concat_axis=0, tiled=True)  10.4 us
    unnamed x30, local copies, waits for them, and re-layouts  4.85 us
  transfers between devices with their start and end apart: 20, of which 12 were waited for; matrix products, arithmetic and copies ran while one was open for 2% of the time, Pallas kernels for 11%

profile of v7, /device:TPU:16, one launch (start us, length us, event | category | flops | bytes accessed | tf_op | source)
XLA Modules:
  0.0 143.0 jit_solution(10564441309769980620)
XLA Ops:
  0.6 3.3 %shard_map.94 = bf16[32,32,1024]{2,1,0:T(8,128)(2,1)} custom-call(s32[2,128]{1,0:T(2,128)} %bitcast.6, f32[2,128]{1,0:T(2,128)} %bitcast.8, bf16[128,1024]{1,0:T(8,128)(2,1)} %refs_2_.1, bf16[128,1024]{1,0:T(8,128)(2,1)} %refs_3_.1), custom_call_target="tpu_custom_call" | custom-call | flops 300000000 | bytes 4194304 | tf_op jit(solution)/shard_map/pallas_call | solution.py:276
  3.9 11.6 %all-to-all-start = ((bf16[32,32,1024]{2,1,0:T(8,128)(2,1)}), bf16[32,32,1024]{2,1,0:T(8,128)(2,1)}, u32[]{:S(2)}, u32[]{:S(2)}) async-start(bf16[32,32,1024]{2,1,0:T(8,128)(2,1)} %shard_map.94), calls=%async_computation | async-start | bytes 4194304 | tf_op jit(solution)/shard_map/all_to_all | solution.py:288
  15.5 1.4 collective-permute-start
  16.9 12.1 %collective-permute-done = bf16[256,1024]{1,0:T(8,128)(2,1)S(1)} collective-permute-done((bf16[256,1024]{1,0:T(8,128)(2,1)S(1)}, bf16[256,1024]{1,0:T(8,128)(2,1)S(1)}, u32[]{:S(2)}, u32[]{:S(2)}) %collective-permute-start) | collective-permute-done | bytes 524320 | tf_op jit(solution)/shard_map/ppermute | solution.py:292
  30.1 2.0 %collective-permute-start.5 = (bf16[512,1024]{1,0:T(8,128)(2,1)S(1)}, bf16[512,1024]{1,0:T(8,128)(2,1)S(1)}, u32[]{:S(2)}, u32[]{:S(2)}) collective-permute-start(bf16[512,1024]{1,0:T(8,128)(2,1)S(1)} %pad_maximum_fusion.1.refs_4_), channel_id=1, source_target_pairs={{0,64},{32,96},{64,0},{96,32},{128,192},{160,224},{192,128},{224,1... | collective-permute-start | bytes 3145736 | tf_op jit(solution)/shard_map/ppermute | solution.py:292
  32.6 20.4 %collective-permute-done.1.refs_1_ = bf16[512,1024]{1,0:T(8,128)(2,1)S(1)} collective-permute-done((bf16[512,1024]{1,0:T(8,128)(2,1)S(1)}, bf16[512,1024]{1,0:T(8,128)(2,1)S(1)}, u32[]{:S(2)}, u32[]{:S(2)}) %collective-permute-start.1) | collective-permute-done | bytes 1048608 | tf_op jit(solution)/shard_map/ppermute | solution.py:292
  57.3 8.2 %all-to-all-done.rows_hbm = bf16[32,32,1024]{2,1,0:T(8,128)(2,1)} async-done(((bf16[32,32,1024]{2,1,0:T(8,128)(2,1)}), bf16[32,32,1024]{2,1,0:T(8,128)(2,1)}, u32[]{:S(2)}, u32[]{:S(2)}) %all-to-all-start) | async-done | bytes 2097184 | tf_op jit(solution)/shard_map/all_to_all | solution.py:288
  65.5 1.2 copy-done.5
  66.8 1.2 copy-done.7
  68.0 17.8 %shard_map.95 = (bf16[32,32,1024]{2,1,0:T(8,128)(2,1)}, bf16[512,2048]{1,0:T(8,128)(2,1)}, bf16[512,2048]{1,0:T(8,128)(2,1)}, bf16[1024,1024]{1,0:T(8,128)(2,1)}) custom-call(bf16[32,32,1024]{2,1,0:T(8,128)(2,1)} %all-to-all-done.rows_hbm, bf16[512,1024]{1,0:T(8,128)(2,1)S(1)} %pad_maximum_fusion.refs_0_, ...), custom_call_target="tpu_custom_call" | custom-call | flops 9663676416 | bytes 16777216 | tf_op jit(solution)/shard_map/pallas_call | solution.py:276
  85.8 6.1 %all-to-all-start.1 = ((bf16[32,32,1024]{2,1,0:T(8,128)(2,1)}), bf16[32,32,1024]{2,1,0:T(8,128)(2,1)S(1)}, u32[]{:S(2)}, u32[]{:S(2)}) async-start(bf16[32,32,1024]{2,1,0:T(8,128)(2,1)} %get-tuple-element.26), calls=%async_computation.1 | async-start | bytes 4194304 | tf_op jit(solution)/shard_map/all_to_all | solution.py:288
  92.0 4.0 %shard_map.97 = bf16[1024,1024]{1,0:T(8,128)(2,1)} custom-call(bf16[512,2048]{1,0:T(8,128)(2,1)} %get-tuple-element.29.acts_hbm, bf16[32,32,1024]{2,1,0:T(8,128)(2,1)} %all-to-all-done.rows_hbm), custom_call_target="tpu_custom_call" | custom-call | flops 1073741824 | bytes 4194304 | tf_op jit(solution)/shard_map/pallas_call | solution.py:276
  96.8 4.9 %shard_map.100 = (f32[256,1024]{1,0:T(8,128)}, bf16[512,512]{1,0:T(8,128)(2,1)}, bf16[512,512]{1,0:T(8,128)(2,1)}, f32[256,512]{1,0:T(8,128)}, f32[256,512]{1,0:T(8,128)}) custom-call(bf16[512,2048]{1,0:T(8,128)(2,1)} %get-tuple-element.35.acts_hbm, bf16[32,32,1024]{2,1,0:T(8,128)(2,1)} %all-to-all-done.rows_hbm, ...), custom_call_target="tpu_custom_call" | custom-call | flops 1073741824 | bytes 4194304 | tf_op jit(solution)/shard_map/pallas_call | solution.py:276
  103.2 4.9 %shard_map.98 = (f32[256,1024]{1,0:T(8,128)}, bf16[512,512]{1,0:T(8,128)(2,1)}, bf16[512,512]{1,0:T(8,128)(2,1)}, f32[256,512]{1,0:T(8,128)}, f32[256,512]{1,0:T(8,128)}) custom-call(bf16[512,2048]{1,0:T(8,128)(2,1)} %get-tuple-element.29.acts_hbm, bf16[32,32,1024]{2,1,0:T(8,128)(2,1)} %all-to-all-done.rows_hbm, ...), custom_call_target="tpu_custom_call" | custom-call | flops 1073741824 | bytes 4194304 | tf_op jit(solution)/shard_map/pallas_call | solution.py:276
  108.1 2.5 %collective-permute-start.11 = (bf16[512,512]{1,0:T(8,128)(2,1)}, bf16[512,512]{1,0:T(8,128)(2,1)S(1)}, u32[]{:S(2)}, u32[]{:S(2)}) collective-permute-start(bf16[512,512]{1,0:T(8,128)(2,1)} %get-tuple-element.33), channel_id=1, source_target_pairs={{0,192},{32,224},{64,128},{96,160},{128,64},{160,96},{192,0},{224,... | collective-permute-start | bytes 1572872 | tf_op jit(solution)/shard_map/ppermute | solution.py:292
  111.4 5.4 %collective-permute-done.16.first_r_ref = bf16[512,512]{1,0:T(8,128)(2,1)S(1)} collective-permute-done((bf16[512,512]{1,0:T(8,128)(2,1)}, bf16[512,512]{1,0:T(8,128)(2,1)S(1)}, u32[]{:S(2)}, u32[]{:S(2)}) %collective-permute-start.16) | collective-permute-done | bytes 524320 | tf_op jit(solution)/shard_map/ppermute | solution.py:292
  117.9 2.6 %collective-permute-start.17 = (bf16[256,512]{1,0:T(8,128)(2,1)S(1)}, bf16[256,512]{1,0:T(8,128)(2,1)S(1)}, u32[]{:S(2)}, u32[]{:S(2)}) collective-permute-start(bf16[256,512]{1,0:T(8,128)(2,1)S(1)} %add_convert_fusion), channel_id=1, source_target_pairs={{0,64},{32,96},{64,0},{96,32},{128,192},{160,224},{192,128},{224,1... | collective-permute-start | bytes 786440 | tf_op jit(solution)/shard_map/ppermute | solution.py:292
  120.5 1.2 add_convert_fusion.1
  121.8 6.2 %collective-permute-done.11.first_r_ref = bf16[512,512]{1,0:T(8,128)(2,1)S(1)} collective-permute-done((bf16[512,512]{1,0:T(8,128)(2,1)}, bf16[512,512]{1,0:T(8,128)(2,1)S(1)}, u32[]{:S(2)}, u32[]{:S(2)}) %collective-permute-start.11) | collective-permute-done | bytes 524320 | tf_op jit(solution)/shard_map/ppermute | solution.py:292
  128.1 2.6 %collective-permute-start.12 = (bf16[256,512]{1,0:T(8,128)(2,1)S(1)}, bf16[256,512]{1,0:T(8,128)(2,1)S(1)}, u32[]{:S(2)}, u32[]{:S(2)}) collective-permute-start(bf16[256,512]{1,0:T(8,128)(2,1)S(1)} %add_convert_fusion.2), channel_id=1, source_target_pairs={{0,64},{32,96},{64,0},{96,32},{128,192},{160,224},{192,128},{224,1... | collective-permute-start | bytes 786440 | tf_op jit(solution)/shard_map/ppermute | solution.py:292
  131.2 2.8 %collective-permute-done.17.got_r_ref = bf16[256,512]{1,0:T(8,128)(2,1)S(1)} collective-permute-done((bf16[256,512]{1,0:T(8,128)(2,1)S(1)}, bf16[256,512]{1,0:T(8,128)(2,1)S(1)}, u32[]{:S(2)}, u32[]{:S(2)}) %collective-permute-start.17) | collective-permute-done | bytes 262176 | tf_op jit(solution)/shard_map/ppermute | solution.py:292
  135.2 3.3 %collective-permute-done.12.got_r_ref = bf16[256,512]{1,0:T(8,128)(2,1)S(1)} collective-permute-done((bf16[256,512]{1,0:T(8,128)(2,1)S(1)}, bf16[256,512]{1,0:T(8,128)(2,1)S(1)}, u32[]{:S(2)}, u32[]{:S(2)}) %collective-permute-start.12) | collective-permute-done | bytes 262176 | tf_op jit(solution)/shard_map/ppermute | solution.py:292
  139.6 2.2 %all-to-all-done.1.rows_ref = bf16[32,32,1024]{2,1,0:T(8,128)(2,1)S(1)} async-done(((bf16[32,32,1024]{2,1,0:T(8,128)(2,1)}), bf16[32,32,1024]{2,1,0:T(8,128)(2,1)S(1)}, u32[]{:S(2)}, u32[]{:S(2)}) %all-to-all-start.1) | async-done | bytes 2097184 | tf_op jit(solution)/shard_map/all_to_all | solution.py:288
  141.7 1.3 shard_map.96
  (61 shorter events, 13.2 us)
Async XLA Ops:
  3.9 61.6 %all-to-all-start = ((bf16[32,32,1024]{2,1,0:T(8,128)(2,1)}), bf16[32,32,1024]{2,1,0:T(8,128)(2,1)}, u32[]{:S(2)}, u32[]{:S(2)}) async-start(bf16[32,32,1024]{2,1,0:T(8,128)(2,1)} %shard_map.94), calls=%async_computation | async-start | bytes 4194304 | tf_op jit(solution)/shard_map/all_to_all | solution.py:288
  15.5 14.5 %copy-start.12 = (bf16[1,256,1024]{2,1,0:T(8,128)(2,1)S(1)}, bf16[1,256,1024]{2,1,0:T(8,128)(2,1)}, u32[]{:S(2)}) copy-start(bf16[1,256,1024]{2,1,0:T(8,128)(2,1)} %param.10) | copy-start | bytes 1572868
  15.5 13.5 %collective-permute-start = (bf16[256,1024]{1,0:T(8,128)(2,1)S(1)}, bf16[256,1024]{1,0:T(8,128)(2,1)S(1)}, u32[]{:S(2)}, u32[]{:S(2)}) collective-permute-start(bf16[256,1024]{1,0:T(8,128)(2,1)S(1)} %bitcast.12), channel_id=1, source_target_pairs={{0,64},{32,96},{64,0},{96,32},{128,192},{160,224},{192,128},{224,1... | collective-permute-start | bytes 1572872 | tf_op jit(solution)/shard_map/ppermute | solution.py:292
  16.9 13.1 %collective-permute-start.4 = (bf16[256,1024]{1,0:T(8,128)(2,1)S(1)}, bf16[256,1024]{1,0:T(8,128)(2,1)S(1)}, u32[]{:S(2)}, u32[]{:S(2)}) collective-permute-start(bf16[256,1024]{1,0:T(8,128)(2,1)S(1)} %bitcast.14), channel_id=1, source_target_pairs={{0,192},{32,224},{64,128},{96,160},{128,64},{160,96},{192,0},{224,... | collective-permute-start | bytes 1572872 | tf_op jit(solution)/shard_map/ppermute | solution.py:292
  29.1 24.0 %collective-permute-start.1 = (bf16[512,1024]{1,0:T(8,128)(2,1)S(1)}, bf16[512,1024]{1,0:T(8,128)(2,1)S(1)}, u32[]{:S(2)}, u32[]{:S(2)}) collective-permute-start(bf16[512,1024]{1,0:T(8,128)(2,1)S(1)} %pad_maximum_fusion.refs_0_), channel_id=1, source_target_pairs={{0,192},{32,224},{64,128},{96,160},{128,64},{160,96},{192,0},{224,... | collective-permute-start | bytes 3145736 | tf_op jit(solution)/shard_map/ppermute | solution.py:292
  30.1 23.9 %collective-permute-start.5 = (bf16[512,1024]{1,0:T(8,128)(2,1)S(1)}, bf16[512,1024]{1,0:T(8,128)(2,1)S(1)}, u32[]{:S(2)}, u32[]{:S(2)}) collective-permute-start(bf16[512,1024]{1,0:T(8,128)(2,1)S(1)} %pad_maximum_fusion.1.refs_4_), channel_id=1, source_target_pairs={{0,64},{32,96},{64,0},{96,32},{128,192},{160,224},{192,128},{224,1... | collective-permute-start | bytes 3145736 | tf_op jit(solution)/shard_map/ppermute | solution.py:292
  32.1 21.9 %collective-permute-start.2 = (bf16[512,1024]{1,0:T(8,128)(2,1)S(1)}, bf16[512,1024]{1,0:T(8,128)(2,1)S(1)}, u32[]{:S(2)}, u32[]{:S(2)}) collective-permute-start(bf16[512,1024]{1,0:T(8,128)(2,1)S(1)} %pad_maximum_fusion.refs_0_), channel_id=1, source_target_pairs={{0,32},{32,0},{64,96},{96,64},{128,160},{160,128},{192,224},{224,1... | collective-permute-start | bytes 3145736 | tf_op jit(solution)/shard_map/ppermute | solution.py:292
  32.1 22.9 %collective-permute-start.6 = (bf16[512,1024]{1,0:T(8,128)(2,1)S(1)}, bf16[512,1024]{1,0:T(8,128)(2,1)S(1)}, u32[]{:S(2)}, u32[]{:S(2)}) collective-permute-start(bf16[512,1024]{1,0:T(8,128)(2,1)S(1)} %pad_maximum_fusion.1.refs_4_), channel_id=1, source_target_pairs={{0,32},{32,0},{64,96},{96,64},{128,160},{160,128},{192,224},{224,1... | collective-permute-start | bytes 3145736 | tf_op jit(solution)/shard_map/ppermute | solution.py:292
  53.0 2.7 %collective-permute-start.3 = (bf16[512,1024]{1,0:T(8,128)(2,1)S(1)}, bf16[512,1024]{1,0:T(8,128)(2,1)S(1)}, u32[]{:S(2)}, u32[]{:S(2)}) collective-permute-start(bf16[512,1024]{1,0:T(8,128)(2,1)S(1)} %collective-permute-done.1.refs_1_), channel_id=1, source_target_pairs={{0,32},{32,0},{64,96},{96,64},{128,160},{160,128},{192,224},{224,1... | collective-permute-start | bytes 3145736 | tf_op jit(solution)/shard_map/ppermute | solution.py:292
  54.0 3.3 %collective-permute-start.7 = (bf16[512,1024]{1,0:T(8,128)(2,1)S(1)}, bf16[512,1024]{1,0:T(8,128)(2,1)}, u32[]{:S(2)}, u32[]{:S(2)}) collective-permute-start(bf16[512,1024]{1,0:T(8,128)(2,1)S(1)} %collective-permute-done.5.refs_5_), channel_id=1, source_target_pairs={{0,32},{32,0},{64,96},{96,64},{128,160},{160,128},{192,224},{224,1... | collective-permute-start | bytes 3145736 | tf_op jit(solution)/shard_map/ppermute | solution.py:292
  85.8 55.9 %all-to-all-start.1 = ((bf16[32,32,1024]{2,1,0:T(8,128)(2,1)}), bf16[32,32,1024]{2,1,0:T(8,128)(2,1)S(1)}, u32[]{:S(2)}, u32[]{:S(2)}) async-start(bf16[32,32,1024]{2,1,0:T(8,128)(2,1)} %get-tuple-element.26), calls=%async_computation.1 | async-start | bytes 4194304 | tf_op jit(solution)/shard_map/all_to_all | solution.py:288
  91.9 4.8 %collective-permute-start.13 = (bf16[1024,1024]{1,0:T(8,128)(2,1)}, bf16[1024,1024]{1,0:T(8,128)(2,1)}, u32[]{:S(2)}, u32[]{:S(2)}) collective-permute-start(bf16[1024,1024]{1,0:T(8,128)(2,1)} %get-tuple-element.36), channel_id=1, source_target_pairs={{0,32},{32,0},{64,96},{96,64},{128,160},{160,128},{192,224},{224,1... | collective-permute-start | bytes 6291464 | tf_op jit(solution)/shard_map/ppermute | solution.py:292
  96.0 7.2 %collective-permute-start.8 = (bf16[1024,1024]{1,0:T(8,128)(2,1)}, bf16[1024,1024]{1,0:T(8,128)(2,1)}, u32[]{:S(2)}, u32[]{:S(2)}) collective-permute-start(bf16[1024,1024]{1,0:T(8,128)(2,1)} %shard_map.97), channel_id=1, source_target_pairs={{0,32},{32,0},{64,96},{96,64},{128,160},{160,128},{192,224},{224,1... | collective-permute-start | bytes 6291464 | tf_op jit(solution)/shard_map/ppermute | solution.py:292
  101.6 15.1 %collective-permute-start.16 = (bf16[512,512]{1,0:T(8,128)(2,1)}, bf16[512,512]{1,0:T(8,128)(2,1)S(1)}, u32[]{:S(2)}, u32[]{:S(2)}) collective-permute-start(bf16[512,512]{1,0:T(8,128)(2,1)} %get-tuple-element.40), channel_id=1, source_target_pairs={{0,192},{32,224},{64,128},{96,160},{128,64},{160,96},{192,0},{224,... | collective-permute-start | bytes 1572872 | tf_op jit(solution)/shard_map/ppermute | solution.py:292
  102.2 18.3 %collective-permute-start.14 = (bf16[512,512]{1,0:T(8,128)(2,1)}, bf16[512,512]{1,0:T(8,128)(2,1)S(1)}, u32[]{:S(2)}, u32[]{:S(2)}) collective-permute-start(bf16[512,512]{1,0:T(8,128)(2,1)} %get-tuple-element.38), channel_id=1, source_target_pairs={{0,64},{32,96},{64,0},{96,32},{128,192},{160,224},{192,128},{224,1... | collective-permute-start | bytes 1572872 | tf_op jit(solution)/shard_map/ppermute | solution.py:292
  108.1 19.9 %copy-start.9 = (f32[256,512]{1,0:T(8,128)S(1)}, f32[256,512]{1,0:T(8,128)}, u32[]{:S(2)}) copy-start(f32[256,512]{1,0:T(8,128)} %get-tuple-element.34) | copy-start | bytes 1572868
  108.1 22.5 %copy-start.8 = (f32[256,512]{1,0:T(8,128)S(1)}, f32[256,512]{1,0:T(8,128)}, u32[]{:S(2)}) copy-start(f32[256,512]{1,0:T(8,128)} %get-tuple-element.32) | copy-start | bytes 1572868
  108.1 19.8 %collective-permute-start.11 = (bf16[512,512]{1,0:T(8,128)(2,1)}, bf16[512,512]{1,0:T(8,128)(2,1)S(1)}, u32[]{:S(2)}, u32[]{:S(2)}) collective-permute-start(bf16[512,512]{1,0:T(8,128)(2,1)} %get-tuple-element.33), channel_id=1, source_target_pairs={{0,192},{32,224},{64,128},{96,160},{128,64},{160,96},{192,0},{224,... | collective-permute-start | bytes 1572872 | tf_op jit(solution)/shard_map/ppermute | solution.py:292
  110.6 20.0 %collective-permute-start.9 = (bf16[512,512]{1,0:T(8,128)(2,1)}, bf16[512,512]{1,0:T(8,128)(2,1)S(1)}, u32[]{:S(2)}, u32[]{:S(2)}) collective-permute-start(bf16[512,512]{1,0:T(8,128)(2,1)} %get-tuple-element.31), channel_id=1, source_target_pairs={{0,64},{32,96},{64,0},{96,32},{128,192},{160,224},{192,128},{224,1... | collective-permute-start | bytes 1572872 | tf_op jit(solution)/shard_map/ppermute | solution.py:292
  116.7 14.1 %copy-start.3 = (f32[128,2]{0,1:T(2,128)S(1)}, f32[128,2]{0,1:T(2,128)}, u32[]{:S(2)}) copy-start(f32[128,2]{0,1:T(2,128)} %param.8) | copy-start | bytes 3076
  117.9 16.2 %collective-permute-start.17 = (bf16[256,512]{1,0:T(8,128)(2,1)S(1)}, bf16[256,512]{1,0:T(8,128)(2,1)S(1)}, u32[]{:S(2)}, u32[]{:S(2)}) collective-permute-start(bf16[256,512]{1,0:T(8,128)(2,1)S(1)} %add_convert_fusion), channel_id=1, source_target_pairs={{0,64},{32,96},{64,0},{96,32},{128,192},{160,224},{192,128},{224,1... | collective-permute-start | bytes 786440 | tf_op jit(solution)/shard_map/ppermute | solution.py:292
  121.7 12.4 %collective-permute-start.15 = (bf16[256,512]{1,0:T(8,128)(2,1)S(1)}, bf16[256,512]{1,0:T(8,128)(2,1)S(1)}, u32[]{:S(2)}, u32[]{:S(2)}) collective-permute-start(bf16[256,512]{1,0:T(8,128)(2,1)S(1)} %add_convert_fusion.1), channel_id=1, source_target_pairs={{0,192},{32,224},{64,128},{96,160},{128,64},{160,96},{192,0},{224,... | collective-permute-start | bytes 786440 | tf_op jit(solution)/shard_map/ppermute | solution.py:292
  128.1 10.4 %collective-permute-start.12 = (bf16[256,512]{1,0:T(8,128)(2,1)S(1)}, bf16[256,512]{1,0:T(8,128)(2,1)S(1)}, u32[]{:S(2)}, u32[]{:S(2)}) collective-permute-start(bf16[256,512]{1,0:T(8,128)(2,1)S(1)} %add_convert_fusion.2), channel_id=1, source_target_pairs={{0,64},{32,96},{64,0},{96,32},{128,192},{160,224},{192,128},{224,1... | collective-permute-start | bytes 786440 | tf_op jit(solution)/shard_map/ppermute | solution.py:292
  130.7 7.7 %collective-permute-start.10 = (bf16[256,512]{1,0:T(8,128)(2,1)S(1)}, bf16[256,512]{1,0:T(8,128)(2,1)S(1)}, u32[]{:S(2)}, u32[]{:S(2)}) collective-permute-start(bf16[256,512]{1,0:T(8,128)(2,1)S(1)} %add_convert_fusion.3), channel_id=1, source_target_pairs={{0,192},{32,224},{64,128},{96,160},{128,64},{160,96},{192,0},{224,... | collective-permute-start | bytes 786440 | tf_op jit(solution)/shard_map/ppermute | solution.py:292
  (11 other events, 66.7 us)
